TPU v7x, 256 devices: a whole 4x4x8 slice. The times are simulated.
256 devices in a mesh: seq: 32 (over z_hi, x, core), head: 8 (over y, z_lo).
Axes of the slice: x: 4, y: 4, z: 8 (z_hi: 4, z_lo: 2; z = z_hi * 2 + z_lo), core: 2. Of those that a mesh axis runs over, the one named last changes fastest.
Arguments:
- queries: bfloat16 [6144, 4096], P('seq', 'head'), may hold values from -12.5 to 12.5
- keys: bfloat16 [6144, 1024], P('seq', 'head'), may hold values from -10.5 to 10.5
- values: bfloat16 [6144, 1024], P('seq', 'head'), may hold values from -6 to 6
- d_out: bfloat16 [6144, 4096], P('seq', 'head'), may hold values from -6 to 6
- w_out: bfloat16 [4096, 4096], P('head'), may hold values from -0.09375 to 0.09375
- doc_starts: int32 [4], replicated, may hold values from 0 to 6128, as said below
Outputs:
- query_grad: bfloat16 [6144, 4096], P('seq', 'head')
- key_grad: bfloat16 [6144, 1024], P('seq', 'head')
- value_grad: bfloat16 [6144, 1024], P('seq', 'head')
Inputs may be any that keep to these rules, and one draw needn't show every extreme that they name: doc_starts[0] is 0, the entries rise strictly, every entry is a multiple of 16, and the last entry is 6128, so the last document has 16 positions; a document runs from its start to the next start or to the end of the sequence.
All inputs are finite; a program needn't handle non-finite values.
Results may differ from a plain program's by a relative error of at most 0.0163.
Values may be sent and summed in bfloat16 or wider, within the bound.
A program may use at most 128 MiB of HBM per device.

v0:
```python
import math

import jax
import jax.numpy as jnp
from jax import lax
from jax.sharding import PartitionSpec as P

DH = 128


NEG_FILL = -1e30


def doc_index(doc_starts, places):
    return jnp.sum((places[:, None] >= doc_starts[None, :]).astype(jnp.int32), axis=1)


def allowed_pairs(doc_starts, row_ids, col_ids):
    earlier = col_ids[None, :] <= row_ids[:, None]
    same_doc = doc_index(doc_starts, row_ids)[:, None] == doc_index(doc_starts, col_ids)[None, :]
    return (earlier & same_doc)[None, None]


def softmax_grads(q_four, g_four, key_three, value_three, allowed, log_total, row_delta, scaling):
    scores = (
        jnp.einsum("sghd,kgd->ghsk", q_four, key_three, preferred_element_type=jnp.float32)
        * scaling
    )
    prob_full = jnp.where(allowed, jnp.exp(scores - log_total[..., None]), 0.0)
    grad_dots = jnp.einsum(
        "sghd,kgd->ghsk", g_four, value_three, preferred_element_type=jnp.float32
    )
    dscores = prob_full * (grad_dots - row_delta[..., None]) * scaling
    return (prob_full.astype(jnp.bfloat16), dscores.astype(jnp.bfloat16))


def shards(queries, keys, values, d_out, w_out, doc_starts):
    rows_here = queries.shape[0]
    head_size = DH
    groups = keys.shape[1] // head_size
    per_group = queries.shape[1] // keys.shape[1]
    scaling = 1.0 / math.sqrt(head_size)
    first_row = lax.axis_index("seq") * rows_here
    my_rows = first_row + jnp.arange(rows_here, dtype=jnp.int32)
    weights = w_out
    attn_grad = lax.dot_general(
        lax.all_gather(d_out, "head", axis=1, tiled=True),
        weights,
        (((1,), (1,)), ((), ())),
        preferred_element_type=jnp.float32,
    )
    attn_grad = attn_grad.astype(jnp.bfloat16)
    query_four = queries.reshape(rows_here, groups, per_group, head_size)
    grad_four = attn_grad.reshape(rows_here, groups, per_group, head_size)
    stat_shape = (groups, per_group, rows_here)
    key_block = lax.all_gather(keys, "seq", axis=0, tiled=True)
    value_block = lax.all_gather(values, "seq", axis=0, tiled=True)
    piece_rows = key_block.shape[0]
    allowed = allowed_pairs(doc_starts, my_rows, jnp.arange(piece_rows, dtype=jnp.int32))
    key_three = key_block.reshape(piece_rows, groups, head_size)
    value_three = value_block.reshape(piece_rows, groups, head_size)
    scores = (
        jnp.einsum("sghd,kgd->ghsk", query_four, key_three, preferred_element_type=jnp.float32)
        * scaling
    )
    scores = jnp.where(allowed, scores, NEG_FILL)
    high_old = jnp.full(stat_shape, NEG_FILL, jnp.float32)
    high_new = jnp.maximum(high_old, jnp.max(scores, axis=-1))
    weights = jnp.where(allowed, jnp.exp(scores - high_new[..., None]), 0.0)
    grad_dots = jnp.einsum(
        "sghd,kgd->ghsk", grad_four, value_three, preferred_element_type=jnp.float32
    )
    total_new = jnp.sum(weights, axis=-1)
    accum_new = jnp.sum(weights * grad_dots, axis=-1)
    log_total = high_new + jnp.log(total_new)
    row_delta = accum_new / total_new
    key_block = lax.all_gather(keys, "seq", axis=0, tiled=True)
    value_block = lax.all_gather(values, "seq", axis=0, tiled=True)
    piece_rows = key_block.shape[0]
    allowed = allowed_pairs(doc_starts, my_rows, jnp.arange(piece_rows, dtype=jnp.int32))
    key_three = key_block.reshape(piece_rows, groups, head_size)
    value_three = value_block.reshape(piece_rows, groups, head_size)
    prob_half, dscores = softmax_grads(
        query_four, grad_four, key_three, value_three, allowed, log_total, row_delta, scaling
    )
    key_three, prob_half, dscores, piece_rows = (key_three, prob_half, dscores, piece_rows)
    query_acc = jnp.einsum("ghsk,kgd->sghd", dscores, key_three, preferred_element_type=jnp.float32)
    key_piece = jnp.einsum(
        "ghsk,sghd->kgd", dscores, query_four, preferred_element_type=jnp.float32
    )
    value_piece = jnp.einsum(
        "ghsk,sghd->kgd", prob_half, grad_four, preferred_element_type=jnp.float32
    )
    key_acc = key_piece
    value_acc = value_piece
    query_acc, key_terms, value_terms = (query_acc, key_acc, value_acc)
    key_acc, value_acc = (
        lax.psum_scatter(
            key_terms.astype(jnp.bfloat16), "seq", scatter_dimension=0, tiled=True
        ).astype(jnp.float32),
        lax.psum_scatter(
            value_terms.astype(jnp.bfloat16), "seq", scatter_dimension=0, tiled=True
        ).astype(jnp.float32),
    )
    query_grad = query_acc.reshape(rows_here, groups * per_group * head_size).astype(jnp.bfloat16)
    key_grad = key_acc.reshape(rows_here, groups * head_size).astype(jnp.bfloat16)
    value_grad = value_acc.reshape(rows_here, groups * head_size).astype(jnp.bfloat16)
    return (query_grad, key_grad, value_grad)


def solution(mesh):
    return jax.shard_map(
        shards,
        mesh=mesh,
        in_specs=(
            P("seq", "head"),
            P("seq", "head"),
            P("seq", "head"),
            P("seq", "head"),
            P("head", None),
            P(),
        ),
        out_specs=(P("seq", "head"), P("seq", "head"), P("seq", "head")),
        check_vma=False,
    )
```

profile of v0, /device:TPU:8, one launch (start us, length us, event | category | flops | bytes accessed | tf_op | source)
XLA Modules:
  0.0 378.5 jit_solution(6322208966597983329)
XLA Ops:
  7.2 0.0 copy-start
  7.2 0.0 all-gather.6.cloned.1.call-start
  7.2 0.7 all-gather.6.cloned.1.call-update
  7.9 0.0 all-gather.4.cloned.1.call-start
  8.0 0.7 all-gather.4.cloned.1.call-update
  8.7 0.0 all-gather.8.cloned.1.call-start
  8.7 0.7 all-gather.8.cloned.1.call-update
  9.4 0.0 reduce-scatter.7.cloned.1.call-start
  9.5 0.7 convert_reduce_fusion.1
  10.2 0.8 convert_reduce_fusion
  11.0 1.0 fusion.25
  12.0 45.0 %all-gather.6.cloned.1.call-done = bf16[192,4096]{1,0:T(8,128)(2,1)} async-done(((bf16[192,512]{1,0:T(8,128)(2,1)}), bf16[192,4096]{1,0:T(8,128)(2,1)}) %all-gather.6.cloned.1.call-update) | async-done | bytes 1572880 | tf_op jit(solution)/shard_map/all_gather | solution.py:47
  57.0 4.2 %fusion.38 = bf16[24,4,8,128]{3,2,1,0:T(8,128)(2,1)S(1)} fusion(bf16[192,4096]{1,0:T(8,128)(2,1)} %all-gather.6.cloned.1.call-done, bf16[512,4096]{1,0:T(8,128)(2,1)} %param.10), kind=kOutput, calls=%fused_computation.35 | convolution fusion | flops 805404672 | bytes 5963776 | tf_op jit(solution)/shard_map/dot_general | solution.py:46
  61.2 52.1 %all-gather.4.cloned.1.call-done = bf16[6144,128]{1,0:T(8,128)(2,1)} async-done(((bf16[192,128]{1,0:T(8,128)(2,1)}), bf16[6144,128]{1,0:T(8,128)(2,1)}) %all-gather.4.cloned.1.call-update) | async-done | bytes 1572880 | tf_op jit(solution)/shard_map/all_gather | solution.py:77
  113.3 0.0 copy-done
  113.3 9.9 %fusion.6 = (f32[4,192]{1,0:T(4,128)S(1)}, f32[6144,192,4]{0,1,2:T(8,128)}) fusion(pred[192,6144]{1,0:T(8,128)(4,1)S(1)} %fusion.25, bf16[6144,128]{1,0:T(8,128)(2,1)} %all-gather.4.cloned.1.call-done, bf16[192,512]{1,0:T(8,128)(2,1)S(1)} %copy-done), kind=kOutput, calls=%fused_computation.11 | convolution fusion | flops 1222114560 | bytes 21826560 | tf_op jit(solution)/shard_map/sghd,kgd->ghsk/dot_general | solution.py:26
  123.2 43.0 %all-gather.8.cloned.1.call-done = bf16[6144,128]{1,0:T(8,128)(2,1)} async-done(((bf16[192,128]{1,0:T(8,128)(2,1)}), bf16[6144,128]{1,0:T(8,128)(2,1)}) %all-gather.8.cloned.1.call-update) | async-done | bytes 1572880 | tf_op jit(solution)/shard_map/all_gather | solution.py:78
  166.2 15.5 %fusion.8 = (f32[4,192]{1,0:T(4,128)S(1)}, f32[4,192]{1,0:T(4,128)S(1)}, f32[192,4,6144]{2,0,1:T(8,128)}) fusion(f32[6144,192,4]{0,1,2:T(8,128)} %get-tuple-element.20, f32[4,192]{1,0:T(4,128)S(1)} %broadcast_maximum_fusion, pred[192,6144]{1,0:T(8,128)(4,1)S(1)} %fusion.25, bf16[6144,128]{1,0:T(8,128)(2,1)} %all-gather.8.cloned.1.call-done, ...), kind=kOutput, calls=%fused_computation.13 | convolution fusion | flops 1240988160 | bytes 40707072 | tf_op jit(solution)/shard_map/sghd,kgd->ghsk/dot_general | solution.py:30
  181.8 9.1 %fusion.21 = bf16[6144,128]{0,1:T(8,128)(2,1)S(1)} fusion(f32[6144,192,4]{0,1,2:T(8,128)} %get-tuple-element.20, f32[4,192]{1,0:T(4,128)S(1)} %get-tuple-element.17, pred[192,6144]{1,0:T(8,128)(4,1)S(1)} %fusion.25, bf16[24,4,8,128]{3,2,1,0:T(8,128)(2,1)S(1)} %fusion.38), kind=kOutput, calls=%fused_computation.22 | convolution fusion | flops 1227620352 | bytes 21826560 | tf_op jit(solution)/shard_map/ghsk,sghd->kgd/dot_general | solution.py:91
  190.8 1.6 copy.34
  192.4 0.0 reduce-scatter.7.cloned.1.call-update
  192.5 0.2 reduce-scatter.5.cloned.1.call-start
  192.7 13.7 %fusion.10 = bf16[4,192,6144]{2,1,0:T(8,128)(2,1)S(1)} fusion(f32[192,4,6144]{2,0,1:T(8,128)} %get-tuple-element.21, f32[6144,192,4]{0,1,2:T(8,128)} %get-tuple-element.20, f32[4,192]{1,0:T(4,128)S(1)} %get-tuple-element.18, f32[4,192]{1,0:T(4,128)S(1)} %get-tuple-element.17, pred[192,6144]{1,0:T(8,128)(4,1)S(1)} %fusion.25), kind=kLoop, calls=%fused_computation.15 | loop fusion | flops 33030144 | bytes 48371712 | tf_op jit(solution)/shard_map/reshape.24
  206.4 0.0 copy-start.1
  206.4 3.6 copy-done.1
  210.0 0.0 copy-start.2
  210.0 3.9 %fusion.24 = bf16[6144,1,128]{2,0,1:T(8,128)(2,1)} fusion(bf16[4,192,6144]{2,1,0:T(8,128)(2,1)S(1)} %fusion.10, bf16[192,512]{1,0:T(8,128)(2,1)S(1)} %copy-done), kind=kOutput, calls=%fused_computation.23 | convolution fusion | flops 1208745984 | bytes 11206656 | tf_op jit(solution)/shard_map/ghsk,sghd->kgd/dot_general | solution.py:88
  213.9 0.0 reduce-scatter.5.cloned.1.call-update
  213.9 0.0 copy-done.2
  213.9 6.4 %fusion.35 = bf16[192,1,4,128]{3,0,2,1:T(8,128)(2,1)S(1)} fusion(bf16[4,192,6144]{2,1,0:T(8,128)(2,1)} %copy-done.1, bf16[6144,128]{1,0:T(8,128)(2,1)S(1)} %copy-done.2), kind=kOutput, calls=%fused_computation.34 | convolution fusion | flops 1208057856 | bytes 11206656 | tf_op jit(solution)/shard_map/ghsk,kgd->sghd/dot_general | solution.py:87
  220.3 0.2 copy.28
  220.5 0.7 copy.60
  221.2 58.7 %reduce-scatter.7.cloned.1.call-done = bf16[192,128]{1,0:T(8,128)(2,1)} async-done(((bf16[6144,128]{1,0:T(8,128)(2,1)}), bf16[192,128]{1,0:T(8,128)(2,1)}) %reduce-scatter.7.cloned.1.call-update) | async-done | bytes 49168
  279.9 92.1 %reduce-scatter.5.cloned.1.call-done = bf16[192,1,128]{2,0,1:T(8,128)(2,1)} async-done(((bf16[6144,1,128]{2,0,1:T(8,128)(2,1)}), bf16[192,1,128]{2,0,1:T(8,128)(2,1)}) %reduce-scatter.5.cloned.1.call-update) | async-done | bytes 49168 | tf_op jit(solution)/shard_map/reduce_scatter | solution.py:98
  (3 shorter events, 0.0 us)
Async XLA Ops:
  7.2 106.2 %copy-start = (bf16[192,512]{1,0:T(8,128)(2,1)S(1)}, bf16[192,512]{1,0:T(8,128)(2,1)}, u32[]{:S(2)}) copy-start(bf16[192,512]{1,0:T(8,128)(2,1)} %param.6) | copy-start | bytes 589828
  7.2 49.8 %all-gather.6.cloned.1.call-start = ((), (), s32[]{:S(2)}) async-start(), calls=%async_computation.3 | async-start | bytes 1769472 | tf_op jit(solution)/shard_map/all_gather | solution.py:47
  7.9 105.4 %all-gather.4.cloned.1.call-start = ((), (), s32[]{:S(2)}) async-start(), calls=%async_computation.2 | async-start | bytes 1622016 | tf_op jit(solution)/shard_map/all_gather | solution.py:77
  8.7 157.5 %all-gather.8.cloned.1.call-start = ((), (), s32[]{:S(2)}) async-start(), calls=%async_computation.4 | async-start | bytes 1622016 | tf_op jit(solution)/shard_map/all_gather | solution.py:78
  9.4 270.5 %reduce-scatter.7.cloned.1.call-start = ((), (), s32[]{:S(2)}) async-start(), calls=%async_computation.6 | async-start | bytes 1622016
  192.5 179.5 %reduce-scatter.5.cloned.1.call-start = ((), (), s32[]{:S(2)}) async-start(), calls=%async_computation.5 | async-start | bytes 1622016 | tf_op jit(solution)/shard_map/reduce_scatter | solution.py:98
  206.4 3.6 copy-start.1
  210.0 3.9 %copy-start.2 = (bf16[6144,128]{1,0:T(8,128)(2,1)S(1)}, bf16[6144,128]{1,0:T(8,128)(2,1)}, u32[]{:S(2)}) copy-start(bf16[6144,128]{1,0:T(8,128)(2,1)} %all-gather.4.cloned.1.call-done) | copy-start | bytes 4718596
Sparse Core Ops, SparseCore 0:
  9.8 47.1 all-gather.5
  59.5 53.7 all-gather.3
  115.9 50.2 all-gather.7
  192.6 87.3 reduce-scatter.6
  284.2 87.7 reduce-scatter.4
where the time goes:
time: 379 us
  waiting for transfers between devices  293 us (77%)
  matrix products  49 us (13%)
  other arithmetic  16.2 us (4%)
  between operations  13.9 us (4%)
  local copies, waits for them, and re-layouts  6.1 us (2%)
    reduce_scatter x1, waiting for transfers between devices, shards(): lax.psum_scatter(key_terms.astype(jnp.bfloat16), 'seq', scatter_dimension...  92.1 us
    unnamed x6, waiting for transfers between devices  60.8 us
    all_gather x1, waiting for transfers between devices, shards(): key_block = lax.all_gather(keys, 'seq', axis=0, tiled=True)  52.1 us
    all_gather x1, waiting for transfers between devices, shards(): lax.all_gather(d_out, 'head', axis=1, tiled=True)  45 us
    all_gather x1, waiting for transfers between devices, shards(): value_block = lax.all_gather(values, 'seq', axis=0, tiled=True)  43 us
    dot_general x1, matrix products, softmax_grads(): jnp.einsum('sghd,kgd->ghsk', g_four, value_three, preferred_element_type=...  15.5 us
    another operation x1, other arithmetic  13.7 us
    dot_general x1, matrix products, softmax_grads(): jnp.einsum('sghd,kgd->ghsk', q_four, key_three, preferred_element_type=jn...  9.9 us
  transfers between devices with their start and end apart: 5, of which 5 were waited for; matrix products, arithmetic and copies ran while one was open for 11% of the time, Pallas kernels for 0%

commit v1 on v0

v1 whole, which is shorter than its diff:
```python
import math

import jax
import jax.numpy as jnp
from jax import lax
from jax.sharding import PartitionSpec as P

DH = 128


NEG_FILL = -1e30


def doc_index(doc_starts, places):
    return jnp.sum((places[:, None] >= doc_starts[None, :]).astype(jnp.int32), axis=1)


def allowed_pairs(doc_starts, row_ids, col_ids):
    earlier = col_ids[None, :] <= row_ids[:, None]
    same_doc = doc_index(doc_starts, row_ids)[:, None] == doc_index(doc_starts, col_ids)[None, :]
    return (earlier & same_doc)[None, None]


def shards(queries, keys, values, d_out, w_out, doc_starts):
    rows_here = queries.shape[0]
    head_size = DH
    groups = keys.shape[1] // head_size
    per_group = queries.shape[1] // keys.shape[1]
    kv_cols = keys.shape[1]
    scaling = 1.0 / math.sqrt(head_size)
    first_row = lax.axis_index("seq") * rows_here
    my_rows = first_row + jnp.arange(rows_here, dtype=jnp.int32)
    kv_block = lax.all_gather(
        jnp.concatenate([keys, values], axis=1), "seq", axis=0, tiled=True
    )
    attn_grad = lax.dot_general(
        lax.all_gather(d_out, "head", axis=1, tiled=True),
        w_out,
        (((1,), (1,)), ((), ())),
        preferred_element_type=jnp.float32,
    ).astype(jnp.bfloat16)
    query_four = queries.reshape(rows_here, groups, per_group, head_size)
    grad_four = attn_grad.reshape(rows_here, groups, per_group, head_size)
    piece_rows = kv_block.shape[0]
    allowed = allowed_pairs(doc_starts, my_rows, jnp.arange(piece_rows, dtype=jnp.int32))
    key_three = kv_block[:, :kv_cols].reshape(piece_rows, groups, head_size)
    value_three = kv_block[:, kv_cols:].reshape(piece_rows, groups, head_size)
    scores = (
        jnp.einsum("sghd,kgd->ghsk", query_four, key_three, preferred_element_type=jnp.float32)
        * scaling
    )
    scores = jnp.where(allowed, scores, NEG_FILL)
    high = jnp.max(scores, axis=-1)
    weights = jnp.where(allowed, jnp.exp(scores - high[..., None]), 0.0)
    total = jnp.sum(weights, axis=-1)
    log_total = high + jnp.log(total)
    prob_full = jnp.where(allowed, jnp.exp(scores - log_total[..., None]), 0.0)
    grad_dots = jnp.einsum(
        "sghd,kgd->ghsk", grad_four, value_three, preferred_element_type=jnp.float32
    )
    row_delta = jnp.sum(prob_full * grad_dots, axis=-1)
    dscores = (prob_full * (grad_dots - row_delta[..., None]) * scaling).astype(jnp.bfloat16)
    prob_half = prob_full.astype(jnp.bfloat16)
    query_acc = jnp.einsum("ghsk,kgd->sghd", dscores, key_three, preferred_element_type=jnp.float32)
    key_terms = jnp.einsum(
        "ghsk,sghd->kgd", dscores, query_four, preferred_element_type=jnp.float32
    ).reshape(piece_rows, kv_cols)
    value_terms = jnp.einsum(
        "ghsk,sghd->kgd", prob_half, grad_four, preferred_element_type=jnp.float32
    ).reshape(piece_rows, kv_cols)
    kv_grad = lax.psum_scatter(
        jnp.concatenate([key_terms, value_terms], axis=1).astype(jnp.bfloat16),
        "seq", scatter_dimension=0, tiled=True,
    )
    query_grad = query_acc.reshape(rows_here, groups * per_group * head_size).astype(jnp.bfloat16)
    key_grad = kv_grad[:, :kv_cols]
    value_grad = kv_grad[:, kv_cols:]
    return (query_grad, key_grad, value_grad)


def solution(mesh):
    return jax.shard_map(
        shards,
        mesh=mesh,
        in_specs=(
            P("seq", "head"),
            P("seq", "head"),
            P("seq", "head"),
            P("seq", "head"),
            P("head", None),
            P(),
        ),
        out_specs=(P("seq", "head"), P("seq", "head"), P("seq", "head")),
        check_vma=False,
    )
```

time: 379 us -> 274 us (0.72)
  waiting for transfers between devices: 293 us -> 188 us
  matrix products: 49 us -> 38.5 us
  other arithmetic: 16.2 us -> 24.6 us
    reduce_scatter x1 -> x0, waiting for transfers between devices: 92.1 us -> none  [shards(): lax.psum_scatter(key_terms.astype(jnp.bfloat16), 'seq', scatter_dimension...]
    all_gather x2 -> x1, waiting for transfers between devices: 95.1 us -> 56.6 us  [shards(): lax.all_gather(jnp.concatenate([keys, values], axis=1), 'seq', axis=0, ti...]
    unnamed x6 -> x4, waiting for transfers between devices: 60.8 us -> 86.8 us
    reduce_sum x0 -> x1, other arithmetic: none -> 6.34 us  [shards(): total = jnp.sum(weights, axis=-1)]
    dot_general x3, matrix products: 29.6 us -> 24.4 us  [the longest x1 14.9 us: shards(): jnp.einsum('sghd,kgd->ghsk', grad_four, value_three, preferred_element_ty...]
    another operation x2 -> x1, other arithmetic: 13.7 us -> 13.9 us
  transfers between devices with their start and end apart: 5 -> 3, of which waited for: 5 -> 3; matrix products, arithmetic and copies ran while one was open for 11% -> 6% of each run, Pallas kernels for 0% -> 0%
where the time goes in v1:
time: 274 us
  waiting for transfers between devices  188 us (69%)
  matrix products  38.5 us (14%)
  other arithmetic  24.6 us (9%)
  between operations  13.9 us (5%)
  local copies, waits for them, and re-layouts  8.88 us (3%)
    unnamed x4, waiting for transfers between devices  86.8 us
    all_gather x1, waiting for transfers between devices, shards(): lax.all_gather(jnp.concatenate([keys, values], axis=1), 'seq', axis=0, ti...  56.6 us
    all_gather x1, waiting for transfers between devices, shards(): lax.all_gather(d_out, 'head', axis=1, tiled=True)  44.9 us
    dot_general x1, matrix products, shards(): jnp.einsum('sghd,kgd->ghsk', grad_four, value_three, preferred_element_ty...  14.9 us
    another operation x1, other arithmetic  13.9 us
    unnamed x8, local copies, waits for them, and re-layouts  7.26 us
    dot_general x1, matrix products, shards(): jnp.einsum('ghsk,kgd->sghd', dscores, key_three, preferred_element_type=j...  6.77 us
    reduce_sum x1, other arithmetic, shards(): total = jnp.sum(weights, axis=-1)  6.34 us
  transfers between devices with their start and end apart: 3, of which 3 were waited for; matrix products, arithmetic and copies ran while one was open for 6% of the time, Pallas kernels for 0%

profile of v1, /device:TPU:8, one launch (start us, length us, event | category | flops | bytes accessed | tf_op | source)
XLA Modules:
  0.0 274.2 jit_solution(5804958162041991944)
XLA Ops:
  7.2 0.0 copy-start
  7.2 0.0 all-gather.5.cloned.1.call-start
  7.2 0.7 all-gather.5.cloned.1.call-update
  7.9 0.0 all-gather.3.cloned.1.call-start
  8.0 1.5 pad_maximum_fusion.1
  9.4 0.0 all-gather.3.cloned.1.call-update
  9.5 0.0 reduce-scatter.4.cloned.1.call-start
  9.5 0.7 convert_reduce_fusion.1
  10.3 0.8 convert_reduce_fusion
  11.1 1.0 fusion.19
  12.1 44.9 %all-gather.5.cloned.1.call-done = bf16[192,4096]{1,0:T(8,128)(2,1)} async-done(((bf16[192,512]{1,0:T(8,128)(2,1)}), bf16[192,4096]{1,0:T(8,128)(2,1)}) %all-gather.5.cloned.1.call-update) | async-done | bytes 1572880 | tf_op jit(solution)/shard_map/all_gather | solution.py:37
  57.0 4.2 %fusion.25 = bf16[24,4,8,128]{3,2,1,0:T(8,128)(2,1)S(1)} fusion(bf16[192,4096]{1,0:T(8,128)(2,1)} %all-gather.5.cloned.1.call-done, bf16[512,4096]{1,0:T(8,128)(2,1)} %param.10), kind=kOutput, calls=%fused_computation.30 | convolution fusion | flops 805404672 | bytes 5963776 | tf_op jit(solution)/shard_map/dot_general | solution.py:36
  61.2 56.6 %all-gather.3.cloned.1.call-done = bf16[6144,256]{1,0:T(8,128)(2,1)} async-done(((bf16[192,256]{1,0:T(8,128)(2,1)}), bf16[6144,256]{1,0:T(8,128)(2,1)}) %all-gather.3.cloned.1.call-update) | async-done | bytes 3145744 | tf_op jit(solution)/shard_map/all_gather | solution.py:33
  117.8 0.0 copy-done
  117.8 5.2 %fusion.4 = (f32[4,192]{1,0:T(4,128)S(1)}, f32[6144,192,4]{0,1,2:T(8,128)S(1)}) fusion(pred[192,6144]{1,0:T(8,128)(4,1)S(1)} %fusion.19, bf16[6144,256]{1,0:T(8,128)(2,1)} %all-gather.3.cloned.1.call-done, bf16[192,512]{1,0:T(8,128)(2,1)S(1)} %copy-done), kind=kOutput, calls=%fused_computation.9 | convolution fusion | flops 1222114560 | bytes 21826560 | tf_op jit(solution)/shard_map/sghd,kgd->ghsk/dot_general | solution.py:49
  123.0 0.0 copy-start.2
  123.0 6.3 %select_reduce_fusion = f32[4,192]{1,0:T(4,128)S(1)} fusion(f32[6144,192,4]{0,1,2:T(8,128)S(1)} %get-tuple-element.18, f32[4,192]{1,0:T(4,128)S(1)} %get-tuple-element.17, pred[192,6144]{1,0:T(8,128)(4,1)S(1)} %fusion.19), kind=kLoop, calls=%fused_computation.8 | loop fusion | flops 23592192 | bytes 20060160 | tf_op jit(solution)/shard_map/reduce_sum | solution.py:55
  129.4 0.1 copy-done.2
  129.5 5.8 %fusion.16 = bf16[6144,128]{0,1:T(8,128)(2,1)S(1)} fusion(f32[4,192]{1,0:T(4,128)S(1)} %log_add_fusion, f32[6144,192,4]{0,1,2:T(8,128)S(1)} %get-tuple-element.18, pred[192,6144]{1,0:T(8,128)(4,1)S(1)} %fusion.19, bf16[24,4,8,128]{3,2,1,0:T(8,128)(2,1)S(1)} %fusion.25), kind=kOutput, calls=%fused_computation.18 | convolution fusion | flops 1232338944 | bytes 21826560 | tf_op jit(solution)/shard_map/ghsk,sghd->kgd/dot_general | solution.py:68
  135.3 14.9 %fusion = (f32[4,192]{1,0:T(4,128)S(1)}, f32[6144,192,4]{0,1,2:T(8,128)}) fusion(f32[4,192]{1,0:T(4,128)S(1)} %log_add_fusion, f32[6144,192,4]{0,1,2:T(8,128)} %copy-done.2, pred[192,6144]{1,0:T(8,128)(4,1)S(1)} %fusion.19, bf16[24,4,8,128]{3,2,1,0:T(8,128)(2,1)S(1)} %fusion.25, bf16[6144,256]{1,0:T(8,128)(2,1)} %all-gather.3.cloned.1.call-done), kind=kOutput, calls=%fused_computation.3 | convolution fusion | flops 1236270336 | bytes 40704000 | tf_op jit(solution)/shard_map/sghd,kgd->ghsk/dot_general | solution.py:58
  150.2 13.9 %fusion.5 = bf16[4,192,6144]{2,1,0:T(8,128)(2,1)S(1)} fusion(f32[6144,192,4]{0,1,2:T(8,128)} %get-tuple-element.20, f32[4,192]{1,0:T(4,128)S(1)} %get-tuple-element.19, f32[4,192]{1,0:T(4,128)S(1)} %log_add_fusion, f32[6144,192,4]{0,1,2:T(8,128)} %copy-done.2, pred[192,6144]{1,0:T(8,128)(4,1)S(1)} %fusion.19), kind=kLoop, calls=%fused_computation.10 | loop fusion | flops 37748736 | bytes 48371712 | tf_op jit(solution)/shard_map/reshape.22
  164.1 0.0 copy-start.1
  164.2 3.6 %copy-done.1 = bf16[4,192,6144]{2,1,0:T(8,128)(2,1)} copy-done((bf16[4,192,6144]{2,1,0:T(8,128)(2,1)}, bf16[4,192,6144]{2,1,0:T(8,128)(2,1)S(1)}, u32[]{:S(2)}) %copy-start.1) | copy-done | bytes 9437208
  167.8 1.6 fusion.12
  169.3 0.3 pad_maximum_fusion
  169.6 2.8 %copy.36 = bf16[6144,256]{1,0:T(8,128)(2,1)} copy(bf16[6144,256]{0,1:T(8,128)(2,1)S(1)} %pad_maximum_fusion) | data formatting | bytes 6291456
  172.4 0.0 reduce-scatter.4.cloned.1.call-update
  172.5 6.8 %fusion.24 = bf16[192,1,4,128]{3,0,2,1:T(8,128)(2,1)S(1)} fusion(bf16[4,192,6144]{2,1,0:T(8,128)(2,1)} %copy-done.1, bf16[6144,256]{1,0:T(8,128)(2,1)} %all-gather.3.cloned.1.call-done), kind=kOutput, calls=%fused_computation.29 | convolution fusion | flops 1208057856 | bytes 11206656 | tf_op jit(solution)/shard_map/ghsk,kgd->sghd/dot_general | solution.py:64
  179.2 0.2 copy.31
  179.4 0.7 copy.64
  180.1 86.1 %reduce-scatter.4.cloned.1.call-done = bf16[192,256]{1,0:T(8,128)(2,1)} async-done(((bf16[6144,256]{1,0:T(8,128)(2,1)}), bf16[192,256]{1,0:T(8,128)(2,1)}) %reduce-scatter.4.cloned.1.call-update) | async-done | bytes 98320
  266.2 1.5 fusion.37
  (2 shorter events, 0.0 us)
Async XLA Ops:
  7.2 110.6 %copy-start = (bf16[192,512]{1,0:T(8,128)(2,1)S(1)}, bf16[192,512]{1,0:T(8,128)(2,1)}, u32[]{:S(2)}) copy-start(bf16[192,512]{1,0:T(8,128)(2,1)} %param.6) | copy-start | bytes 589828
  7.2 49.8 %all-gather.5.cloned.1.call-start = ((), (), s32[]{:S(2)}) async-start(), calls=%async_computation.2 | async-start | bytes 1769472 | tf_op jit(solution)/shard_map/all_gather | solution.py:37
  7.9 109.9 %all-gather.3.cloned.1.call-start = ((), (), s32[]{:S(2)}) async-start(), calls=%async_computation.1 | async-start | bytes 3244032 | tf_op jit(solution)/shard_map/all_gather | solution.py:33
  9.5 256.7 %reduce-scatter.4.cloned.1.call-start = ((), (), s32[]{:S(2)}) async-start(), calls=%async_computation.3 | async-start | bytes 3244032
  123.0 6.5 %copy-start.2 = (f32[6144,192,4]{0,1,2:T(8,128)}, f32[6144,192,4]{0,1,2:T(8,128)S(1)}, u32[]{:S(2)}) copy-start(f32[6144,192,4]{0,1,2:T(8,128)S(1)} %get-tuple-element.18) | copy-start | bytes 56623108
  164.1 3.6 %copy-start.1 = (bf16[4,192,6144]{2,1,0:T(8,128)(2,1)}, bf16[4,192,6144]{2,1,0:T(8,128)(2,1)S(1)}, u32[]{:S(2)}) copy-start(bf16[4,192,6144]{2,1,0:T(8,128)(2,1)S(1)} %fusion.5) | copy-start | bytes 28311556
Sparse Core Ops, SparseCore 0:
  9.8 47.1 all-gather.4
  60.1 57.6 all-gather.2
  172.6 93.5 reduce-scatter.3

commit v2 on v1

--- a/solution.py
+++ b/solution.py
@@ -1,9 +1,12 @@
+import functools
 import math
 
 import jax
 import jax.numpy as jnp
 from jax import lax
 from jax.sharding import PartitionSpec as P
+from jax.experimental import pallas as pl
+from jax.experimental.pallas import tpu as pltpu
 
 DH = 128
 
@@ -21,6 +24,62 @@
     return (earlier & same_doc)[None, None]
 
 
+def _peer_kernel(n, axis, upward, per_target, src_ref, out_ref, send_sem, recv_sem):
+    me = lax.axis_index(axis)
+    step = 1 if upward else -1
+
+    def send_desc(k):
+        tgt = me + step * k
+        src = src_ref.at[tgt] if per_target else src_ref
+        return pltpu.make_async_remote_copy(
+            src, out_ref.at[me], send_sem.at[k - 1], recv_sem.at[k - 1],
+            device_id={axis: tgt}, device_id_type=pl.DeviceIdType.MESH)
+
+    def recv_desc(k):
+        origin = me - step * k
+        src = src_ref.at[me] if per_target else src_ref
+        return pltpu.make_async_remote_copy(
+            src, out_ref.at[origin], send_sem.at[k - 1], recv_sem.at[k - 1],
+            device_id={axis: origin}, device_id_type=pl.DeviceIdType.MESH)
+
+    def can_send(k):
+        return (me + k < n) if upward else (me - k >= 0)
+
+    def can_recv(k):
+        return (me - k >= 0) if upward else (me + k < n)
+
+    def start_one(k, carry):
+        @pl.when(can_send(k))
+        def _():
+            send_desc(k).start()
+        return carry
+
+    def finish_one(k, carry):
+        @pl.when(can_send(k))
+        def _():
+            send_desc(k).wait_send()
+
+        @pl.when(can_recv(k))
+        def _():
+            recv_desc(k).wait_recv()
+        return carry
+
+    lax.fori_loop(1, n, start_one, 0)
+    lax.fori_loop(1, n, finish_one, 0)
+
+
+def peer_blocks(src, n, axis, upward, per_target):
+    blk = src.shape[1:] if per_target else src.shape
+    return pl.pallas_call(
+        functools.partial(_peer_kernel, n, axis, upward, per_target),
+        out_shape=jax.ShapeDtypeStruct((n,) + tuple(blk), src.dtype),
+        in_specs=[pl.BlockSpec(memory_space=pl.ANY)],
+        out_specs=pl.BlockSpec(memory_space=pl.ANY),
+        scratch_shapes=[pltpu.SemaphoreType.DMA((n - 1,)), pltpu.SemaphoreType.DMA((n - 1,))],
+        compiler_params=pltpu.CompilerParams(has_side_effects=True),
+    )(src)
+
+
 def shards(queries, keys, values, d_out, w_out, doc_starts):
     rows_here = queries.shape[0]
     head_size = DH
@@ -30,9 +89,14 @@
     scaling = 1.0 / math.sqrt(head_size)
     first_row = lax.axis_index("seq") * rows_here
     my_rows = first_row + jnp.arange(rows_here, dtype=jnp.int32)
-    kv_block = lax.all_gather(
-        jnp.concatenate([keys, values], axis=1), "seq", axis=0, tiled=True
-    )
+    n_seq = lax.axis_size("seq")
+    me = lax.axis_index("seq")
+    kv_here = jnp.concatenate([keys, values], axis=1)
+    kv_slots = peer_blocks(kv_here, n_seq, "seq", True, False)
+    slot_ids = jnp.arange(n_seq, dtype=jnp.int32)[:, None, None]
+    kv_block = jnp.where(
+        slot_ids == me, kv_here[None], jnp.where(slot_ids < me, kv_slots, 0)
+    ).reshape(n_seq * rows_here, 2 * keys.shape[1])
     attn_grad = lax.dot_general(
         lax.all_gather(d_out, "head", axis=1, tiled=True),
         w_out,
@@ -68,10 +132,14 @@
     value_terms = jnp.einsum(
         "ghsk,sghd->kgd", prob_half, grad_four, preferred_element_type=jnp.float32
     ).reshape(piece_rows, kv_cols)
-    kv_grad = lax.psum_scatter(
-        jnp.concatenate([key_terms, value_terms], axis=1).astype(jnp.bfloat16),
-        "seq", scatter_dimension=0, tiled=True,
+    kv_terms = jnp.concatenate([key_terms, value_terms], axis=1).reshape(
+        n_seq, rows_here, 2 * kv_cols
     )
+    kv_recv = peer_blocks(kv_terms.astype(jnp.bfloat16), n_seq, "seq", False, True)
+    kv_grad = (
+        jnp.sum(jnp.where(slot_ids > me, kv_recv.astype(jnp.float32), 0.0), axis=0)
+        + lax.dynamic_index_in_dim(kv_terms, me, 0, keepdims=False)
+    ).astype(jnp.bfloat16)
     query_grad = query_acc.reshape(rows_here, groups * per_group * head_size).astype(jnp.bfloat16)
     key_grad = kv_grad[:, :kv_cols]
     value_grad = kv_grad[:, kv_cols:]

time: 274 us -> 361 us (1.32)
  the two profiles are of different devices: /device:TPU:8 before, /device:TPU:32 now
where the time goes in v2:
time: 361 us; the launch traced here: 360 us
  Pallas kernels  217 us (60%)
  matrix products  62.2 us (17%)
  other arithmetic  34.3 us (10%)
  local copies, waits for them, and re-layouts  30.8 us (9%)
  between operations  14.2 us (4%)
    pallas_call x2, Pallas kernels, peer_blocks(): pl.pallas_call(functools.partial(_peer_kernel, n, axis, upward, per_targe...  217 us
    dot_general x1, matrix products, shards(): jnp.einsum('ghsk,sghd->kgd', dscores, query_four, preferred_element_type=...  22.3 us
    dot_general x1, local copies, waits for them, and re-layouts, shards(): jnp.einsum('ghsk,sghd->kgd', dscores, query_four, preferred_element_type=...  21 us
    dot_general x1, matrix products, shards(): jnp.einsum('sghd,kgd->ghsk', grad_four, value_three, preferred_element_ty...  17 us
    convert_element_type x1, other arithmetic, shards(): (prob_full * (grad_dots - row_delta[..., None]) * scaling).astype(jnp.bfl...  13.9 us
    dot_general x1, matrix products, shards(): jnp.einsum('ghsk,sghd->kgd', prob_half, grad_four, preferred_element_type...  10.8 us
  transfers between devices with their start and end apart: 1, of which 0 were waited for; matrix products, arithmetic and copies ran while one was open for 5% of the time, Pallas kernels for 27%

profile of v2, /device:TPU:32, one launch (start us, length us, event | category | flops | bytes accessed | tf_op | source)
XLA Modules:
  0.0 359.6 jit_solution(8189246820225960045)
XLA Ops:
  7.2 0.0 copy-start
  7.2 0.0 all-gather.2.cloned.1.call-start
  7.2 0.7 all-gather.2.cloned.1.call-update
  8.0 0.8 convert_reduce_fusion
  8.8 0.7 convert_reduce_fusion.1
  9.5 0.8 constant_dynamic-update-slice_fusion.1
  10.3 0.8 constant_dynamic-update-slice_fusion.src_ref
  11.1 0.0 copy-start.4
  11.1 0.6 copy-done.4
  11.8 98.7 %shard_map.85 = bf16[32,192,256]{2,1,0:T(8,128)(2,1)} custom-call(bf16[192,256]{1,0:T(8,128)(2,1)} %copy-done.4), custom_call_target="tpu_custom_call" | custom-call | tf_op jit(solution)/shard_map/pallas_call | solution.py:73
  110.5 1.0 fusion.16
  111.5 3.9 %select_select_fusion = bf16[32,192,256]{2,1,0:T(8,128)(2,1)} fusion(bf16[32,192,256]{2,1,0:T(8,128)(2,1)} %shard_map.85, pred[32]{0:T(512)(128)(4,1)S(1)} %get-tuple-element.10, pred[32]{0:T(512)(128)(4,1)S(1)} %iota_compare_fusion.4, bf16[192,256]{1,0:T(8,128)(2,1)} %copy-done.4), kind=kLoop, calls=%fused_computation.25 | loop fusion | flops 3145728 | bytes 6389824 | tf_op jit(solution)/shard_map/jit(_where)/select_n | solution.py:97
  115.4 0.0 copy-done
  115.4 5.2 %fusion.4 = (f32[4,192]{1,0:T(4,128)S(1)}, f32[6144,192,4]{0,1,2:T(8,128)S(1)}) fusion(pred[192,6144]{1,0:T(8,128)(4,1)S(1)} %fusion.16, bf16[6144,256]{1,0:T(8,128)(2,1)} %bitcast.118, bf16[192,512]{1,0:T(8,128)(2,1)S(1)} %copy-done), kind=kOutput, calls=%fused_computation.9 | convolution fusion | flops 1222114560 | bytes 21826560 | tf_op jit(solution)/shard_map/sghd,kgd->ghsk/dot_general | solution.py:113
  120.6 0.0 copy-start.2
  120.6 6.3 %select_reduce_fusion = f32[4,192]{1,0:T(4,128)S(1)} fusion(f32[6144,192,4]{0,1,2:T(8,128)S(1)} %get-tuple-element.6, f32[4,192]{1,0:T(4,128)S(1)} %get-tuple-element.5, pred[192,6144]{1,0:T(8,128)(4,1)S(1)} %fusion.16), kind=kLoop, calls=%fused_computation.8 | loop fusion | flops 23592192 | bytes 20060160 | tf_op jit(solution)/shard_map/reduce_sum | solution.py:119
  127.0 0.1 copy-done.2
  127.1 0.0 all-gather.2.cloned.1.call-done
  127.1 0.0 copy-start.3
  127.1 4.3 %fusion.28 = bf16[24,4,8,128]{3,2,1,0:T(8,128)(2,1)S(1)} fusion(bf16[192,4096]{1,0:T(8,128)(2,1)} %all-gather.2.cloned.1.call-done, bf16[512,4096]{1,0:T(8,128)(2,1)} %param.10), kind=kOutput, calls=%fused_computation.34 | convolution fusion | flops 805404672 | bytes 5963776 | tf_op jit(solution)/shard_map/dot_general | solution.py:100
  131.5 0.0 copy-done.3
  131.5 17.0 %fusion = (f32[4,192]{1,0:T(4,128)S(1)}, f32[6144,192,4]{0,1,2:T(8,128)}) fusion(f32[4,192]{1,0:T(4,128)S(1)} %log_add_fusion, f32[6144,192,4]{0,1,2:T(8,128)} %copy-done.2, pred[192,6144]{1,0:T(8,128)(4,1)S(1)} %fusion.16, bf16[24,4,8,128]{3,2,1,0:T(8,128)(2,1)S(1)} %fusion.28, bf16[6144,256]{1,0:T(8,128)(2,1)S(1)} %bitcast.119), kind=kOutput, calls=%fused_computation.3 | convolution fusion | flops 1236270336 | bytes 40705024 | tf_op jit(solution)/shard_map/sghd,kgd->ghsk/dot_general | solution.py:122
  148.5 10.8 %fusion.12 = f32[6144,1,128]{0,2,1:T(8,128)} fusion(f32[4,192]{1,0:T(4,128)S(1)} %log_add_fusion, f32[6144,192,4]{0,1,2:T(8,128)} %copy-done.2, pred[192,6144]{1,0:T(8,128)(4,1)S(1)} %fusion.16, bf16[24,4,8,128]{3,2,1,0:T(8,128)(2,1)S(1)} %fusion.28), kind=kOutput, calls=%fused_computation.20 | convolution fusion | flops 1231552512 | bytes 23399424 | tf_op jit(solution)/shard_map/ghsk,sghd->kgd/dot_general | solution.py:132
  159.3 13.9 %fusion.3 = bf16[1,4,192,6144]{3,2,1,0:T(8,128)(2,1)S(1)} fusion(f32[6144,192,4]{0,1,2:T(8,128)} %get-tuple-element.8, f32[4,192]{1,0:T(4,128)S(1)} %get-tuple-element.7, f32[4,192]{1,0:T(4,128)S(1)} %log_add_fusion, f32[6144,192,4]{0,1,2:T(8,128)} %copy-done.2, pred[192,6144]{1,0:T(8,128)(4,1)S(1)} %fusion.16), kind=kLoop, calls=%fused_computation.6 | loop fusion | flops 37748736 | bytes 48371712 | tf_op jit(solution)/shard_map/convert_element_type | solution.py:126
  173.2 0.0 copy-start.1
  173.2 3.6 copy-done.1
  176.8 2.6 fusion.25
  179.4 21.0 %dot_general.32 = bf16[32,192,4,192]{1,0,3,2:T(8,128)(2,1)} reshape(bf16[6144,4,192]{0,2,1:T(8,128)(2,1)} %bitcast.115) | data formatting | bytes 18874368 | tf_op jit(solution)/shard_map/ghsk,sghd->kgd/dot_general | solution.py:129
  200.4 22.3 %fusion.17 = f32[32,192,128]{2,1,0:T(8,128)} fusion(bf16[32,192,4,192]{1,0,3,2:T(8,128)(2,1)} %dot_general.32, bf16[192,512]{1,0:T(8,128)(2,1)S(1)} %copy-done), kind=kOutput, calls=%fused_computation.26 | convolution fusion | flops 1207959552 | bytes 12779520 | tf_op jit(solution)/shard_map/ghsk,sghd->kgd/dot_general | solution.py:129
  222.6 2.4 copy.28
  225.0 3.9 %fusion.15.src_ref = bf16[32,192,256]{2,1,0:T(8,128)(2,1)} fusion(f32[32,192,128]{2,1,0:T(8,128)S(1)} %bitcast.116, f32[32,192,128]{2,1,0:T(8,128)} %fusion.17), kind=kLoop, calls=%fused_computation.21 | loop fusion | flops 6291456 | bytes 9437184 | tf_op jit(solution)/shard_map/convert_element_type | solution.py:138
  228.9 118.7 %shard_map.86 = bf16[32,192,256]{2,1,0:T(8,128)(2,1)} custom-call(bf16[32,192,256]{2,1,0:T(8,128)(2,1)} %fusion.15.src_ref), custom_call_target="tpu_custom_call" | custom-call | tf_op jit(solution)/shard_map/pallas_call | solution.py:73
  347.6 2.7 select_reduce_fusion.1
  350.4 0.9 fusion.33
  351.3 0.6 fusion.41
  351.9 0.2 copy.24
  352.1 0.7 copy.58
  (4 shorter events, 0.0 us)
Async XLA Ops:
  7.2 108.2 %copy-start = (bf16[192,512]{1,0:T(8,128)(2,1)S(1)}, bf16[192,512]{1,0:T(8,128)(2,1)}, u32[]{:S(2)}) copy-start(bf16[192,512]{1,0:T(8,128)(2,1)} %param.6) | copy-start | bytes 589828
  7.2 119.9 %all-gather.2.cloned.1.call-start = ((), (), s32[]{:S(2)}) async-start(), calls=%async_computation | async-start | bytes 1769472 | tf_op jit(solution)/shard_map/all_gather | solution.py:101
  11.1 0.6 copy-start.4
  120.6 6.5 %copy-start.2 = (f32[6144,192,4]{0,1,2:T(8,128)}, f32[6144,192,4]{0,1,2:T(8,128)S(1)}, u32[]{:S(2)}) copy-start(f32[6144,192,4]{0,1,2:T(8,128)S(1)} %get-tuple-element.6) | copy-start | bytes 56623108
  127.1 4.4 %copy-start.3 = (bf16[32,192,256]{2,1,0:T(8,128)(2,1)S(1)}, bf16[32,192,256]{2,1,0:T(8,128)(2,1)}, u32[]{:S(2)}) copy-start(bf16[32,192,256]{2,1,0:T(8,128)(2,1)} %select_select_fusion) | copy-start | bytes 9437188
  173.2 3.6 copy-start.1
Sparse Core Ops, SparseCore 0:
  9.8 92.9 all-gather.1

commit v3 on v2

--- a/solution.py
+++ b/solution.py
@@ -26,26 +26,30 @@
 
 def _peer_kernel(n, axis, upward, per_target, src_ref, out_ref, send_sem, recv_sem):
     me = lax.axis_index(axis)
-    step = 1 if upward else -1
+    step = -1 if upward is False else 1
 
     def send_desc(k):
-        tgt = me + step * k
+        tgt = lax.rem(me + k, n) if upward is None else me + step * k
         src = src_ref.at[tgt] if per_target else src_ref
         return pltpu.make_async_remote_copy(
             src, out_ref.at[me], send_sem.at[k - 1], recv_sem.at[k - 1],
             device_id={axis: tgt}, device_id_type=pl.DeviceIdType.MESH)
 
     def recv_desc(k):
-        origin = me - step * k
+        origin = lax.rem(me + n - k, n) if upward is None else me - step * k
         src = src_ref.at[me] if per_target else src_ref
         return pltpu.make_async_remote_copy(
             src, out_ref.at[origin], send_sem.at[k - 1], recv_sem.at[k - 1],
             device_id={axis: origin}, device_id_type=pl.DeviceIdType.MESH)
 
     def can_send(k):
+        if upward is None:
+            return k > 0
         return (me + k < n) if upward else (me - k >= 0)
 
     def can_recv(k):
+        if upward is None:
+            return k > 0
         return (me - k >= 0) if upward else (me + k < n)
 
     def start_one(k, carry):
@@ -89,18 +93,18 @@
     scaling = 1.0 / math.sqrt(head_size)
     first_row = lax.axis_index("seq") * rows_here
     my_rows = first_row + jnp.arange(rows_here, dtype=jnp.int32)
-    n_seq = lax.axis_size("seq")
-    me = lax.axis_index("seq")
-    kv_here = jnp.concatenate([keys, values], axis=1)
-    kv_slots = peer_blocks(kv_here, n_seq, "seq", True, False)
-    slot_ids = jnp.arange(n_seq, dtype=jnp.int32)[:, None, None]
-    kv_block = jnp.where(
-        slot_ids == me, kv_here[None], jnp.where(slot_ids < me, kv_slots, 0)
-    ).reshape(n_seq * rows_here, 2 * keys.shape[1])
-    attn_grad = lax.dot_general(
-        lax.all_gather(d_out, "head", axis=1, tiled=True),
-        w_out,
-        (((1,), (1,)), ((), ())),
+    kv_block = lax.all_gather(
+        jnp.concatenate([keys, values], axis=1), "seq", axis=0, tiled=True
+    )
+    n_head = lax.axis_size("head")
+    me_head = lax.axis_index("head")
+    d_slots = peer_blocks(d_out, n_head, "head", None, False)
+    head_ids = jnp.arange(n_head, dtype=jnp.int32)[:, None, None]
+    d_all = jnp.where(head_ids == me_head, d_out[None], d_slots)
+    attn_grad = jnp.einsum(
+        "hte,che->tc",
+        d_all,
+        w_out.reshape(w_out.shape[0], n_head, d_out.shape[1]),
         preferred_element_type=jnp.float32,
     ).astype(jnp.bfloat16)
     query_four = queries.reshape(rows_here, groups, per_group, head_size)
@@ -132,14 +136,10 @@
     value_terms = jnp.einsum(
         "ghsk,sghd->kgd", prob_half, grad_four, preferred_element_type=jnp.float32
     ).reshape(piece_rows, kv_cols)
-    kv_terms = jnp.concatenate([key_terms, value_terms], axis=1).reshape(
-        n_seq, rows_here, 2 * kv_cols
+    kv_grad = lax.psum_scatter(
+        jnp.concatenate([key_terms, value_terms], axis=1).astype(jnp.bfloat16),
+        "seq", scatter_dimension=0, tiled=True,
     )
-    kv_recv = peer_blocks(kv_terms.astype(jnp.bfloat16), n_seq, "seq", False, True)
-    kv_grad = (
-        jnp.sum(jnp.where(slot_ids > me, kv_recv.astype(jnp.float32), 0.0), axis=0)
-        + lax.dynamic_index_in_dim(kv_terms, me, 0, keepdims=False)
-    ).astype(jnp.bfloat16)
     query_grad = query_acc.reshape(rows_here, groups * per_group * head_size).astype(jnp.bfloat16)
     key_grad = kv_grad[:, :kv_cols]
     value_grad = kv_grad[:, kv_cols:]

time: 361 us -> 229 us (0.63)
  the two profiles are of different devices: /device:TPU:32 before, /device:TPU:8 now
where the time goes in v3:
time: 229 us
  waiting for transfers between devices  106 us (46%)
  matrix products  38.8 us (17%)
  Pallas kernels  36 us (16%)
  other arithmetic  24.6 us (11%)
  between operations  14.2 us (6%)
  local copies, waits for them, and re-layouts  8.88 us (4%)
    unnamed x3, waiting for transfers between devices  86 us
    pallas_call x1, Pallas kernels, peer_blocks(): pl.pallas_call(functools.partial(_peer_kernel, n, axis, upward, per_targe...  36 us
    all_gather x1, waiting for transfers between devices, shards(): lax.all_gather(jnp.concatenate([keys, values], axis=1), 'seq', axis=0, ti...  20.2 us
    dot_general x1, matrix products, shards(): jnp.einsum('sghd,kgd->ghsk', grad_four, value_three, preferred_element_ty...  15.1 us
    another operation x1, other arithmetic  13.9 us
    unnamed x8, local copies, waits for them, and re-layouts  7.26 us
    dot_general x1, matrix products, shards(): jnp.einsum('ghsk,kgd->sghd', dscores, key_three, preferred_element_type=j...  6.77 us
    reduce_sum x1, other arithmetic, shards(): total = jnp.sum(weights, axis=-1)  6.34 us
  transfers between devices with their start and end apart: 2, of which 2 were waited for; matrix products, arithmetic and copies ran while one was open for 6% of the time, Pallas kernels for 16%

profile of v3, /device:TPU:8, one launch (start us, length us, event | category | flops | bytes accessed | tf_op | source)
XLA Modules:
  0.0 228.7 jit_solution(17978769890286422323)
XLA Ops:
  7.2 0.0 copy-start
  7.2 0.0 all-gather.2.cloned.1.call-start
  7.2 1.5 pad_maximum_fusion.1
  8.7 0.0 all-gather.2.cloned.1.call-update
  8.8 0.0 reduce-scatter.4.cloned.1.call-start
  8.8 36.0 %shard_map.85 = bf16[8,192,512]{2,1,0:T(8,128)(2,1)} custom-call(bf16[192,512]{1,0:T(8,128)(2,1)} %src_ref.1), custom_call_target="tpu_custom_call" | custom-call | tf_op jit(solution)/shard_map/pallas_call | solution.py:77
  44.9 0.7 convert_reduce_fusion.1
  45.6 0.8 convert_reduce_fusion
  46.4 4.3 %fusion.40 = bf16[24,4,8,128]{3,2,1,0:T(8,128)(2,1)S(1)} fusion(bf16[64,8,8,512]{3,2,1,0:T(8,128)(2,1)} %bitcast.134, bf16[8,192,512]{2,1,0:T(8,128)(2,1)} %shard_map.85, pred[8]{0:T(512)(128)(4,1)S(1)} %iota_compare_fusion.2, bf16[192,512]{1,0:T(8,128)(2,1)} %src_ref.1), kind=kOutput, calls=%fused_computation.36 | convolution fusion | flops 806191104 | bytes 6160392 | tf_op jit(solution)/shard_map/hte,che->tc/dot_general | solution.py:104
  50.7 1.0 fusion.19
  51.8 20.2 %all-gather.2.cloned.1.call-done = bf16[6144,256]{1,0:T(8,128)(2,1)} async-done(((bf16[192,256]{1,0:T(8,128)(2,1)}), bf16[6144,256]{1,0:T(8,128)(2,1)}) %all-gather.2.cloned.1.call-update) | async-done | bytes 3145744 | tf_op jit(solution)/shard_map/all_gather | solution.py:96
  72.0 0.0 copy-done
  72.0 5.2 %fusion.4 = (f32[4,192]{1,0:T(4,128)S(1)}, f32[6144,192,4]{0,1,2:T(8,128)S(1)}) fusion(pred[192,6144]{1,0:T(8,128)(4,1)S(1)} %fusion.19, bf16[6144,256]{1,0:T(8,128)(2,1)} %all-gather.2.cloned.1.call-done, bf16[192,512]{1,0:T(8,128)(2,1)S(1)} %copy-done), kind=kOutput, calls=%fused_computation.9 | convolution fusion | flops 1222114560 | bytes 21826560 | tf_op jit(solution)/shard_map/sghd,kgd->ghsk/dot_general | solution.py:117
  77.2 0.0 copy-start.2
  77.2 6.3 %select_reduce_fusion = f32[4,192]{1,0:T(4,128)S(1)} fusion(f32[6144,192,4]{0,1,2:T(8,128)S(1)} %get-tuple-element.18, f32[4,192]{1,0:T(4,128)S(1)} %get-tuple-element.17, pred[192,6144]{1,0:T(8,128)(4,1)S(1)} %fusion.19), kind=kLoop, calls=%fused_computation.8 | loop fusion | flops 23592192 | bytes 20060160 | tf_op jit(solution)/shard_map/reduce_sum | solution.py:123
  83.6 0.1 copy-done.2
  83.7 5.8 %fusion.16 = bf16[6144,128]{0,1:T(8,128)(2,1)S(1)} fusion(f32[4,192]{1,0:T(4,128)S(1)} %log_add_fusion, f32[6144,192,4]{0,1,2:T(8,128)S(1)} %get-tuple-element.18, pred[192,6144]{1,0:T(8,128)(4,1)S(1)} %fusion.19, bf16[24,4,8,128]{3,2,1,0:T(8,128)(2,1)S(1)} %fusion.40), kind=kOutput, calls=%fused_computation.18 | convolution fusion | flops 1232338944 | bytes 21826560 | tf_op jit(solution)/shard_map/ghsk,sghd->kgd/dot_general | solution.py:136
  89.5 15.1 %fusion = (f32[4,192]{1,0:T(4,128)S(1)}, f32[6144,192,4]{0,1,2:T(8,128)}) fusion(f32[4,192]{1,0:T(4,128)S(1)} %log_add_fusion, f32[6144,192,4]{0,1,2:T(8,128)} %copy-done.2, pred[192,6144]{1,0:T(8,128)(4,1)S(1)} %fusion.19, bf16[24,4,8,128]{3,2,1,0:T(8,128)(2,1)S(1)} %fusion.40, bf16[6144,256]{1,0:T(8,128)(2,1)} %all-gather.2.cloned.1.call-done), kind=kOutput, calls=%fused_computation.3 | convolution fusion | flops 1236270336 | bytes 40704000 | tf_op jit(solution)/shard_map/sghd,kgd->ghsk/dot_general | solution.py:126
  104.6 13.9 %fusion.5 = bf16[4,192,6144]{2,1,0:T(8,128)(2,1)S(1)} fusion(f32[6144,192,4]{0,1,2:T(8,128)} %get-tuple-element.20, f32[4,192]{1,0:T(4,128)S(1)} %get-tuple-element.19, f32[4,192]{1,0:T(4,128)S(1)} %log_add_fusion, f32[6144,192,4]{0,1,2:T(8,128)} %copy-done.2, pred[192,6144]{1,0:T(8,128)(4,1)S(1)} %fusion.19), kind=kLoop, calls=%fused_computation.10 | loop fusion | flops 37748736 | bytes 48371712 | tf_op jit(solution)/shard_map/reshape.23
  118.5 0.0 copy-start.1
  118.5 3.6 %copy-done.1 = bf16[4,192,6144]{2,1,0:T(8,128)(2,1)} copy-done((bf16[4,192,6144]{2,1,0:T(8,128)(2,1)}, bf16[4,192,6144]{2,1,0:T(8,128)(2,1)S(1)}, u32[]{:S(2)}) %copy-start.1) | copy-done | bytes 9437208
  122.1 1.6 fusion.12
  123.7 0.3 pad_maximum_fusion
  124.0 2.8 %copy.40 = bf16[6144,256]{1,0:T(8,128)(2,1)} copy(bf16[6144,256]{0,1:T(8,128)(2,1)S(1)} %pad_maximum_fusion) | data formatting | bytes 6291456
  126.8 0.0 reduce-scatter.4.cloned.1.call-update
  126.8 6.8 %fusion.39 = bf16[192,1,4,128]{3,0,2,1:T(8,128)(2,1)S(1)} fusion(bf16[4,192,6144]{2,1,0:T(8,128)(2,1)} %copy-done.1, bf16[6144,256]{1,0:T(8,128)(2,1)} %all-gather.2.cloned.1.call-done), kind=kOutput, calls=%fused_computation.35 | convolution fusion | flops 1208057856 | bytes 11206656 | tf_op jit(solution)/shard_map/ghsk,kgd->sghd/dot_general | solution.py:132
  133.6 0.2 copy.35
  133.8 0.7 copy.79
  134.5 86.0 %reduce-scatter.4.cloned.1.call-done = bf16[192,256]{1,0:T(8,128)(2,1)} async-done(((bf16[6144,256]{1,0:T(8,128)(2,1)}), bf16[192,256]{1,0:T(8,128)(2,1)}) %reduce-scatter.4.cloned.1.call-update) | async-done | bytes 98320
  220.4 1.5 fusion.57
  (3 shorter events, 0.0 us)
Async XLA Ops:
  7.2 64.8 %copy-start = (bf16[192,512]{1,0:T(8,128)(2,1)S(1)}, bf16[192,512]{1,0:T(8,128)(2,1)}, u32[]{:S(2)}) copy-start(bf16[192,512]{1,0:T(8,128)(2,1)} %param.6) | copy-start | bytes 589828
  7.2 64.8 %all-gather.2.cloned.1.call-start = ((), (), s32[]{:S(2)}) async-start(), calls=%async_computation.1 | async-start | bytes 3244032 | tf_op jit(solution)/shard_map/all_gather | solution.py:96
  8.8 211.7 %reduce-scatter.4.cloned.1.call-start = ((), (), s32[]{:S(2)}) async-start(), calls=%async_computation.2 | async-start | bytes 3244032
  77.2 6.5 %copy-start.2 = (f32[6144,192,4]{0,1,2:T(8,128)}, f32[6144,192,4]{0,1,2:T(8,128)S(1)}, u32[]{:S(2)}) copy-start(f32[6144,192,4]{0,1,2:T(8,128)S(1)} %get-tuple-element.18) | copy-start | bytes 56623108
  118.5 3.6 %copy-start.1 = (bf16[4,192,6144]{2,1,0:T(8,128)(2,1)}, bf16[4,192,6144]{2,1,0:T(8,128)(2,1)S(1)}, u32[]{:S(2)}) copy-start(bf16[4,192,6144]{2,1,0:T(8,128)(2,1)S(1)} %fusion.5) | copy-start | bytes 28311556
Sparse Core Ops, SparseCore 0:
  11.1 60.7 all-gather.1
  126.9 93.4 reduce-scatter.3

commit v4 on v3

--- a/solution.py
+++ b/solution.py
@@ -91,10 +91,15 @@
     per_group = queries.shape[1] // keys.shape[1]
     kv_cols = keys.shape[1]
     scaling = 1.0 / math.sqrt(head_size)
-    first_row = lax.axis_index("seq") * rows_here
+    n_hi = lax.axis_size("seqhi")
+    n_core = lax.axis_size("core")
+    my_core = lax.axis_index("core")
+    me = lax.axis_index("seqhi") * n_core + my_core
+    first_row = me * rows_here
     my_rows = first_row + jnp.arange(rows_here, dtype=jnp.int32)
     kv_block = lax.all_gather(
-        jnp.concatenate([keys, values], axis=1), "seq", axis=0, tiled=True
+        lax.all_gather(jnp.concatenate([keys, values], axis=1), "seqhi", axis=0),
+        "core", axis=0,
     )
     n_head = lax.axis_size("head")
     me_head = lax.axis_index("head")
@@ -109,8 +114,12 @@
     ).astype(jnp.bfloat16)
     query_four = queries.reshape(rows_here, groups, per_group, head_size)
     grad_four = attn_grad.reshape(rows_here, groups, per_group, head_size)
+    kv_block = kv_block.reshape(n_core * n_hi * rows_here, 2 * kv_cols)
     piece_rows = kv_block.shape[0]
-    allowed = allowed_pairs(doc_starts, my_rows, jnp.arange(piece_rows, dtype=jnp.int32))
+    slot_core = jnp.arange(piece_rows, dtype=jnp.int32) // (n_hi * rows_here)
+    slot_hi = (jnp.arange(piece_rows, dtype=jnp.int32) // rows_here) % n_hi
+    col_ids = (slot_hi * n_core + slot_core) * rows_here + jnp.arange(piece_rows, dtype=jnp.int32) % rows_here
+    allowed = allowed_pairs(doc_starts, my_rows, col_ids)
     key_three = kv_block[:, :kv_cols].reshape(piece_rows, groups, head_size)
     value_three = kv_block[:, kv_cols:].reshape(piece_rows, groups, head_size)
     scores = (
@@ -136,9 +145,13 @@
     value_terms = jnp.einsum(
         "ghsk,sghd->kgd", prob_half, grad_four, preferred_element_type=jnp.float32
     ).reshape(piece_rows, kv_cols)
+    kv_terms = jnp.concatenate([key_terms, value_terms], axis=1).astype(jnp.bfloat16)
     kv_grad = lax.psum_scatter(
-        jnp.concatenate([key_terms, value_terms], axis=1).astype(jnp.bfloat16),
-        "seq", scatter_dimension=0, tiled=True,
+        lax.psum_scatter(
+            kv_terms.reshape(n_core, n_hi * rows_here, 2 * kv_cols), "core",
+            scatter_dimension=0, tiled=False,
+        ),
+        "seqhi", scatter_dimension=0, tiled=True,
     )
     query_grad = query_acc.reshape(rows_here, groups * per_group * head_size).astype(jnp.bfloat16)
     key_grad = kv_grad[:, :kv_cols]
@@ -147,17 +160,22 @@
 
 
 def solution(mesh):
+    n_seq, n_head = mesh.shape["seq"], mesh.shape["head"]
+    split = jax.sharding.Mesh(
+        mesh.devices.reshape(n_seq // 2, 2, n_head), ("seqhi", "core", "head")
+    )
+    rows = ("seqhi", "core")
     return jax.shard_map(
         shards,
-        mesh=mesh,
+        mesh=split,
         in_specs=(
-            P("seq", "head"),
-            P("seq", "head"),
-            P("seq", "head"),
-            P("seq", "head"),
+            P(rows, "head"),
+            P(rows, "head"),
+            P(rows, "head"),
+            P(rows, "head"),
             P("head", None),
             P(),
         ),
-        out_specs=(P("seq", "head"), P("seq", "head"), P("seq", "head")),
+        out_specs=(P(rows, "head"), P(rows, "head"), P(rows, "head")),
         check_vma=False,
     )

time: 229 us -> 285 us (1.24)
  waiting for transfers between devices: 106 us -> 162 us
  Pallas kernels: 36 us -> 27.9 us
  matrix products: 38.8 us -> 46 us
    all_gather x1 -> x2, waiting for transfers between devices: 20.2 us -> 61 us  [the longest x1 61 us: shards(): lax.all_gather(jnp.concatenate([keys, values], axis=1), 'seqhi', axis=0)]
    reduce_scatter x0 -> x1, waiting for transfers between devices: none -> 18.2 us  [shards(): lax.psum_scatter(kv_terms.reshape(n_core, n_hi * rows_here, 2 * kv_cols),...]
    another operation x1 -> x0, other arithmetic: 13.9 us -> none
    convert_element_type x0 -> x1, other arithmetic: none -> 10.7 us  [shards(): (prob_full * (grad_dots - row_delta[..., None]) * scaling).astype(jnp.bfl...]
    pallas_call x1, Pallas kernels: 36 us -> 27.9 us  [peer_blocks(): pl.pallas_call(functools.partial(_peer_kernel, n, axis, upward, per_targe...]
    dot_general x1, matrix products: 5.78 us -> 10.9 us  [shards(): jnp.einsum('ghsk,sghd->kgd', prob_half, grad_four, preferred_element_type...]
    unnamed x3 -> x5, waiting for transfers between devices: 86 us -> 82.5 us
    concatenate x1, other arithmetic: 0.27 us -> 3.27 us  [shards(): jnp.concatenate([key_terms, value_terms], axis=1).astype(jnp.bfloat16)]
  transfers between devices with their start and end apart: 2 -> 4, of which waited for: 2 -> 3; matrix products, arithmetic and copies ran while one was open for 6% -> 5% of each run, Pallas kernels for 16% -> 10%
where the time goes in v4:
time: 285 us; the launch traced here: 284 us
  waiting for transfers between devices  162 us (57%)
  matrix products  46 us (16%)
  Pallas kernels  27.9 us (10%)
  other arithmetic  24.4 us (9%)
  between operations  14 us (5%)
  local copies, waits for them, and re-layouts  10.4 us (4%)
    unnamed x5, waiting for transfers between devices  82.5 us
    all_gather x1, waiting for transfers between devices, shards(): lax.all_gather(jnp.concatenate([keys, values], axis=1), 'seqhi', axis=0)  61 us
    pallas_call x1, Pallas kernels, peer_blocks(): pl.pallas_call(functools.partial(_peer_kernel, n, axis, upward, per_targe...  27.9 us
    reduce_scatter x1, waiting for transfers between devices, shards(): lax.psum_scatter(kv_terms.reshape(n_core, n_hi * rows_here, 2 * kv_cols),...  18.2 us
    dot_general x1, matrix products, shards(): jnp.einsum('sghd,kgd->ghsk', grad_four, value_three, preferred_element_ty...  15.6 us
    dot_general x1, matrix products, shards(): jnp.einsum('ghsk,sghd->kgd', prob_half, grad_four, preferred_element_type...  10.9 us
    convert_element_type x1, other arithmetic, shards(): (prob_full * (grad_dots - row_delta[..., None]) * scaling).astype(jnp.bfl...  10.7 us
    unnamed x24, local copies, waits for them, and re-layouts  7.14 us
  transfers between devices with their start and end apart: 4, of which 3 were waited for; matrix products, arithmetic and copies ran while one was open for 5% of the time, Pallas kernels for 10%

profile of v4, /device:TPU:8, one launch (start us, length us, event | category | flops | bytes accessed | tf_op | source)
XLA Modules:
  0.0 284.5 jit_solution(7074033148052092790)
XLA Ops:
  7.2 0.0 copy-start
  7.2 0.0 all-gather.5.cloned.1.call-start
  7.2 1.5 pad_maximum_fusion.1
  8.7 0.0 all-gather.5.cloned.1.call-update
  8.8 0.0 all-gather.7.cloned.1.call-start
  8.8 61.0 %all-gather.5.cloned.1.call-done = bf16[3072,256]{1,0:T(8,128)(2,1)} async-done(((bf16[192,256]{1,0:T(8,128)(2,1)}), bf16[3072,256]{1,0:T(8,128)(2,1)}) %all-gather.5.cloned.1.call-update) | async-done | bytes 1572880 | tf_op jit(solution)/shard_map/all_gather | solution.py:101
  69.8 0.0 all-gather.7.cloned.1.call-update
  69.8 0.0 reduce-scatter.5.cloned.1.call-start
  69.9 27.9 %shard_map.85 = bf16[8,192,512]{2,1,0:T(8,128)(2,1)} custom-call(bf16[192,512]{1,0:T(8,128)(2,1)} %src_ref.1), custom_call_target="tpu_custom_call" | custom-call | tf_op jit(solution)/shard_map/pallas_call | solution.py:77
  97.8 0.7 convert_reduce_fusion.1
  98.6 0.8 convert_reduce_fusion
  99.4 4.3 %fusion.51 = bf16[24,4,8,128]{3,2,1,0:T(8,128)(2,1)S(1)} fusion(bf16[64,8,8,512]{3,2,1,0:T(8,128)(2,1)} %bitcast.160, bf16[8,192,512]{2,1,0:T(8,128)(2,1)} %shard_map.85, pred[8]{0:T(512)(128)(4,1)S(1)} %iota_compare_fusion, bf16[192,512]{1,0:T(8,128)(2,1)} %src_ref.1), kind=kOutput, calls=%fused_computation.38 | convolution fusion | flops 806191104 | bytes 6160392 | tf_op jit(solution)/shard_map/hte,che->tc/dot_general | solution.py:109
  103.7 1.0 compare_and_fusion
  104.7 0.0 copy-start.3
  104.7 0.0 all-gather.7.cloned.1.call-done
  104.7 0.0 copy-done
  104.7 5.6 %fusion.4 = (f32[4,192]{1,0:T(4,128)S(1)}, f32[6144,192,4]{0,1,2:T(8,128)S(1)}) fusion(pred[192,6144]{1,0:T(8,128)(4,1)S(1)} %compare_and_fusion, bf16[6144,256]{1,0:T(8,128)(2,1)} %bitcast.156, bf16[192,512]{1,0:T(8,128)(2,1)S(1)} %copy-done), kind=kOutput, calls=%fused_computation.9 | convolution fusion | flops 1222114560 | bytes 21826560 | tf_op jit(solution)/shard_map/sghd,kgd->ghsk/dot_general | solution.py:126
  110.4 0.0 copy-start.1
  110.4 0.0 copy-done.3
  110.4 6.3 %select_reduce_fusion = f32[4,192]{1,0:T(4,128)S(1)} fusion(f32[6144,192,4]{0,1,2:T(8,128)S(1)} %get-tuple-element.18, f32[4,192]{1,0:T(4,128)S(1)} %get-tuple-element.17, pred[192,6144]{1,0:T(8,128)(4,1)S(1)} %compare_and_fusion), kind=kLoop, calls=%fused_computation.8 | loop fusion | flops 23592192 | bytes 20060160 | tf_op jit(solution)/shard_map/reduce_sum | solution.py:132
  116.7 0.1 copy-done.1
  116.9 0.0 slice-start
  116.9 0.0 slice-start.1
  116.9 0.0 slice-start.2
  116.9 15.6 %fusion = (f32[4,192]{1,0:T(4,128)S(1)}, f32[6144,192,4]{0,1,2:T(8,128)}) fusion(f32[4,192]{1,0:T(4,128)S(1)} %log_add_fusion, f32[6144,192,4]{0,1,2:T(8,128)} %copy-done.1, pred[192,6144]{1,0:T(8,128)(4,1)} %copy-done.3, bf16[24,4,8,128]{3,2,1,0:T(8,128)(2,1)S(1)} %fusion.51, bf16[6144,256]{1,0:T(8,128)(2,1)} %bitcast.157), kind=kOutput, calls=%fused_computation.3 | convolution fusion | flops 1236270336 | bytes 40704000 | tf_op jit(solution)/shard_map/sghd,kgd->ghsk/dot_general | solution.py:135
  132.5 0.0 slice-start.3
  132.5 0.0 slice-start.4
  132.5 0.0 copy-start.4
  132.5 10.9 %fusion.19 = bf16[6144,1,128]{0,2,1:T(8,128)(2,1)} fusion(f32[4,192]{1,0:T(4,128)S(1)} %log_add_fusion, f32[6144,192,4]{0,1,2:T(8,128)} %copy-done.1, pred[192,6144]{1,0:T(8,128)(4,1)} %copy-done.3, bf16[24,4,8,128]{3,2,1,0:T(8,128)(2,1)S(1)} %fusion.51), kind=kOutput, calls=%fused_computation.20 | convolution fusion | flops 1232338944 | bytes 21826560 | tf_op jit(solution)/shard_map/ghsk,sghd->kgd/dot_general | solution.py:145
  143.4 0.0 slice-done
  143.4 0.0 slice-done.1
  143.4 0.0 slice-done.2
  143.5 0.0 slice-done.3
  143.5 0.0 slice-done.4
  143.5 0.0 copy-done.4
  143.5 10.7 %fusion.3 = bf16[1,4,192,6144]{3,2,1,0:T(8,128)(2,1)S(1)} fusion(f32[6144,192,4]{0,1,2:T(8,128)} %get-tuple-element.20, f32[4,192]{1,0:T(4,128)S(1)} %get-tuple-element.19, f32[4,192]{1,0:T(4,128)S(1)} %log_add_fusion, f32[6144,192,4]{0,1,2:T(8,128)S(1)} %bitcast.150, pred[192,6144]{1,0:T(8,128)(4,1)S(1)} %copy-done.4), kind=kLoop, calls=%fused_computation.6 | loop fusion | flops 37748736 | bytes 48371712 | tf_op jit(solution)/shard_map/convert_element_type | solution.py:139
  154.2 0.0 copy-start.2
  154.2 0.0 copy-start.5
  154.2 3.7 %copy-done.2 = bf16[1,4,192,6144]{3,2,1,0:T(8,128)(2,1)} copy-done((bf16[1,4,192,6144]{3,2,1,0:T(8,128)(2,1)}, bf16[1,4,192,6144]{3,2,1,0:T(8,128)(2,1)S(1)}, u32[]{:S(2)}) %copy-start.2) | copy-done | bytes 9437208
  157.9 2.7 fusion.28
  160.6 0.0 copy-done.5
  160.6 0.9 copy.46
  161.5 0.7 copy.47
  162.2 3.3 %pad_maximum_fusion = bf16[2,3072,256]{1,2,0:T(8,128)(2,1)} fusion(bf16[2,3072,128]{1,2,0:T(8,128)(2,1)S(1)} %copy.47, bf16[2,3072,128]{1,2,0:T(8,128)(2,1)} %fusion.28), kind=kLoop, calls=%fused_computation.27 | loop fusion | flops 6291456 | bytes 6291456 | tf_op jit(solution)/shard_map/concatenate | solution.py:148
  165.5 0.0 reduce-scatter.5.cloned.1.call-update
  165.5 0.0 reduce-scatter.7.cloned.1.call-start
  165.5 18.2 %reduce-scatter.5.cloned.1.call-done = bf16[1,3072,256]{1,2,0:T(8,128)(2,1)} async-done(((bf16[2,3072,256]{1,2,0:T(8,128)(2,1)}), bf16[1,3072,256]{1,2,0:T(8,128)(2,1)}) %reduce-scatter.5.cloned.1.call-update) | async-done | bytes 1572880 | tf_op jit(solution)/shard_map/reduce_scatter | solution.py:150
  183.7 2.6 copy.51
  186.3 0.0 reduce-scatter.7.cloned.1.call-update
  186.4 6.8 %fusion.48 = bf16[192,1,4,128]{3,0,2,1:T(8,128)(2,1)S(1)} fusion(bf16[1,4,192,6144]{3,2,1,0:T(8,128)(2,1)} %copy-done.2, bf16[6144,256]{1,0:T(8,128)(2,1)} %bitcast.158), kind=kOutput, calls=%fused_computation.37 | convolution fusion | flops 1208057856 | bytes 11206656 | tf_op jit(solution)/shard_map/ghsk,kgd->sghd/dot_general | solution.py:141
  193.1 0.2 copy.42
  193.3 0.7 copy.99
  194.0 82.5 %reduce-scatter.7.cloned.1.call-done = bf16[192,256]{1,0:T(8,128)(2,1)} async-done(((bf16[3072,256]{1,0:T(8,128)(2,1)}), bf16[192,256]{1,0:T(8,128)(2,1)}) %reduce-scatter.7.cloned.1.call-update) | async-done | bytes 98320
  276.5 1.5 fusion.81
  (5 shorter events, 0.1 us)
Async XLA Ops:
  7.2 97.6 %copy-start = (bf16[192,512]{1,0:T(8,128)(2,1)S(1)}, bf16[192,512]{1,0:T(8,128)(2,1)}, u32[]{:S(2)}) copy-start(bf16[192,512]{1,0:T(8,128)(2,1)} %param.6) | copy-start | bytes 589828
  7.2 62.6 %all-gather.5.cloned.1.call-start = ((), (), s32[]{:S(2)}) async-start(), calls=%async_computation.3 | async-start | bytes 1671168 | tf_op jit(solution)/shard_map/all_gather | solution.py:101
  8.8 96.0 %all-gather.7.cloned.1.call-start = ((), (), s32[]{:S(2)}) async-start(), calls=%async_computation.4 | async-start | bytes 4718592 | tf_op jit(solution)/shard_map/all_gather | solution.py:100
  69.8 113.9 %reduce-scatter.5.cloned.1.call-start = ((), (), s32[]{:S(2)}) async-start(), calls=%async_computation.2 | async-start | bytes 4718592 | tf_op jit(solution)/shard_map/reduce_scatter | solution.py:150
  104.7 5.7 %copy-start.3 = (pred[192,6144]{1,0:T(8,128)(4,1)}, pred[192,6144]{1,0:T(8,128)(4,1)S(1)}, u32[]{:S(2)}) copy-start(pred[192,6144]{1,0:T(8,128)(4,1)S(1)} %compare_and_fusion) | copy-start | bytes 3538948
  110.4 6.5 %copy-start.1 = (f32[6144,192,4]{0,1,2:T(8,128)}, f32[6144,192,4]{0,1,2:T(8,128)S(1)}, u32[]{:S(2)}) copy-start(f32[6144,192,4]{0,1,2:T(8,128)S(1)} %get-tuple-element.18) | copy-start | bytes 56623108
  116.9 26.6 %slice-start = ((s8[18874368]{0:T(1024)(128)(4,1)}), s8[4194304]{0:T(1024)(128)(4,1)S(1)}, s32[]{:S(2)}) async-start(s8[18874368]{0:T(1024)(128)(4,1)} %bitcast.149), calls=%async_computation.6 | async-start | bytes 8388608
  116.9 26.6 %slice-start.1 = ((s8[18874368]{0:T(1024)(128)(4,1)}), s8[4194304]{0:T(1024)(128)(4,1)S(1)}, s32[]{:S(2)}) async-start(s8[18874368]{0:T(1024)(128)(4,1)} %bitcast.149), calls=%async_computation.7 | async-start | bytes 8388608
  116.9 26.6 %slice-start.2 = ((s8[18874368]{0:T(1024)(128)(4,1)}), s8[2097152]{0:T(1024)(128)(4,1)S(1)}, s32[]{:S(2)}) async-start(s8[18874368]{0:T(1024)(128)(4,1)} %bitcast.149), calls=%async_computation.8 | async-start | bytes 4194304
  132.5 10.9 %slice-start.3 = ((s8[18874368]{0:T(1024)(128)(4,1)}), s8[4194304]{0:T(1024)(128)(4,1)S(1)}, s32[]{:S(2)}) async-start(s8[18874368]{0:T(1024)(128)(4,1)} %bitcast.149), calls=%async_computation.9 | async-start | bytes 8388608
  132.5 10.9 %slice-start.4 = ((s8[18874368]{0:T(1024)(128)(4,1)}), s8[4194304]{0:T(1024)(128)(4,1)S(1)}, s32[]{:S(2)}) async-start(s8[18874368]{0:T(1024)(128)(4,1)} %bitcast.149), calls=%async_computation.10 | async-start | bytes 8388608
  132.5 10.9 %copy-start.4 = (pred[192,6144]{1,0:T(8,128)(4,1)S(1)}, pred[192,6144]{1,0:T(8,128)(4,1)}, u32[]{:S(2)}) copy-start(pred[192,6144]{1,0:T(8,128)(4,1)} %copy-done.3) | copy-start | bytes 3538948
  154.2 3.7 %copy-start.2 = (bf16[1,4,192,6144]{3,2,1,0:T(8,128)(2,1)}, bf16[1,4,192,6144]{3,2,1,0:T(8,128)(2,1)S(1)}, u32[]{:S(2)}) copy-start(bf16[1,4,192,6144]{3,2,1,0:T(8,128)(2,1)S(1)} %fusion.3) | copy-start | bytes 28311556
  154.2 6.4 %copy-start.5 = (bf16[6144,1,128]{0,2,1:T(8,128)(2,1)S(1)}, bf16[6144,1,128]{0,2,1:T(8,128)(2,1)}, u32[]{:S(2)}) copy-start(bf16[6144,1,128]{0,2,1:T(8,128)(2,1)} %fusion.19) | copy-start | bytes 4718596
  165.5 111.0 %reduce-scatter.7.cloned.1.call-start = ((), (), s32[]{:S(2)}) async-start(), calls=%async_computation.5 | async-start | bytes 1671168
Sparse Core Ops, SparseCore 0:
  11.0 58.7 all-gather.4
  71.6 15.2 all-gather.6
  165.6 18.0 reduce-scatter.4
  187.5 88.8 reduce-scatter.6

commit v5 on v4

--- a/solution.py
+++ b/solution.py
@@ -91,14 +91,18 @@
     per_group = queries.shape[1] // keys.shape[1]
     kv_cols = keys.shape[1]
     scaling = 1.0 / math.sqrt(head_size)
-    n_hi = lax.axis_size("seqhi")
+    n_zh = lax.axis_size("zhi")
+    n_x = lax.axis_size("xx")
     n_core = lax.axis_size("core")
-    my_core = lax.axis_index("core")
-    me = lax.axis_index("seqhi") * n_core + my_core
+    n_hi = n_zh * n_x
+    me = (lax.axis_index("zhi") * n_x + lax.axis_index("xx")) * n_core + lax.axis_index("core")
     first_row = me * rows_here
     my_rows = first_row + jnp.arange(rows_here, dtype=jnp.int32)
     kv_block = lax.all_gather(
-        lax.all_gather(jnp.concatenate([keys, values], axis=1), "seqhi", axis=0),
+        lax.all_gather(
+            lax.all_gather(jnp.concatenate([keys, values], axis=1), "zhi", axis=0),
+            "xx", axis=0,
+        ),
         "core", axis=0,
     )
     n_head = lax.axis_size("head")
@@ -117,7 +121,9 @@
     kv_block = kv_block.reshape(n_core * n_hi * rows_here, 2 * kv_cols)
     piece_rows = kv_block.shape[0]
     slot_core = jnp.arange(piece_rows, dtype=jnp.int32) // (n_hi * rows_here)
-    slot_hi = (jnp.arange(piece_rows, dtype=jnp.int32) // rows_here) % n_hi
+    slot_x = (jnp.arange(piece_rows, dtype=jnp.int32) // (n_zh * rows_here)) % n_x
+    slot_zh = (jnp.arange(piece_rows, dtype=jnp.int32) // rows_here) % n_zh
+    slot_hi = slot_zh * n_x + slot_x
     col_ids = (slot_hi * n_core + slot_core) * rows_here + jnp.arange(piece_rows, dtype=jnp.int32) % rows_here
     allowed = allowed_pairs(doc_starts, my_rows, col_ids)
     key_three = kv_block[:, :kv_cols].reshape(piece_rows, groups, head_size)
@@ -148,10 +154,13 @@
     kv_terms = jnp.concatenate([key_terms, value_terms], axis=1).astype(jnp.bfloat16)
     kv_grad = lax.psum_scatter(
         lax.psum_scatter(
-            kv_terms.reshape(n_core, n_hi * rows_here, 2 * kv_cols), "core",
-            scatter_dimension=0, tiled=False,
+            lax.psum_scatter(
+                kv_terms.reshape(n_core, n_x, n_zh * rows_here, 2 * kv_cols), "core",
+                scatter_dimension=0, tiled=False,
+            ),
+            "xx", scatter_dimension=0, tiled=False,
         ),
-        "seqhi", scatter_dimension=0, tiled=True,
+        "zhi", scatter_dimension=0, tiled=True,
     )
     query_grad = query_acc.reshape(rows_here, groups * per_group * head_size).astype(jnp.bfloat16)
     key_grad = kv_grad[:, :kv_cols]
@@ -162,9 +171,9 @@
 def solution(mesh):
     n_seq, n_head = mesh.shape["seq"], mesh.shape["head"]
     split = jax.sharding.Mesh(
-        mesh.devices.reshape(n_seq // 2, 2, n_head), ("seqhi", "core", "head")
+        mesh.devices.reshape(n_seq // 8, 4, 2, n_head), ("zhi", "xx", "core", "head")
     )
-    rows = ("seqhi", "core")
+    rows = ("zhi", "xx", "core")
     return jax.shard_map(
         shards,
         mesh=split,

time: 285 us -> 260 us (0.912)
  waiting for transfers between devices: 162 us -> 97.8 us
  blocking collectives: 0 us -> 19.3 us
  local copies, waits for them, and re-layouts: 10.4 us -> 22.4 us
    unnamed x5 -> x6, waiting for transfers between devices: 82.5 us -> 19.6 us
    all_gather x2, waiting for transfers between devices: 61 us -> 28 us  [the longest x1 28 us: shards(): lax.all_gather(lax.all_gather(jnp.concatenate([keys, values], axis=1), 'z...]
    reduce_scatter x1 -> x2, waiting for transfers between devices: 18.2 us -> 50.3 us  [the longest x1 32.1 us: shards(): lax.psum_scatter(lax.psum_scatter(kv_terms.reshape(n_core, n_x, n_zh * ro...]
    all_gather x0 -> x1, blocking collectives: none -> 19.3 us  [shards(): lax.all_gather(jnp.concatenate([keys, values], axis=1), 'zhi', axis=0)]
    dot_general x0 -> x1, local copies, waits for them, and re-layouts: none -> 15.4 us  [shards(): jnp.einsum('ghsk,sghd->kgd', dscores, query_four, preferred_element_type=...]
    unnamed x24 -> x22, local copies, waits for them, and re-layouts: 7.14 us -> 2.78 us
    convert_element_type x1, other arithmetic: 10.7 us -> 14.4 us  [shards(): (prob_full * (grad_dots - row_delta[..., None]) * scaling).astype(jnp.bfl...]
  transfers between devices with their start and end apart: 4 -> 5, of which waited for: 3 -> 4; matrix products, arithmetic and copies ran while one was open for 5% -> 6% of each run, Pallas kernels for 10% -> 12%
where the time goes in v5:
time: 260 us; the launch traced here: 259 us
  waiting for transfers between devices  97.8 us (38%)
  matrix products  48.8 us (19%)
  Pallas kernels  30.2 us (12%)
  other arithmetic  26.2 us (10%)
  local copies, waits for them, and re-layouts  22.4 us (9%)
  blocking collectives  19.3 us (7%)
  between operations  14 us (5%)
    reduce_scatter x1, waiting for transfers between devices, shards(): lax.psum_scatter(lax.psum_scatter(kv_terms.reshape(n_core, n_x, n_zh * ro...  32.1 us
    pallas_call x1, Pallas kernels, peer_blocks(): pl.pallas_call(functools.partial(_peer_kernel, n, axis, upward, per_targe...  30.2 us
    all_gather x1, waiting for transfers between devices, shards(): lax.all_gather(lax.all_gather(jnp.concatenate([keys, values], axis=1), 'z...  28 us
    unnamed x6, waiting for transfers between devices  19.6 us
    all_gather x1, blocking collectives, shards(): lax.all_gather(jnp.concatenate([keys, values], axis=1), 'zhi', axis=0)  19.3 us
    reduce_scatter x1, waiting for transfers between devices, shards(): lax.psum_scatter(kv_terms.reshape(n_core, n_x, n_zh * rows_here, 2 * kv_c...  18.2 us
    dot_general x1, matrix products, shards(): jnp.einsum('sghd,kgd->ghsk', grad_four, value_three, preferred_element_ty...  15.6 us
    dot_general x1, local copies, waits for them, and re-layouts, shards(): jnp.einsum('ghsk,sghd->kgd', dscores, query_four, preferred_element_type=...  15.4 us
  transfers between devices with their start and end apart: 5, of which 4 were waited for; matrix products, arithmetic and copies ran while one was open for 6% of the time, Pallas kernels for 12%

profile of v5, /device:TPU:8, one launch (start us, length us, event | category | flops | bytes accessed | tf_op | source)
XLA Modules:
  0.0 258.9 jit_solution(1929046131264300926)
XLA Ops:
  7.2 0.0 copy-start.4
  7.2 0.0 all-gather.6.cloned.1.call-start
  7.2 0.9 pad_maximum_fusion.1
  8.1 19.3 %all-gather = bf16[768,256]{1,0:T(8,128)(2,1)} all-gather(bf16[192,256]{1,0:T(8,128)(2,1)S(1)} %pad_maximum_fusion.1), channel_id=2, replica_groups=mesh['zhi'=4,'xx'=4,'core'=2,'head'=8] {'zhi'}, dimensions={0}, use_global_device_ids=true | all-gather | bytes 491520 | tf_op jit(solution)/shard_map/all_gather | solution.py:103
  27.4 0.0 all-gather.6.cloned.1.call-update
  27.5 0.0 all-gather.8.cloned.1.call-start
  27.5 28.0 %all-gather.6.cloned.1.call-done = bf16[16,192,256]{2,1,0:T(8,128)(2,1)} async-done(((bf16[4,192,256]{2,1,0:T(8,128)(2,1)}), bf16[16,192,256]{2,1,0:T(8,128)(2,1)}) %all-gather.6.cloned.1.call-update) | async-done | bytes 1572880 | tf_op jit(solution)/shard_map/all_gather | solution.py:102
  55.5 0.0 all-gather.8.cloned.1.call-update
  55.5 0.0 reduce-scatter.6.cloned.1.call-start
  55.6 30.2 %shard_map.85 = bf16[8,192,512]{2,1,0:T(8,128)(2,1)} custom-call(bf16[192,512]{1,0:T(8,128)(2,1)} %src_ref.1), custom_call_target="tpu_custom_call" | custom-call | tf_op jit(solution)/shard_map/pallas_call | solution.py:77
  85.7 1.0 reshape.286
  86.8 0.7 convert_reduce_fusion.1
  87.5 0.8 convert_reduce_fusion
  88.3 4.3 %fusion.46 = bf16[24,4,8,128]{3,2,1,0:T(8,128)(2,1)S(1)} fusion(bf16[64,8,8,512]{3,2,1,0:T(8,128)(2,1)} %bitcast.150, bf16[8,192,512]{2,1,0:T(8,128)(2,1)} %shard_map.85, pred[8]{0:T(512)(128)(4,1)S(1)} %iota_compare_fusion, bf16[192,512]{1,0:T(8,128)(2,1)} %src_ref.1), kind=kOutput, calls=%fused_computation.36 | convolution fusion | flops 806191104 | bytes 6160392 | tf_op jit(solution)/shard_map/hte,che->tc/dot_general | solution.py:113
  92.7 1.0 compare_and_fusion
  93.7 0.0 copy-start.1
  93.7 0.0 all-gather.8.cloned.1.call-done
  93.7 0.0 copy-done.4
  93.7 5.6 %fusion.4 = (f32[4,192]{1,0:T(4,128)S(1)}, f32[6144,192,4]{0,1,2:T(8,128)S(1)}) fusion(pred[192,6144]{1,0:T(8,128)(4,1)S(1)} %compare_and_fusion, bf16[6144,256]{1,0:T(8,128)(2,1)} %bitcast.144, bf16[192,512]{1,0:T(8,128)(2,1)S(1)} %copy-done.4), kind=kOutput, calls=%fused_computation.9 | convolution fusion | flops 1222114560 | bytes 21826560 | tf_op jit(solution)/shard_map/sghd,kgd->ghsk/dot_general | solution.py:132
  99.4 0.0 copy-start
  99.4 0.0 copy-done.1
  99.4 6.3 %select_reduce_fusion = f32[4,192]{1,0:T(4,128)S(1)} fusion(f32[6144,192,4]{0,1,2:T(8,128)S(1)} %get-tuple-element.18, f32[4,192]{1,0:T(4,128)S(1)} %get-tuple-element.17, pred[192,6144]{1,0:T(8,128)(4,1)S(1)} %compare_and_fusion), kind=kLoop, calls=%fused_computation.8 | loop fusion | flops 23592192 | bytes 20060160 | tf_op jit(solution)/shard_map/reduce_sum | solution.py:138
  105.7 0.1 copy-done
  105.8 0.0 slice-start
  105.9 0.0 slice-start.1
  105.9 0.0 slice-start.2
  105.9 15.6 %fusion = (f32[4,192]{1,0:T(4,128)S(1)}, f32[6144,192,4]{0,1,2:T(8,128)}) fusion(f32[4,192]{1,0:T(4,128)S(1)} %log_add_fusion, f32[6144,192,4]{0,1,2:T(8,128)} %copy-done, pred[192,6144]{1,0:T(8,128)(4,1)} %copy-done.1, bf16[24,4,8,128]{3,2,1,0:T(8,128)(2,1)S(1)} %fusion.46, bf16[6144,256]{1,0:T(8,128)(2,1)} %bitcast.145), kind=kOutput, calls=%fused_computation.3 | convolution fusion | flops 1236270336 | bytes 40704000 | tf_op jit(solution)/shard_map/sghd,kgd->ghsk/dot_general | solution.py:141
  121.5 0.0 slice-start.3
  121.5 0.0 slice-start.4
  121.5 0.0 copy-start.2
  121.5 10.9 %fusion.18 = bf16[6144,1,128]{0,2,1:T(8,128)(2,1)} fusion(f32[4,192]{1,0:T(4,128)S(1)} %log_add_fusion, f32[6144,192,4]{0,1,2:T(8,128)} %copy-done, pred[192,6144]{1,0:T(8,128)(4,1)} %copy-done.1, bf16[24,4,8,128]{3,2,1,0:T(8,128)(2,1)S(1)} %fusion.46), kind=kOutput, calls=%fused_computation.19 | convolution fusion | flops 1232338944 | bytes 21826560 | tf_op jit(solution)/shard_map/ghsk,sghd->kgd/dot_general | solution.py:151
  132.4 0.0 slice-done
  132.4 0.0 slice-done.1
  132.4 0.0 slice-done.2
  132.4 0.0 slice-done.3
  132.4 0.0 slice-done.4
  132.5 0.0 copy-done.2
  132.5 14.4 %fusion.3 = bf16[1,4,192,6144]{3,2,1,0:T(8,128)(2,1)} fusion(f32[6144,192,4]{0,1,2:T(8,128)} %get-tuple-element.20, f32[4,192]{1,0:T(4,128)S(1)} %get-tuple-element.19, f32[4,192]{1,0:T(4,128)S(1)} %log_add_fusion, f32[6144,192,4]{0,1,2:T(8,128)S(1)} %bitcast.138, pred[192,6144]{1,0:T(8,128)(4,1)S(1)} %copy-done.2), kind=kLoop, calls=%fused_computation.6 | loop fusion | flops 37748736 | bytes 48371712 | tf_op jit(solution)/shard_map/convert_element_type | solution.py:145
  146.9 0.0 copy-start.3
  146.9 15.4 %dot_general.32 = bf16[2,4,768,4,192]{2,1,0,4,3:T(4,128)(2,1)} reshape(bf16[6144,4,192]{0,2,1:T(8,128)(2,1)} %bitcast.136) | data formatting | bytes 18874368 | tf_op jit(solution)/shard_map/ghsk,sghd->kgd/dot_general | solution.py:148
  162.3 0.0 copy-done.3
  162.3 0.9 copy.46
  163.2 0.7 copy.47
  164.0 5.5 %bitcast_convert_fusion = bf16[2,4,768,128]{2,3,1,0:T(8,128)(2,1)S(1)} fusion(bf16[2,4,768,4,192]{2,1,0,4,3:T(4,128)(2,1)} %dot_general.32, bf16[192,4,128,1,1]{2,1,0,4,3:T(4,128)(2,1)S(1)} %bitcast.148), kind=kOutput, calls=%fused_computation.25 | convolution fusion | flops 1208745984 | bytes 11206656 | tf_op jit(solution)/shard_map/ghsk,sghd->kgd/dot_general | solution.py:148
  169.5 1.9 pad_maximum_fusion
  171.4 0.0 reduce-scatter.6.cloned.1.call-update
  171.5 0.0 reduce-scatter.8.cloned.1.call-start
  171.5 18.2 %reduce-scatter.6.cloned.1.call-done = bf16[1,4,768,256]{2,3,1,0:T(8,128)(2,1)} async-done(((bf16[2,4,768,256]{2,3,1,0:T(8,128)(2,1)}), bf16[1,4,768,256]{2,3,1,0:T(8,128)(2,1)}) %reduce-scatter.6.cloned.1.call-update) | async-done | bytes 1572880 | tf_op jit(solution)/shard_map/reduce_scatter | solution.py:157
  189.7 0.0 reduce-scatter.8.cloned.1.call-update
  189.7 0.0 reduce-scatter.10.cloned.1.call-start
  189.8 32.1 %reduce-scatter.8.cloned.1.call-done = bf16[1,768,256]{1,2,0:T(8,128)(2,1)} async-done(((bf16[4,768,256]{1,2,0:T(8,128)(2,1)}), bf16[1,768,256]{1,2,0:T(8,128)(2,1)}) %reduce-scatter.8.cloned.1.call-update) | async-done | bytes 393232 | tf_op jit(solution)/shard_map/reduce_scatter | solution.py:156
  221.9 1.9 copy.54
  223.8 0.0 reduce-scatter.10.cloned.1.call-update
  223.8 6.8 %fusion.43 = bf16[192,1,4,128]{3,0,2,1:T(8,128)(2,1)S(1)} fusion(bf16[1,4,192,6144]{3,2,1,0:T(8,128)(2,1)} %fusion.3, bf16[6144,256]{1,0:T(8,128)(2,1)} %bitcast.146), kind=kOutput, calls=%fused_computation.35 | convolution fusion | flops 1208057856 | bytes 11206656 | tf_op jit(solution)/shard_map/ghsk,kgd->sghd/dot_general | solution.py:147
  230.6 0.2 copy.42
  230.8 0.7 copy.95
  231.5 19.5 %reduce-scatter.10.cloned.1.call-done = bf16[192,256]{1,0:T(8,128)(2,1)} async-done(((bf16[768,256]{1,0:T(8,128)(2,1)}), bf16[192,256]{1,0:T(8,128)(2,1)}) %reduce-scatter.10.cloned.1.call-update) | async-done | bytes 98320
  250.9 1.5 fusion.81
  (5 shorter events, 0.1 us)
Async XLA Ops:
  7.2 86.5 %copy-start.4 = (bf16[192,512]{1,0:T(8,128)(2,1)S(1)}, bf16[192,512]{1,0:T(8,128)(2,1)}, u32[]{:S(2)}) copy-start(bf16[192,512]{1,0:T(8,128)(2,1)} %param.6) | copy-start | bytes 589828
  7.2 48.3 %all-gather.6.cloned.1.call-start = ((), (), s32[]{:S(2)}) async-start(), calls=%async_computation.5 | async-start | bytes 1966080 | tf_op jit(solution)/shard_map/all_gather | solution.py:102
  27.5 66.2 %all-gather.8.cloned.1.call-start = ((), (), s32[]{:S(2)}) async-start(), calls=%async_computation.6 | async-start | bytes 4718592 | tf_op jit(solution)/shard_map/all_gather | solution.py:101
  55.5 134.2 %reduce-scatter.6.cloned.1.call-start = ((), (), s32[]{:S(2)}) async-start(), calls=%async_computation.3 | async-start | bytes 4718592 | tf_op jit(solution)/shard_map/reduce_scatter | solution.py:157
  93.7 5.7 %copy-start.1 = (pred[192,6144]{1,0:T(8,128)(4,1)}, pred[192,6144]{1,0:T(8,128)(4,1)S(1)}, u32[]{:S(2)}) copy-start(pred[192,6144]{1,0:T(8,128)(4,1)S(1)} %compare_and_fusion) | copy-start | bytes 3538948
  99.4 6.5 %copy-start = (f32[6144,192,4]{0,1,2:T(8,128)}, f32[6144,192,4]{0,1,2:T(8,128)S(1)}, u32[]{:S(2)}) copy-start(f32[6144,192,4]{0,1,2:T(8,128)S(1)} %get-tuple-element.18) | copy-start | bytes 56623108
  105.8 26.6 %slice-start = ((s8[18874368]{0:T(1024)(128)(4,1)}), s8[4194304]{0:T(1024)(128)(4,1)S(1)}, s32[]{:S(2)}) async-start(s8[18874368]{0:T(1024)(128)(4,1)} %bitcast.137), calls=%async_computation.8 | async-start | bytes 8388608
  105.9 26.6 %slice-start.1 = ((s8[18874368]{0:T(1024)(128)(4,1)}), s8[4194304]{0:T(1024)(128)(4,1)S(1)}, s32[]{:S(2)}) async-start(s8[18874368]{0:T(1024)(128)(4,1)} %bitcast.137), calls=%async_computation.9 | async-start | bytes 8388608
  105.9 26.6 %slice-start.2 = ((s8[18874368]{0:T(1024)(128)(4,1)}), s8[2097152]{0:T(1024)(128)(4,1)S(1)}, s32[]{:S(2)}) async-start(s8[18874368]{0:T(1024)(128)(4,1)} %bitcast.137), calls=%async_computation.10 | async-start | bytes 4194304
  121.5 10.9 %slice-start.3 = ((s8[18874368]{0:T(1024)(128)(4,1)}), s8[4194304]{0:T(1024)(128)(4,1)S(1)}, s32[]{:S(2)}) async-start(s8[18874368]{0:T(1024)(128)(4,1)} %bitcast.137), calls=%async_computation.11 | async-start | bytes 8388608
  121.5 10.9 %slice-start.4 = ((s8[18874368]{0:T(1024)(128)(4,1)}), s8[4194304]{0:T(1024)(128)(4,1)S(1)}, s32[]{:S(2)}) async-start(s8[18874368]{0:T(1024)(128)(4,1)} %bitcast.137), calls=%async_computation.12 | async-start | bytes 8388608
  121.5 10.9 %copy-start.2 = (pred[192,6144]{1,0:T(8,128)(4,1)S(1)}, pred[192,6144]{1,0:T(8,128)(4,1)}, u32[]{:S(2)}) copy-start(pred[192,6144]{1,0:T(8,128)(4,1)} %copy-done.1) | copy-start | bytes 3538948
  146.9 15.4 %copy-start.3 = (bf16[6144,1,128]{0,2,1:T(8,128)(2,1)S(1)}, bf16[6144,1,128]{0,2,1:T(8,128)(2,1)}, u32[]{:S(2)}) copy-start(bf16[6144,1,128]{0,2,1:T(8,128)(2,1)} %fusion.18) | copy-start | bytes 4718596
  171.5 50.4 %reduce-scatter.8.cloned.1.call-start = ((), (), s32[]{:S(2)}) async-start(), calls=%async_computation.4 | async-start | bytes 1966080 | tf_op jit(solution)/shard_map/reduce_scatter | solution.py:156
  189.7 61.2 %reduce-scatter.10.cloned.1.call-start = ((), (), s32[]{:S(2)}) async-start(), calls=%async_computation.7 | async-start | bytes 491520
Sparse Core Ops, SparseCore 0:
  27.6 27.8 all-gather.5
  57.3 17.5 all-gather.7
  171.6 18.0 reduce-scatter.5
  192.3 29.5 reduce-scatter.7
  224.4 26.5 reduce-scatter.9

commit v6 on v3

--- a/solution.py
+++ b/solution.py
@@ -82,6 +82,143 @@
         scratch_shapes=[pltpu.SemaphoreType.DMA((n - 1,)), pltpu.SemaphoreType.DMA((n - 1,))],
         compiler_params=pltpu.CompilerParams(has_side_effects=True),
     )(src)
+
+
+KEY_TILE = 512
+
+
+def _tile_mask(j, tk, rowpos_ref, rowdoc_ref, coldoc_ref):
+    col = j * tk + lax.broadcasted_iota(jnp.int32, (1, tk), 1)
+    return (col <= rowpos_ref[...]) & (coldoc_ref[...] == rowdoc_ref[...])
+
+
+def _stats_kernel(scaling, tk, dh, bounds_ref, q_ref, g_ref, kv_ref, rowpos_ref, rowdoc_ref,
+                  coldoc_ref, lt_ref, delta_ref, m_sc, l_sc, a_sc):
+    j = pl.program_id(0)
+
+    @pl.when(j == 0)
+    def _():
+        m_sc[...] = jnp.full(m_sc.shape, NEG_FILL, jnp.float32)
+        l_sc[...] = jnp.zeros(l_sc.shape, jnp.float32)
+        a_sc[...] = jnp.zeros(a_sc.shape, jnp.float32)
+
+    @pl.when((j >= bounds_ref[0]) & (j <= bounds_ref[1]))
+    def _():
+        dims = (((1,), (1,)), ((), ()))
+        scores = lax.dot_general(q_ref[...], kv_ref[:, :dh], dims,
+                                 preferred_element_type=jnp.float32) * scaling
+        allowed = _tile_mask(j, tk, rowpos_ref, rowdoc_ref, coldoc_ref)
+        scores = jnp.where(allowed, scores, NEG_FILL)
+        m_old = m_sc[...]
+        m_new = jnp.maximum(m_old, jnp.max(scores, axis=1, keepdims=True))
+        e = jnp.where(allowed, jnp.exp(scores - m_new), 0.0)
+        gd = lax.dot_general(g_ref[...], kv_ref[:, dh:], dims,
+                             preferred_element_type=jnp.float32)
+        alpha = jnp.exp(m_old - m_new)
+        l_sc[...] = alpha * l_sc[...] + jnp.sum(e, axis=1, keepdims=True)
+        a_sc[...] = alpha * a_sc[...] + jnp.sum(e * gd, axis=1, keepdims=True)
+        m_sc[...] = m_new
+
+    @pl.when(j == pl.num_programs(0) - 1)
+    def _():
+        lt_ref[...] = m_sc[...] + jnp.log(l_sc[...])
+        delta_ref[...] = a_sc[...] / l_sc[...]
+
+
+def _grad_kernel(scaling, tk, dh, bounds_ref, q_ref, g_ref, kv_ref, rowpos_ref, rowdoc_ref,
+                 coldoc_ref, lt_ref, delta_ref, dq_ref, dkv_ref, dq_sc):
+    j = pl.program_id(0)
+    active = (j >= bounds_ref[0]) & (j <= bounds_ref[1])
+
+    @pl.when(j == 0)
+    def _():
+        dq_sc[...] = jnp.zeros(dq_sc.shape, jnp.float32)
+
+    @pl.when(active)
+    def _():
+        dims = (((1,), (1,)), ((), ()))
+        tdims = (((0,), (0,)), ((), ()))
+        k_t = kv_ref[:, :dh]
+        scores = lax.dot_general(q_ref[...], k_t, dims,
+                                 preferred_element_type=jnp.float32) * scaling
+        allowed = _tile_mask(j, tk, rowpos_ref, rowdoc_ref, coldoc_ref)
+        probs = jnp.where(allowed, jnp.exp(scores - lt_ref[...]), 0.0)
+        gd = lax.dot_general(g_ref[...], kv_ref[:, dh:], dims,
+                             preferred_element_type=jnp.float32)
+        ds = (probs * (gd - delta_ref[...]) * scaling).astype(jnp.bfloat16)
+        dq_sc[...] += jnp.dot(ds, k_t, preferred_element_type=jnp.float32)
+        dk = lax.dot_general(ds, q_ref[...], tdims, preferred_element_type=jnp.float32)
+        dv = lax.dot_general(probs.astype(jnp.bfloat16), g_ref[...], tdims,
+                             preferred_element_type=jnp.float32)
+        dkv_ref[:, :dh] = dk.astype(dkv_ref.dtype)
+        dkv_ref[:, dh:] = dv.astype(dkv_ref.dtype)
+
+    @pl.when(jnp.logical_not(active))
+    def _():
+        dkv_ref[...] = jnp.zeros(dkv_ref.shape, dkv_ref.dtype)
+
+    @pl.when(j == pl.num_programs(0) - 1)
+    def _():
+        dq_ref[...] = dq_sc[...].astype(dq_ref.dtype)
+
+
+def attention_grads(q_rows, g_rows, kv_full, doc_starts, first_row, rows_here, scaling):
+    n_rows, dh = q_rows.shape
+    n_keys = kv_full.shape[0]
+    tk = KEY_TILE
+    n_tiles = n_keys // tk
+    row_pos = first_row + jnp.arange(n_rows, dtype=jnp.int32) % rows_here
+    row_doc = doc_index(doc_starts, row_pos)
+    col_doc = doc_index(doc_starts, jnp.arange(n_keys, dtype=jnp.int32))[None, :]
+    doc_first = jnp.max(jnp.where(doc_starts <= first_row, doc_starts, 0))
+    bounds = jnp.stack([doc_first // tk, (first_row + rows_here - 1) // tk]).astype(jnp.int32)
+    row_pos = row_pos[:, None]
+    row_doc = row_doc[:, None]
+
+    def tile_of(j, b):
+        return jnp.minimum(jnp.maximum(j, b[0]), b[1])
+
+    full = lambda shape: pl.BlockSpec(shape, lambda j, b: (0, 0))
+    in_specs = [
+        full((n_rows, dh)),
+        full((n_rows, dh)),
+        pl.BlockSpec((tk, 2 * dh), lambda j, b: (tile_of(j, b), 0)),
+        full((n_rows, 1)),
+        full((n_rows, 1)),
+        pl.BlockSpec((1, tk), lambda j, b: (0, tile_of(j, b))),
+    ]
+    params = pltpu.CompilerParams(dimension_semantics=("arbitrary",))
+    mm = 2 * n_rows * n_keys * dh
+    log_total, delta = pl.pallas_call(
+        functools.partial(_stats_kernel, scaling, tk, dh),
+        grid_spec=pltpu.PrefetchScalarGridSpec(
+            num_scalar_prefetch=1,
+            grid=(n_tiles,),
+            in_specs=in_specs,
+            out_specs=[full((n_rows, 1)), full((n_rows, 1))],
+            scratch_shapes=[pltpu.VMEM((n_rows, 1), jnp.float32)] * 3,
+        ),
+        out_shape=[jax.ShapeDtypeStruct((n_rows, 1), jnp.float32)] * 2,
+        compiler_params=params,
+        cost_estimate=pl.CostEstimate(flops=2 * mm, transcendentals=n_rows * n_keys,
+                                      bytes_accessed=n_keys * 4 * dh),
+    )(bounds, q_rows, g_rows, kv_full, row_pos, row_doc, col_doc)
+    dq, dkv = pl.pallas_call(
+        functools.partial(_grad_kernel, scaling, tk, dh),
+        grid_spec=pltpu.PrefetchScalarGridSpec(
+            num_scalar_prefetch=1,
+            grid=(n_tiles,),
+            in_specs=in_specs + [full((n_rows, 1)), full((n_rows, 1))],
+            out_specs=[full((n_rows, dh)), pl.BlockSpec((tk, 2 * dh), lambda j, b: (j, 0))],
+            scratch_shapes=[pltpu.VMEM((n_rows, dh), jnp.float32)],
+        ),
+        out_shape=[jax.ShapeDtypeStruct((n_rows, dh), jnp.bfloat16),
+                   jax.ShapeDtypeStruct((n_keys, 2 * dh), jnp.bfloat16)],
+        compiler_params=params,
+        cost_estimate=pl.CostEstimate(flops=5 * mm, transcendentals=n_rows * n_keys,
+                                      bytes_accessed=n_keys * 8 * dh),
+    )(bounds, q_rows, g_rows, kv_full, row_pos, row_doc, col_doc, log_total, delta)
+    return dq, dkv
 
 
 def shards(queries, keys, values, d_out, w_out, doc_starts):
@@ -107,40 +244,16 @@
         w_out.reshape(w_out.shape[0], n_head, d_out.shape[1]),
         preferred_element_type=jnp.float32,
     ).astype(jnp.bfloat16)
-    query_four = queries.reshape(rows_here, groups, per_group, head_size)
-    grad_four = attn_grad.reshape(rows_here, groups, per_group, head_size)
-    piece_rows = kv_block.shape[0]
-    allowed = allowed_pairs(doc_starts, my_rows, jnp.arange(piece_rows, dtype=jnp.int32))
-    key_three = kv_block[:, :kv_cols].reshape(piece_rows, groups, head_size)
-    value_three = kv_block[:, kv_cols:].reshape(piece_rows, groups, head_size)
-    scores = (
-        jnp.einsum("sghd,kgd->ghsk", query_four, key_three, preferred_element_type=jnp.float32)
-        * scaling
-    )
-    scores = jnp.where(allowed, scores, NEG_FILL)
-    high = jnp.max(scores, axis=-1)
-    weights = jnp.where(allowed, jnp.exp(scores - high[..., None]), 0.0)
-    total = jnp.sum(weights, axis=-1)
-    log_total = high + jnp.log(total)
-    prob_full = jnp.where(allowed, jnp.exp(scores - log_total[..., None]), 0.0)
-    grad_dots = jnp.einsum(
-        "sghd,kgd->ghsk", grad_four, value_three, preferred_element_type=jnp.float32
-    )
-    row_delta = jnp.sum(prob_full * grad_dots, axis=-1)
-    dscores = (prob_full * (grad_dots - row_delta[..., None]) * scaling).astype(jnp.bfloat16)
-    prob_half = prob_full.astype(jnp.bfloat16)
-    query_acc = jnp.einsum("ghsk,kgd->sghd", dscores, key_three, preferred_element_type=jnp.float32)
-    key_terms = jnp.einsum(
-        "ghsk,sghd->kgd", dscores, query_four, preferred_element_type=jnp.float32
-    ).reshape(piece_rows, kv_cols)
-    value_terms = jnp.einsum(
-        "ghsk,sghd->kgd", prob_half, grad_four, preferred_element_type=jnp.float32
-    ).reshape(piece_rows, kv_cols)
-    kv_grad = lax.psum_scatter(
-        jnp.concatenate([key_terms, value_terms], axis=1).astype(jnp.bfloat16),
-        "seq", scatter_dimension=0, tiled=True,
-    )
-    query_grad = query_acc.reshape(rows_here, groups * per_group * head_size).astype(jnp.bfloat16)
+    heads = groups * per_group
+    q_rows = queries.reshape(rows_here, heads, head_size).transpose(1, 0, 2).reshape(
+        heads * rows_here, head_size)
+    g_rows = attn_grad.reshape(rows_here, heads, head_size).transpose(1, 0, 2).reshape(
+        heads * rows_here, head_size)
+    dq_rows, kv_terms = attention_grads(
+        q_rows, g_rows, kv_block, doc_starts, first_row, rows_here, scaling)
+    query_grad = dq_rows.reshape(heads, rows_here, head_size).transpose(1, 0, 2).reshape(
+        rows_here, heads * head_size)
+    kv_grad = lax.psum_scatter(kv_terms, "seq", scatter_dimension=0, tiled=True)
     key_grad = kv_grad[:, :kv_cols]
     value_grad = kv_grad[:, kv_cols:]
     return (query_grad, key_grad, value_grad)

time: 229 us -> 206 us (0.90)
  matrix products: 38.8 us -> 4.59 us
  other arithmetic: 24.6 us -> 5.89 us
  waiting for transfers between devices: 106 us -> 124 us
  Pallas kernels: 36 us -> 48.8 us
  local copies, waits for them, and re-layouts: 8.88 us -> 5.45 us
  between operations: 14.2 us -> 16.7 us
    reduce_scatter x0 -> x1, waiting for transfers between devices: none -> 111 us  [shards(): kv_grad = lax.psum_scatter(kv_terms, 'seq', scatter_dimension=0, tiled=True)]
    unnamed x3 -> x2, waiting for transfers between devices: 86 us -> 0.03 us
    dot_general x5 -> x0, matrix products: 34.4 us -> none  [the longest x1 15.1 us: shards(): jnp.einsum('sghd,kgd->ghsk', grad_four, value_three, preferred_element_ty...]
    pallas_call x0 -> x2, Pallas kernels: none -> 13.8 us  [the longest x1 8.44 us: attention_grads(): pl.pallas_call(functools.partial(_grad_kernel, scaling, tk, dh), grid_spe...]
    another operation x1, other arithmetic: 13.9 us -> 0.66 us  [attention_grads(): jnp.stack([doc_first // tk, (first_row + rows_here - 1) // tk])]
    all_gather x1, waiting for transfers between devices: 20.2 us -> 13 us  [shards(): lax.all_gather(jnp.concatenate([keys, values], axis=1), 'seq', axis=0, ti...]
    unnamed x8 -> x6, local copies, waits for them, and re-layouts: 7.26 us -> 0.92 us
    reduce_sum x1 -> x0, other arithmetic: 6.34 us -> none  [shards(): total = jnp.sum(weights, axis=-1)]
  transfers between devices with their start and end apart: 2 -> 2, of which waited for: 2 -> 2; matrix products, arithmetic and copies ran while one was open for 6% -> 6% of each run, Pallas kernels for 16% -> 17%
where the time goes in v6:
time: 206 us
  waiting for transfers between devices  124 us (60%)
  Pallas kernels  48.8 us (24%)
  between operations  16.7 us (8%)
  other arithmetic  5.89 us (3%)
  local copies, waits for them, and re-layouts  5.45 us (3%)
  matrix products  4.59 us (2%)
    reduce_scatter x1, waiting for transfers between devices, shards(): kv_grad = lax.psum_scatter(kv_terms, 'seq', scatter_dimension=0, tiled=True)  111 us
    pallas_call x1, Pallas kernels, peer_blocks(): pl.pallas_call(functools.partial(_peer_kernel, n, axis, upward, per_targe...  35 us
    all_gather x1, waiting for transfers between devices, shards(): lax.all_gather(jnp.concatenate([keys, values], axis=1), 'seq', axis=0, ti...  13 us
    pallas_call x1, Pallas kernels, attention_grads(): pl.pallas_call(functools.partial(_grad_kernel, scaling, tk, dh), grid_spe...  8.44 us
    pallas_call x1, Pallas kernels, attention_grads(): pl.pallas_call(functools.partial(_stats_kernel, scaling, tk, dh), grid_sp...  5.33 us
    dot_general x1, matrix products, shards(): jnp.einsum('hte,che->tc', d_all, w_out.reshape(w_out.shape[0], n_head, d_...  4.59 us
  transfers between devices with their start and end apart: 2, of which 2 were waited for; matrix products, arithmetic and copies ran while one was open for 6% of the time, Pallas kernels for 17%

profile of v6, /device:TPU:8, one launch (start us, length us, event | category | flops | bytes accessed | tf_op | source)
XLA Modules:
  0.0 205.8 jit_solution(5134768664680136938)
XLA Ops:
  7.2 0.0 copy-start
  7.2 0.0 all-gather.2.cloned.1.call-start
  7.2 1.5 pad_maximum_fusion
  8.7 0.0 all-gather.2.cloned.1.call-update
  8.8 0.0 reduce-scatter.2.cloned.1.call-start
  8.8 1.3 fusion.29
  12.7 0.7 convert_reduce_fusion.1
  13.5 0.9 broadcast_in_dim.38.rowdoc_ref
  14.4 35.0 %shard_map.85 = bf16[8,192,512]{2,1,0:T(8,128)(2,1)} custom-call(bf16[192,512]{1,0:T(8,128)(2,1)} %src_ref.1), custom_call_target="tpu_custom_call" | custom-call | tf_op jit(solution)/shard_map/pallas_call | solution.py:77
  49.5 0.0 copy-start.2
  49.5 4.6 %fusion.15 = bf16[24,4,8,128]{3,2,1,0:T(8,128)(2,1)S(1)} fusion(bf16[64,8,8,512]{3,2,1,0:T(8,128)(2,1)} %bitcast.50, bf16[8,192,512]{2,1,0:T(8,128)(2,1)} %shard_map.85, pred[8]{0:T(512)(128)(4,1)S(1)} %iota_compare_fusion.1, bf16[192,512]{1,0:T(8,128)(2,1)} %src_ref.1), kind=kOutput, calls=%fused_computation.7 | convolution fusion | flops 806191104 | bytes 6160392 | tf_op jit(solution)/shard_map/hte,che->tc/dot_general | solution.py:241
  54.1 0.7 copy.43
  54.8 0.7 pad_add_fusion.bounds_ref
  55.5 0.0 copy-done.2
  55.5 0.7 convert_reduce_fusion
  56.2 0.9 fusion.21.rowpos_ref
  57.1 0.0 copy-done
  57.1 0.7 copy_bitcast_fusion.2
  57.8 13.0 %all-gather.2.cloned.1.call-done.kv_ref = bf16[6144,256]{1,0:T(8,128)(2,1)} async-done(((bf16[192,256]{1,0:T(8,128)(2,1)}), bf16[6144,256]{1,0:T(8,128)(2,1)}) %all-gather.2.cloned.1.call-update) | async-done | bytes 3145744 | tf_op jit(solution)/shard_map/all_gather | solution.py:233
  70.8 5.3 %shard_map.86 = (f32[768,1]{1,0:T(8,128)}, f32[768,1]{1,0:T(8,128)}) custom-call(s32[2]{0:T(128)} %pad_add_fusion.bounds_ref, bf16[768,128]{1,0:T(8,128)(2,1)} %bitcast.45, bf16[768,128]{1,0:T(8,128)(2,1)} %bitcast.42, bf16[6144,256]{1,0:T(8,128)(2,1)} %all-gather.2.cloned.1.call-done.kv_ref, s32[768,1]{1,0:T(8,128)} %fusion.21.rowpos_ref, ...), custom_call_target="tpu_custom_call" | custom-call | flops 2415919104 | bytes 3145728 | tf_op jit(solution)/shard_map/pallas_call | solution.py:192
  76.1 8.4 %shard_map.87 = (bf16[768,128]{1,0:T(8,128)(2,1)}, bf16[6144,256]{1,0:T(8,128)(2,1)}) custom-call(s32[2]{0:T(128)} %pad_add_fusion.bounds_ref, bf16[768,128]{1,0:T(8,128)(2,1)} %bitcast.46, bf16[768,128]{1,0:T(8,128)(2,1)} %bitcast.43, bf16[6144,256]{1,0:T(8,128)(2,1)} %all-gather.2.cloned.1.call-done.kv_ref, s32[768,1]{1,0:T(8,128)} %fusion.21.rowpos_ref, ...), custom_call_target="tpu_custom_call" | custom-call | flops 6039797760 | bytes 6291456 | tf_op jit(solution)/shard_map/pallas_call | solution.py:206
  84.6 0.0 copy-start.1
  84.6 0.0 reduce-scatter.2.cloned.1.call-update
  84.6 0.9 copy-done.1
  85.5 0.7 copy.42
  86.2 111.3 %reduce-scatter.2.cloned.1.call-done = bf16[192,256]{1,0:T(8,128)(2,1)} async-done(((bf16[6144,256]{1,0:T(8,128)(2,1)}), bf16[192,256]{1,0:T(8,128)(2,1)}) %reduce-scatter.2.cloned.1.call-update) | async-done | bytes 98320 | tf_op jit(solution)/shard_map/reduce_scatter | solution.py:256
  197.5 1.5 fusion.30
  (2 shorter events, 0.0 us)
Async XLA Ops:
  7.2 50.0 %copy-start = (bf16[192,512]{1,0:T(8,128)(2,1)S(1)}, bf16[192,512]{1,0:T(8,128)(2,1)}, u32[]{:S(2)}) copy-start(bf16[192,512]{1,0:T(8,128)(2,1)} %param.6) | copy-start | bytes 589828
  7.2 63.6 %all-gather.2.cloned.1.call-start = ((), (), s32[]{:S(2)}) async-start(), calls=%async_computation.1 | async-start | bytes 3244032 | tf_op jit(solution)/shard_map/all_gather | solution.py:233
  8.8 188.8 %reduce-scatter.2.cloned.1.call-start = ((), (), s32[]{:S(2)}) async-start(), calls=%async_computation.2 | async-start | bytes 3244032 | tf_op jit(solution)/shard_map/reduce_scatter | solution.py:256
  49.5 6.0 %copy-start.2 = (s32[4]{0:T(128)S(1)}, s32[4]{0:T(128)}, u32[]{:S(2)}) copy-start(s32[4]{0:T(128)} %param.11) | copy-start | bytes 52
  84.6 0.9 copy-start.1
Sparse Core Ops, SparseCore 0:
  10.6 60.2 all-gather.1
  84.7 112.7 reduce-scatter.1

commit v7 on v6

--- a/solution.py
+++ b/solution.py
@@ -82,9 +82,6 @@
         scratch_shapes=[pltpu.SemaphoreType.DMA((n - 1,)), pltpu.SemaphoreType.DMA((n - 1,))],
         compiler_params=pltpu.CompilerParams(has_side_effects=True),
     )(src)
-
-
-KEY_TILE = 512
 
 
 def _tile_mask(j, tk, rowpos_ref, rowdoc_ref, coldoc_ref):
@@ -150,8 +147,11 @@
         dk = lax.dot_general(ds, q_ref[...], tdims, preferred_element_type=jnp.float32)
         dv = lax.dot_general(probs.astype(jnp.bfloat16), g_ref[...], tdims,
                              preferred_element_type=jnp.float32)
-        dkv_ref[:, :dh] = dk.astype(dkv_ref.dtype)
-        dkv_ref[:, dh:] = dv.astype(dkv_ref.dtype)
+        owner_rows = dkv_ref.shape[3]
+        for c in range(dkv_ref.shape[0]):
+            part = slice(c * owner_rows, (c + 1) * owner_rows)
+            dkv_ref[c, 0, 0, :, :dh] = dk[part].astype(dkv_ref.dtype)
+            dkv_ref[c, 0, 0, :, dh:] = dv[part].astype(dkv_ref.dtype)
 
     @pl.when(jnp.logical_not(active))
     def _():
@@ -162,10 +162,11 @@
         dq_ref[...] = dq_sc[...].astype(dq_ref.dtype)
 
 
-def attention_grads(q_rows, g_rows, kv_full, doc_starts, first_row, rows_here, scaling):
+def attention_grads(q_rows, g_rows, kv_full, doc_starts, first_row, rows_here, scaling, chips):
     n_rows, dh = q_rows.shape
     n_keys = kv_full.shape[0]
-    tk = KEY_TILE
+    n_zh, n_x, n_core = chips
+    tk = n_core * rows_here
     n_tiles = n_keys // tk
     row_pos = first_row + jnp.arange(n_rows, dtype=jnp.int32) % rows_here
     row_doc = doc_index(doc_starts, row_pos)
@@ -209,16 +210,29 @@
             num_scalar_prefetch=1,
             grid=(n_tiles,),
             in_specs=in_specs + [full((n_rows, 1)), full((n_rows, 1))],
-            out_specs=[full((n_rows, dh)), pl.BlockSpec((tk, 2 * dh), lambda j, b: (j, 0))],
+            out_specs=[
+                full((n_rows, dh)),
+                pl.BlockSpec((n_core, 1, 1, rows_here, 2 * dh),
+                             lambda j, b: (0, j % n_x, j // n_x, 0, 0)),
+            ],
             scratch_shapes=[pltpu.VMEM((n_rows, dh), jnp.float32)],
         ),
         out_shape=[jax.ShapeDtypeStruct((n_rows, dh), jnp.bfloat16),
-                   jax.ShapeDtypeStruct((n_keys, 2 * dh), jnp.bfloat16)],
+                   jax.ShapeDtypeStruct((n_core, n_x, n_zh, rows_here, 2 * dh), jnp.bfloat16)],
         compiler_params=params,
         cost_estimate=pl.CostEstimate(flops=5 * mm, transcendentals=n_rows * n_keys,
                                       bytes_accessed=n_keys * 8 * dh),
     )(bounds, q_rows, g_rows, kv_full, row_pos, row_doc, col_doc, log_total, delta)
     return dq, dkv
+
+
+def stage_reduce(parts, axis):
+    n = lax.axis_size(axis)
+    me = lax.axis_index(axis)
+    slots = peer_blocks(parts.astype(jnp.bfloat16), n, axis, None, True)
+    ids = jnp.arange(n, dtype=jnp.int32).reshape((n,) + (1,) * (parts.ndim - 1))
+    others = jnp.sum(jnp.where(ids == me, 0.0, slots.astype(jnp.float32)), axis=0)
+    return others + lax.dynamic_index_in_dim(parts, me, 0, keepdims=False).astype(jnp.float32)
 
 
 def shards(queries, keys, values, d_out, w_out, doc_starts):
@@ -228,10 +242,14 @@
     per_group = queries.shape[1] // keys.shape[1]
     kv_cols = keys.shape[1]
     scaling = 1.0 / math.sqrt(head_size)
-    first_row = lax.axis_index("seq") * rows_here
+    n_zh = lax.axis_size("zhi")
+    n_x = lax.axis_size("xx")
+    n_core = lax.axis_size("core")
+    me = (lax.axis_index("zhi") * n_x + lax.axis_index("xx")) * n_core + lax.axis_index("core")
+    first_row = me * rows_here
     my_rows = first_row + jnp.arange(rows_here, dtype=jnp.int32)
     kv_block = lax.all_gather(
-        jnp.concatenate([keys, values], axis=1), "seq", axis=0, tiled=True
+        jnp.concatenate([keys, values], axis=1), ("zhi", "xx", "core"), axis=0, tiled=True
     )
     n_head = lax.axis_size("head")
     me_head = lax.axis_index("head")
@@ -250,27 +268,36 @@
     g_rows = attn_grad.reshape(rows_here, heads, head_size).transpose(1, 0, 2).reshape(
         heads * rows_here, head_size)
     dq_rows, kv_terms = attention_grads(
-        q_rows, g_rows, kv_block, doc_starts, first_row, rows_here, scaling)
+        q_rows, g_rows, kv_block, doc_starts, first_row, rows_here, scaling,
+        (n_zh, n_x, n_core))
     query_grad = dq_rows.reshape(heads, rows_here, head_size).transpose(1, 0, 2).reshape(
         rows_here, heads * head_size)
-    kv_grad = lax.psum_scatter(kv_terms, "seq", scatter_dimension=0, tiled=True)
+    kv_grad = kv_terms
+    for axis in ("core", "xx", "zhi"):
+        kv_grad = stage_reduce(kv_grad, axis)
+    kv_grad = kv_grad.astype(jnp.bfloat16)
     key_grad = kv_grad[:, :kv_cols]
     value_grad = kv_grad[:, kv_cols:]
     return (query_grad, key_grad, value_grad)
 
 
 def solution(mesh):
+    n_seq, n_head = mesh.shape["seq"], mesh.shape["head"]
+    split = jax.sharding.Mesh(
+        mesh.devices.reshape(n_seq // 8, 4, 2, n_head), ("zhi", "xx", "core", "head")
+    )
+    rows = ("zhi", "xx", "core")
     return jax.shard_map(
         shards,
-        mesh=mesh,
+        mesh=split,
         in_specs=(
-            P("seq", "head"),
-            P("seq", "head"),
-            P("seq", "head"),
-            P("seq", "head"),
+            P(rows, "head"),
+            P(rows, "head"),
+            P(rows, "head"),
+            P(rows, "head"),
             P("head", None),
             P(),
         ),
-        out_specs=(P("seq", "head"), P("seq", "head"), P("seq", "head")),
+        out_specs=(P(rows, "head"), P(rows, "head"), P(rows, "head")),
         check_vma=False,
     )

time: 206 us -> 191 us (0.927)
  waiting for transfers between devices: 124 us -> 13.6 us
  Pallas kernels: 48.8 us -> 136 us
  other arithmetic: 5.89 us -> 15.1 us
    reduce_scatter x1 -> x0, waiting for transfers between devices: 111 us -> none  [shards(): kv_grad = lax.psum_scatter(kv_terms, 'seq', scatter_dimension=0, tiled=True)]
    pallas_call x1 -> x4, Pallas kernels: 35 us -> 121 us  [peer_blocks(): pl.pallas_call(functools.partial(_peer_kernel, n, axis, upward, per_targe...]
    reduce_sum x0 -> x3, other arithmetic: none -> 6.2 us  [stage_reduce(): jnp.sum(jnp.where(ids == me, 0.0, slots.astype(jnp.float32)), axis=0)]
    convert_element_type x0 -> x3, other arithmetic: none -> 3.79 us  [the longest x2 2.83 us: stage_reduce(): slots = peer_blocks(parts.astype(jnp.bfloat16), n, axis, None, True)]
  transfers between devices with their start and end apart: 2 -> 1, of which waited for: 2 -> 1; matrix products, arithmetic and copies ran while one was open for 6% -> 6% of each run, Pallas kernels for 17% -> 19%
where the time goes in v7:
time: 191 us; the launch traced here: 190 us
  Pallas kernels  136 us (71%)
  between operations  16.1 us (8%)
  other arithmetic  15.1 us (8%)
  waiting for transfers between devices  13.6 us (7%)
  local copies, waits for them, and re-layouts  4.64 us (2%)
  matrix products  4.56 us (2%)
    pallas_call x4, Pallas kernels, peer_blocks(): pl.pallas_call(functools.partial(_peer_kernel, n, axis, upward, per_targe...  121 us
    all_gather x1, waiting for transfers between devices, shards(): lax.all_gather(jnp.concatenate([keys, values], axis=1), ('zhi', 'xx', 'co...  13.6 us
    pallas_call x1, Pallas kernels, attention_grads(): pl.pallas_call(functools.partial(_grad_kernel, scaling, tk, dh), grid_spe...  9.43 us
    reduce_sum x3, other arithmetic, stage_reduce(): jnp.sum(jnp.where(ids == me, 0.0, slots.astype(jnp.float32)), axis=0)  6.2 us
    pallas_call x1, Pallas kernels, attention_grads(): pl.pallas_call(functools.partial(_stats_kernel, scaling, tk, dh), grid_sp...  5.41 us
    dot_general x1, matrix products, shards(): jnp.einsum('hte,che->tc', d_all, w_out.reshape(w_out.shape[0], n_head, d_...  4.56 us
  transfers between devices with their start and end apart: 1, of which 1 were waited for; matrix products, arithmetic and copies ran while one was open for 6% of the time, Pallas kernels for 19%

profile of v7, /device:TPU:8, one launch (start us, length us, event | category | flops | bytes accessed | tf_op | source)
XLA Modules:
  0.0 190.4 jit_solution(15659292861920415267)
XLA Ops:
  7.2 0.0 copy-start
  7.2 0.0 all-gather.2.cloned.1.call-start
  7.2 1.5 pad_maximum_fusion
  8.7 0.0 all-gather.2.cloned.1.call-update
  8.8 1.3 fusion.30
  12.0 36.0 %shard_map.85 = bf16[8,192,512]{2,1,0:T(8,128)(2,1)} custom-call(bf16[192,512]{1,0:T(8,128)(2,1)} %src_ref.1), custom_call_target="tpu_custom_call" | custom-call | tf_op jit(solution)/shard_map/pallas_call | solution.py:77
  48.1 0.0 copy-start.2
  48.1 4.6 %fusion.15 = bf16[24,4,8,128]{3,2,1,0:T(8,128)(2,1)S(1)} fusion(bf16[64,8,8,512]{3,2,1,0:T(8,128)(2,1)} %bitcast.61, bf16[8,192,512]{2,1,0:T(8,128)(2,1)} %shard_map.85, pred[8]{0:T(512)(128)(4,1)S(1)} %iota_compare_fusion.4, bf16[192,512]{1,0:T(8,128)(2,1)} %src_ref.1), kind=kOutput, calls=%fused_computation.10 | convolution fusion | flops 806191104 | bytes 6160392 | tf_op jit(solution)/shard_map/hte,che->tc/dot_general | solution.py:259
  52.6 0.7 copy.43
  53.4 0.0 copy-done.2
  53.4 0.1 convert_reduce_fusion.1
  53.4 0.9 broadcast_in_dim.80.rowdoc_ref
  54.4 0.6 pad_add_fusion.bounds_ref
  55.0 0.7 convert_reduce_fusion
  55.7 0.9 fusion.21.rowpos_ref
  56.6 0.0 copy-done
  56.6 0.7 copy_bitcast_fusion.2
  57.3 13.6 %all-gather.2.cloned.1.call-done.kv_ref = bf16[6144,256]{1,0:T(8,128)(2,1)} async-done(((bf16[192,256]{1,0:T(8,128)(2,1)}), bf16[6144,256]{1,0:T(8,128)(2,1)}) %all-gather.2.cloned.1.call-update) | async-done | bytes 3145744 | tf_op jit(solution)/shard_map/all_gather | solution.py:251
  71.0 5.4 %shard_map.86 = (f32[768,1]{1,0:T(8,128)}, f32[768,1]{1,0:T(8,128)}) custom-call(s32[2]{0:T(128)} %pad_add_fusion.bounds_ref, bf16[768,128]{1,0:T(8,128)(2,1)} %bitcast.56, bf16[768,128]{1,0:T(8,128)(2,1)} %bitcast.53, bf16[6144,256]{1,0:T(8,128)(2,1)} %all-gather.2.cloned.1.call-done.kv_ref, s32[768,1]{1,0:T(8,128)} %fusion.21.rowpos_ref, ...), custom_call_target="tpu_custom_call" | custom-call | flops 2415919104 | bytes 3145728 | tf_op jit(solution)/shard_map/pallas_call | solution.py:193
  76.4 9.4 %shard_map.87 = (bf16[768,128]{1,0:T(8,128)(2,1)}, bf16[2,4,4,192,256]{4,3,2,1,0:T(8,128)(2,1)}) custom-call(s32[2]{0:T(128)} %pad_add_fusion.bounds_ref, bf16[768,128]{1,0:T(8,128)(2,1)} %bitcast.57, bf16[768,128]{1,0:T(8,128)(2,1)} %bitcast.54, bf16[6144,256]{1,0:T(8,128)(2,1)} %all-gather.2.cloned.1.call-done.kv_ref, s32[768,1]{1,0:T(8,128)} %fusion.21.rowpos_ref, ...), custom_call_target="tpu_custom_call" | custom-call | flops 6039797760 | bytes 6291456 | tf_op jit(solution)/shard_map/pallas_call | solution.py:207
  85.8 1.6 copy.42
  87.4 26.2 %shard_map.88 = bf16[2,4,4,192,256]{4,3,2,1,0:T(8,128)(2,1)} custom-call(bf16[2,4,4,192,256]{4,3,2,1,0:T(8,128)(2,1)} %get-tuple-element.10.src_ref), custom_call_target="tpu_custom_call" | custom-call | tf_op jit(solution)/shard_map/pallas_call | solution.py:77
  113.6 0.0 copy-start.1
  113.6 3.2 %select_reduce_fusion = f32[4,4,192,256]{3,2,1,0:T(8,128)S(1)} fusion(bf16[2,4,4,192,256]{4,3,2,1,0:T(8,128)(2,1)} %shard_map.88, pred[2]{0:T(512)(128)(4,1)S(1)} %iota_compare_fusion.1), kind=kLoop, calls=%fused_computation | loop fusion | flops 3932160 | bytes 6291458 | tf_op jit(solution)/shard_map/reduce_sum | solution.py:234
  116.8 0.0 copy-done.1
  116.8 1.7 fusion.32
  118.5 33.0 %shard_map.89 = bf16[4,4,192,256]{3,2,1,0:T(8,128)(2,1)} custom-call(bf16[4,4,192,256]{3,2,1,0:T(8,128)(2,1)} %get-tuple-element.13.src_ref), custom_call_target="tpu_custom_call" | custom-call | tf_op jit(solution)/shard_map/pallas_call | solution.py:77
  151.5 1.9 select_reduce_fusion.1
  153.4 1.1 fusion.31
  154.5 26.2 %shard_map.90 = bf16[4,192,256]{2,1,0:T(8,128)(2,1)} custom-call(bf16[4,192,256]{2,1,0:T(8,128)(2,1)} %get-tuple-element.11.src_ref), custom_call_target="tpu_custom_call" | custom-call | tf_op jit(solution)/shard_map/pallas_call | solution.py:77
  180.8 1.2 select_reduce_fusion.2
  181.9 1.0 fusion.25
  182.9 0.6 fusion.33
  (5 shorter events, 0.0 us)
Async XLA Ops:
  7.2 49.5 %copy-start = (bf16[192,512]{1,0:T(8,128)(2,1)S(1)}, bf16[192,512]{1,0:T(8,128)(2,1)}, u32[]{:S(2)}) copy-start(bf16[192,512]{1,0:T(8,128)(2,1)} %param.6) | copy-start | bytes 589828
  7.2 63.8 %all-gather.2.cloned.1.call-start = ((), (), s32[]{:S(2)}) async-start(), calls=%async_computation | async-start | bytes 3244032 | tf_op jit(solution)/shard_map/all_gather | solution.py:251
  48.1 5.3 %copy-start.2 = (s32[4]{0:T(128)S(1)}, s32[4]{0:T(128)}, u32[]{:S(2)}) copy-start(s32[4]{0:T(128)} %param.11) | copy-start | bytes 52
  113.6 3.2 %copy-start.1 = (bf16[2,4,4,192,256]{4,3,2,1,0:T(8,128)(2,1)S(1)}, bf16[2,4,4,192,256]{4,3,2,1,0:T(8,128)(2,1)}, u32[]{:S(2)}) copy-start(bf16[2,4,4,192,256]{4,3,2,1,0:T(8,128)(2,1)} %get-tuple-element.10.src_ref) | copy-start | bytes 9437188
Sparse Core Ops, SparseCore 0:
  10.6 60.3 all-gather.1

commit v8 on v7

--- a/solution.py
+++ b/solution.py
@@ -26,6 +26,15 @@
 
 def _peer_kernel(n, axis, upward, per_target, src_ref, out_ref, send_sem, recv_sem):
     me = lax.axis_index(axis)
+    barrier = pltpu.get_barrier_semaphore()
+
+    def greet(k, carry):
+        pl.semaphore_signal(barrier, 1, device_id={axis: lax.rem(me + k, n)},
+                            device_id_type=pl.DeviceIdType.MESH)
+        return carry
+
+    lax.fori_loop(1, n, greet, 0)
+    pl.semaphore_wait(barrier, n - 1)
     step = -1 if upward is False else 1
 
     def send_desc(k):
@@ -72,7 +81,7 @@
     lax.fori_loop(1, n, finish_one, 0)
 
 
-def peer_blocks(src, n, axis, upward, per_target):
+def peer_blocks(src, n, axis, upward, per_target, cid):
     blk = src.shape[1:] if per_target else src.shape
     return pl.pallas_call(
         functools.partial(_peer_kernel, n, axis, upward, per_target),
@@ -80,7 +89,7 @@
         in_specs=[pl.BlockSpec(memory_space=pl.ANY)],
         out_specs=pl.BlockSpec(memory_space=pl.ANY),
         scratch_shapes=[pltpu.SemaphoreType.DMA((n - 1,)), pltpu.SemaphoreType.DMA((n - 1,))],
-        compiler_params=pltpu.CompilerParams(has_side_effects=True),
+        compiler_params=pltpu.CompilerParams(collective_id=cid, has_side_effects=True),
     )(src)
 
 
@@ -226,10 +235,10 @@
     return dq, dkv
 
 
-def stage_reduce(parts, axis):
+def stage_reduce(parts, axis, cid):
     n = lax.axis_size(axis)
     me = lax.axis_index(axis)
-    slots = peer_blocks(parts.astype(jnp.bfloat16), n, axis, None, True)
+    slots = peer_blocks(parts.astype(jnp.bfloat16), n, axis, None, True, cid)
     ids = jnp.arange(n, dtype=jnp.int32).reshape((n,) + (1,) * (parts.ndim - 1))
     others = jnp.sum(jnp.where(ids == me, 0.0, slots.astype(jnp.float32)), axis=0)
     return others + lax.dynamic_index_in_dim(parts, me, 0, keepdims=False).astype(jnp.float32)
@@ -253,7 +262,7 @@
     )
     n_head = lax.axis_size("head")
     me_head = lax.axis_index("head")
-    d_slots = peer_blocks(d_out, n_head, "head", None, False)
+    d_slots = peer_blocks(d_out, n_head, "head", None, False, 0)
     head_ids = jnp.arange(n_head, dtype=jnp.int32)[:, None, None]
     d_all = jnp.where(head_ids == me_head, d_out[None], d_slots)
     attn_grad = jnp.einsum(
@@ -273,8 +282,8 @@
     query_grad = dq_rows.reshape(heads, rows_here, head_size).transpose(1, 0, 2).reshape(
         rows_here, heads * head_size)
     kv_grad = kv_terms
-    for axis in ("core", "xx", "zhi"):
-        kv_grad = stage_reduce(kv_grad, axis)
+    for cid, axis in enumerate(("core", "xx", "zhi")):
+        kv_grad = stage_reduce(kv_grad, axis, cid + 1)
     kv_grad = kv_grad.astype(jnp.bfloat16)
     key_grad = kv_grad[:, :kv_cols]
     value_grad = kv_grad[:, kv_cols:]

time: 191 us -> 170 us (0.89)
  Pallas kernels: 136 us -> 103 us
  waiting for transfers between devices: 13.6 us -> 25.1 us
    pallas_call x4, Pallas kernels: 121 us -> 87.9 us  [peer_blocks(): pl.pallas_call(functools.partial(_peer_kernel, n, axis, upward, per_targe...]
    all_gather x1, waiting for transfers between devices: 13.6 us -> 25.1 us  [shards(): lax.all_gather(jnp.concatenate([keys, values], axis=1), ('zhi', 'xx', 'co...]
  transfers between devices with their start and end apart: 1 -> 1, of which waited for: 1 -> 1; matrix products, arithmetic and copies ran while one was open for 6% -> 6% of each run, Pallas kernels for 19% -> 14%
where the time goes in v8:
time: 170 us; the launch traced here: 168 us
  Pallas kernels  103 us (61%)
  waiting for transfers between devices  25.1 us (15%)
  between operations  16.1 us (9%)
  other arithmetic  15.1 us (9%)
  local copies, waits for them, and re-layouts  4.64 us (3%)
  matrix products  4.36 us (3%)
    pallas_call x4, Pallas kernels, peer_blocks(): pl.pallas_call(functools.partial(_peer_kernel, n, axis, upward, per_targe...  87.9 us
    all_gather x1, waiting for transfers between devices, shards(): lax.all_gather(jnp.concatenate([keys, values], axis=1), ('zhi', 'xx', 'co...  25.1 us
    pallas_call x1, Pallas kernels, attention_grads(): pl.pallas_call(functools.partial(_grad_kernel, scaling, tk, dh), grid_spe...  9.43 us
    reduce_sum x3, other arithmetic, stage_reduce(): jnp.sum(jnp.where(ids == me, 0.0, slots.astype(jnp.float32)), axis=0)  6.2 us
    pallas_call x1, Pallas kernels, attention_grads(): pl.pallas_call(functools.partial(_stats_kernel, scaling, tk, dh), grid_sp...  5.41 us
    dot_general x1, matrix products, shards(): jnp.einsum('hte,che->tc', d_all, w_out.reshape(w_out.shape[0], n_head, d_...  4.36 us
  transfers between devices with their start and end apart: 1, of which 1 were waited for; matrix products, arithmetic and copies ran while one was open for 6% of the time, Pallas kernels for 14%

profile of v8, /device:TPU:8, one launch (start us, length us, event | category | flops | bytes accessed | tf_op | source)
XLA Modules:
  0.0 168.2 jit_solution(8567599935562340576)
XLA Ops:
  7.2 0.0 copy-start
  7.2 0.0 all-gather.2.cloned.1.call-start
  7.2 1.5 pad_maximum_fusion
  8.7 0.0 all-gather.2.cloned.1.call-update
  8.8 1.3 fusion.30
  12.0 24.2 %shard_map.85 = bf16[8,192,512]{2,1,0:T(8,128)(2,1)} custom-call(bf16[192,512]{1,0:T(8,128)(2,1)} %src_ref.1), custom_call_target="tpu_custom_call" | custom-call | tf_op jit(solution)/shard_map/pallas_call | solution.py:86
  36.2 0.0 copy-start.2
  36.3 4.4 %fusion.15 = bf16[24,4,8,128]{3,2,1,0:T(8,128)(2,1)S(1)} fusion(bf16[64,8,8,512]{3,2,1,0:T(8,128)(2,1)} %bitcast.61, bf16[8,192,512]{2,1,0:T(8,128)(2,1)} %shard_map.85, pred[8]{0:T(512)(128)(4,1)S(1)} %iota_compare_fusion.4, bf16[192,512]{1,0:T(8,128)(2,1)} %src_ref.1), kind=kOutput, calls=%fused_computation.10 | convolution fusion | flops 806191104 | bytes 6160392 | tf_op jit(solution)/shard_map/hte,che->tc/dot_general | solution.py:268
  40.6 0.7 copy.43
  41.4 0.0 copy-done.2
  41.4 0.1 convert_reduce_fusion.1
  41.4 0.9 broadcast_in_dim.80.rowdoc_ref
  42.4 0.6 pad_add_fusion.bounds_ref
  43.0 0.7 convert_reduce_fusion
  43.7 0.9 fusion.21.rowpos_ref
  44.6 0.0 copy-done
  44.6 0.7 copy_bitcast_fusion.2
  45.3 25.1 %all-gather.2.cloned.1.call-done.kv_ref = bf16[6144,256]{1,0:T(8,128)(2,1)} async-done(((bf16[192,256]{1,0:T(8,128)(2,1)}), bf16[6144,256]{1,0:T(8,128)(2,1)}) %all-gather.2.cloned.1.call-update) | async-done | bytes 3145744 | tf_op jit(solution)/shard_map/all_gather | solution.py:260
  70.5 5.4 %shard_map.86 = (f32[768,1]{1,0:T(8,128)}, f32[768,1]{1,0:T(8,128)}) custom-call(s32[2]{0:T(128)} %pad_add_fusion.bounds_ref, bf16[768,128]{1,0:T(8,128)(2,1)} %bitcast.56, bf16[768,128]{1,0:T(8,128)(2,1)} %bitcast.53, bf16[6144,256]{1,0:T(8,128)(2,1)} %all-gather.2.cloned.1.call-done.kv_ref, s32[768,1]{1,0:T(8,128)} %fusion.21.rowpos_ref, ...), custom_call_target="tpu_custom_call" | custom-call | flops 2415919104 | bytes 3145728 | tf_op jit(solution)/shard_map/pallas_call | solution.py:202
  75.9 9.4 %shard_map.87 = (bf16[768,128]{1,0:T(8,128)(2,1)}, bf16[2,4,4,192,256]{4,3,2,1,0:T(8,128)(2,1)}) custom-call(s32[2]{0:T(128)} %pad_add_fusion.bounds_ref, bf16[768,128]{1,0:T(8,128)(2,1)} %bitcast.57, bf16[768,128]{1,0:T(8,128)(2,1)} %bitcast.54, bf16[6144,256]{1,0:T(8,128)(2,1)} %all-gather.2.cloned.1.call-done.kv_ref, s32[768,1]{1,0:T(8,128)} %fusion.21.rowpos_ref, ...), custom_call_target="tpu_custom_call" | custom-call | flops 6039797760 | bytes 6291456 | tf_op jit(solution)/shard_map/pallas_call | solution.py:216
  85.3 1.6 copy.42
  86.9 3.8 %shard_map.88 = bf16[2,4,4,192,256]{4,3,2,1,0:T(8,128)(2,1)} custom-call(bf16[2,4,4,192,256]{4,3,2,1,0:T(8,128)(2,1)} %get-tuple-element.10.src_ref), custom_call_target="tpu_custom_call" | custom-call | tf_op jit(solution)/shard_map/pallas_call | solution.py:86
  90.7 0.0 copy-start.1
  90.7 3.2 %select_reduce_fusion = f32[4,4,192,256]{3,2,1,0:T(8,128)S(1)} fusion(bf16[2,4,4,192,256]{4,3,2,1,0:T(8,128)(2,1)} %shard_map.88, pred[2]{0:T(512)(128)(4,1)S(1)} %iota_compare_fusion.1), kind=kLoop, calls=%fused_computation | loop fusion | flops 3932160 | bytes 6291458 | tf_op jit(solution)/shard_map/reduce_sum | solution.py:243
  93.9 0.0 copy-done.1
  93.9 1.7 %fusion.32 = (bf16[4,4,192,256]{3,2,1,0:T(8,128)(2,1)}, f32[4,4,192,256]{3,2,1,0:T(8,128)S(1)}) fusion(f32[4,4,192,256]{3,2,1,0:T(8,128)S(1)} %select_reduce_fusion, bf16[2,4,4,192,256]{4,3,2,1,0:T(8,128)(2,1)S(1)} %copy-done.1, s32[]{:T(128)S(6)} %select_n.63), kind=kLoop, calls=%fused_computation.43 | loop fusion | flops 2359296 | bytes 9437188 | tf_op jit(solution)/shard_map/convert_element_type | solution.py:241
  95.6 23.7 %shard_map.89 = bf16[4,4,192,256]{3,2,1,0:T(8,128)(2,1)} custom-call(bf16[4,4,192,256]{3,2,1,0:T(8,128)(2,1)} %get-tuple-element.13.src_ref), custom_call_target="tpu_custom_call" | custom-call | tf_op jit(solution)/shard_map/pallas_call | solution.py:86
  119.3 1.9 %select_reduce_fusion.1 = f32[4,192,256]{2,1,0:T(8,128)S(1)} fusion(bf16[4,4,192,256]{3,2,1,0:T(8,128)(2,1)} %shard_map.89, pred[4]{0:T(512)(128)(4,1)S(1)} %iota_compare_fusion.2), kind=kLoop, calls=%fused_computation.5 | loop fusion | flops 2162688 | bytes 2359300 | tf_op jit(solution)/shard_map/reduce_sum | solution.py:243
  121.2 1.1 fusion.31
  122.3 36.3 %shard_map.90 = bf16[4,192,256]{2,1,0:T(8,128)(2,1)} custom-call(bf16[4,192,256]{2,1,0:T(8,128)(2,1)} %get-tuple-element.11.src_ref), custom_call_target="tpu_custom_call" | custom-call | tf_op jit(solution)/shard_map/pallas_call | solution.py:86
  158.6 1.2 select_reduce_fusion.2
  159.8 1.0 fusion.25
  160.7 0.6 fusion.33
  (5 shorter events, 0.0 us)
Async XLA Ops:
  7.2 37.5 %copy-start = (bf16[192,512]{1,0:T(8,128)(2,1)S(1)}, bf16[192,512]{1,0:T(8,128)(2,1)}, u32[]{:S(2)}) copy-start(bf16[192,512]{1,0:T(8,128)(2,1)} %param.6) | copy-start | bytes 589828
  7.2 63.3 %all-gather.2.cloned.1.call-start = ((), (), s32[]{:S(2)}) async-start(), calls=%async_computation | async-start | bytes 3244032 | tf_op jit(solution)/shard_map/all_gather | solution.py:260
  36.2 5.1 %copy-start.2 = (s32[4]{0:T(128)S(1)}, s32[4]{0:T(128)}, u32[]{:S(2)}) copy-start(s32[4]{0:T(128)} %param.11) | copy-start | bytes 52
  90.7 3.2 %copy-start.1 = (bf16[2,4,4,192,256]{4,3,2,1,0:T(8,128)(2,1)S(1)}, bf16[2,4,4,192,256]{4,3,2,1,0:T(8,128)(2,1)}, u32[]{:S(2)}) copy-start(bf16[2,4,4,192,256]{4,3,2,1,0:T(8,128)(2,1)} %get-tuple-element.10.src_ref) | copy-start | bytes 9437188
Sparse Core Ops, SparseCore 0:
  10.6 59.8 all-gather.1

commit v9 on v8

--- a/solution.py
+++ b/solution.py
@@ -98,6 +98,10 @@
     return (col <= rowpos_ref[...]) & (coldoc_ref[...] == rowdoc_ref[...])
 
 
+def _key_tile(kv_ref):
+    return jnp.concatenate([kv_ref[c, 0, 0] for c in range(kv_ref.shape[0])], axis=0)
+
+
 def _stats_kernel(scaling, tk, dh, bounds_ref, q_ref, g_ref, kv_ref, rowpos_ref, rowdoc_ref,
                   coldoc_ref, lt_ref, delta_ref, m_sc, l_sc, a_sc):
     j = pl.program_id(0)
@@ -111,14 +115,15 @@
     @pl.when((j >= bounds_ref[0]) & (j <= bounds_ref[1]))
     def _():
         dims = (((1,), (1,)), ((), ()))
-        scores = lax.dot_general(q_ref[...], kv_ref[:, :dh], dims,
+        kv = _key_tile(kv_ref)
+        scores = lax.dot_general(q_ref[...], kv[:, :dh], dims,
                                  preferred_element_type=jnp.float32) * scaling
         allowed = _tile_mask(j, tk, rowpos_ref, rowdoc_ref, coldoc_ref)
         scores = jnp.where(allowed, scores, NEG_FILL)
         m_old = m_sc[...]
         m_new = jnp.maximum(m_old, jnp.max(scores, axis=1, keepdims=True))
         e = jnp.where(allowed, jnp.exp(scores - m_new), 0.0)
-        gd = lax.dot_general(g_ref[...], kv_ref[:, dh:], dims,
+        gd = lax.dot_general(g_ref[...], kv[:, dh:], dims,
                              preferred_element_type=jnp.float32)
         alpha = jnp.exp(m_old - m_new)
         l_sc[...] = alpha * l_sc[...] + jnp.sum(e, axis=1, keepdims=True)
@@ -144,12 +149,13 @@
     def _():
         dims = (((1,), (1,)), ((), ()))
         tdims = (((0,), (0,)), ((), ()))
-        k_t = kv_ref[:, :dh]
+        kv = _key_tile(kv_ref)
+        k_t = kv[:, :dh]
         scores = lax.dot_general(q_ref[...], k_t, dims,
                                  preferred_element_type=jnp.float32) * scaling
         allowed = _tile_mask(j, tk, rowpos_ref, rowdoc_ref, coldoc_ref)
         probs = jnp.where(allowed, jnp.exp(scores - lt_ref[...]), 0.0)
-        gd = lax.dot_general(g_ref[...], kv_ref[:, dh:], dims,
+        gd = lax.dot_general(g_ref[...], kv[:, dh:], dims,
                              preferred_element_type=jnp.float32)
         ds = (probs * (gd - delta_ref[...]) * scaling).astype(jnp.bfloat16)
         dq_sc[...] += jnp.dot(ds, k_t, preferred_element_type=jnp.float32)
@@ -173,7 +179,7 @@
 
 def attention_grads(q_rows, g_rows, kv_full, doc_starts, first_row, rows_here, scaling, chips):
     n_rows, dh = q_rows.shape
-    n_keys = kv_full.shape[0]
+    n_keys = kv_full.shape[0] * kv_full.shape[1] * kv_full.shape[2] * kv_full.shape[3]
     n_zh, n_x, n_core = chips
     tk = n_core * rows_here
     n_tiles = n_keys // tk
@@ -192,7 +198,8 @@
     in_specs = [
         full((n_rows, dh)),
         full((n_rows, dh)),
-        pl.BlockSpec((tk, 2 * dh), lambda j, b: (tile_of(j, b), 0)),
+        pl.BlockSpec((n_core, 1, 1, rows_here, 2 * dh),
+                     lambda j, b: (0, tile_of(j, b) % n_x, tile_of(j, b) // n_x, 0, 0)),
         full((n_rows, 1)),
         full((n_rows, 1)),
         pl.BlockSpec((1, tk), lambda j, b: (0, tile_of(j, b))),
@@ -244,6 +251,14 @@
     return others + lax.dynamic_index_in_dim(parts, me, 0, keepdims=False).astype(jnp.float32)
 
 
+def stage_gather(block, axis, cid):
+    n = lax.axis_size(axis)
+    me = lax.axis_index(axis)
+    slots = peer_blocks(block, n, axis, None, False, cid)
+    ids = jnp.arange(n, dtype=jnp.int32).reshape((n,) + (1,) * block.ndim)
+    return jnp.where(ids == me, block[None], slots)
+
+
 def shards(queries, keys, values, d_out, w_out, doc_starts):
     rows_here = queries.shape[0]
     head_size = DH
@@ -257,9 +272,9 @@
     me = (lax.axis_index("zhi") * n_x + lax.axis_index("xx")) * n_core + lax.axis_index("core")
     first_row = me * rows_here
     my_rows = first_row + jnp.arange(rows_here, dtype=jnp.int32)
-    kv_block = lax.all_gather(
-        jnp.concatenate([keys, values], axis=1), ("zhi", "xx", "core"), axis=0, tiled=True
-    )
+    kv_block = jnp.concatenate([keys, values], axis=1)
+    for cid, axis in enumerate(("zhi", "xx", "core")):
+        kv_block = stage_gather(kv_block, axis, cid + 4)
     n_head = lax.axis_size("head")
     me_head = lax.axis_index("head")
     d_slots = peer_blocks(d_out, n_head, "head", None, False, 0)

time: 170 us -> 174 us (1.024)
  Pallas kernels: 103 us -> 134 us
  waiting for transfers between devices: 25.1 us -> 0 us
  between operations: 16.1 us -> 2.81 us
  other arithmetic: 15.1 us -> 23.7 us
    pallas_call x4 -> x7, Pallas kernels: 87.9 us -> 119 us  [peer_blocks(): pl.pallas_call(functools.partial(_peer_kernel, n, axis, upward, per_targe...]
    all_gather x1 -> x0, waiting for transfers between devices: 25.1 us -> none  [shards(): lax.all_gather(jnp.concatenate([keys, values], axis=1), ('zhi', 'xx', 'co...]
    select_n x0 -> x3, other arithmetic: none -> 8.72 us  [stage_gather(): return jnp.where(ids == me, block[None], slots)]
  transfers between devices with their start and end apart: 1 -> 0, of which waited for: 1 -> 0; matrix products, arithmetic and copies ran while one was open for 6% -> 0% of each run, Pallas kernels for 14% -> 0%
where the time goes in v9:
time: 174 us; the launch traced here: 172 us
  Pallas kernels  134 us (77%)
  other arithmetic  23.7 us (14%)
  local copies, waits for them, and re-layouts  6.27 us (4%)
  matrix products  4.22 us (2%)
  between operations  2.81 us (2%)
    pallas_call x7, Pallas kernels, peer_blocks(): pl.pallas_call(functools.partial(_peer_kernel, n, axis, upward, per_targe...  119 us
    pallas_call x1, Pallas kernels, attention_grads(): pl.pallas_call(functools.partial(_grad_kernel, scaling, tk, dh), grid_spe...  9.46 us
    select_n x3, other arithmetic, stage_gather(): return jnp.where(ids == me, block[None], slots)  8.72 us
    reduce_sum x3, other arithmetic, stage_reduce(): jnp.sum(jnp.where(ids == me, 0.0, slots.astype(jnp.float32)), axis=0)  6.2 us
    pallas_call x1, Pallas kernels, attention_grads(): pl.pallas_call(functools.partial(_stats_kernel, scaling, tk, dh), grid_sp...  5.97 us
    dot_general x1, matrix products, shards(): jnp.einsum('hte,che->tc', d_all, w_out.reshape(w_out.shape[0], n_head, d_...  4.22 us

profile of v9, /device:TPU:8, one launch (start us, length us, event | category | flops | bytes accessed | tf_op | source)
XLA Modules:
  0.0 171.5 jit_solution(4955062587772610105)
XLA Ops:
  0.6 0.0 copy-start
  0.7 1.3 fusion.30
  4.0 0.6 pad_add_fusion.bounds_ref
  4.6 0.7 convert_reduce_fusion.1
  5.3 1.4 convert_reduce_fusion
  6.7 0.8 constant_dynamic-update-slice_fusion.1
  7.6 0.8 constant_dynamic-update-slice_fusion.src_ref
  8.4 0.0 copy-done
  8.4 0.0 copy-start.3
  8.4 0.7 copy_bitcast_fusion.2
  9.1 0.9 broadcast_in_dim.128.rowdoc_ref
  10.0 0.9 fusion.21.rowpos_ref
  11.0 0.0 copy-done.3
  11.0 15.8 %shard_map.86 = bf16[4,192,256]{2,1,0:T(8,128)(2,1)} custom-call(bf16[192,256]{1,0:T(8,128)(2,1)} %copy-done.3), custom_call_target="tpu_custom_call" | custom-call | tf_op jit(solution)/shard_map/pallas_call | solution.py:86
  26.8 1.8 %broadcast_select_fusion.2.src_ref = bf16[4,192,256]{2,1,0:T(8,128)(2,1)} fusion(bf16[4,192,256]{2,1,0:T(8,128)(2,1)} %shard_map.86, pred[4]{0:T(512)(128)(4,1)S(1)} %iota_compare_fusion.1, bf16[192,256]{1,0:T(8,128)(2,1)} %copy-done.3), kind=kLoop, calls=%fused_computation.21 | loop fusion | flops 196608 | bytes 884740 | tf_op jit(solution)/shard_map/jit(_where)/select_n | solution.py:259
  28.6 21.2 %shard_map.87 = bf16[4,4,192,256]{3,2,1,0:T(8,128)(2,1)} custom-call(bf16[4,192,256]{2,1,0:T(8,128)(2,1)} %broadcast_select_fusion.2.src_ref), custom_call_target="tpu_custom_call" | custom-call | tf_op jit(solution)/shard_map/pallas_call | solution.py:86
  49.8 0.0 copy-start.4
  49.8 2.9 %broadcast_select_fusion.1.src_ref = bf16[4,4,192,256]{3,2,1,0:T(8,128)(2,1)} fusion(bf16[4,4,192,256]{3,2,1,0:T(8,128)(2,1)} %shard_map.87, pred[4]{0:T(512)(128)(4,1)S(1)} %iota_compare_fusion.2, bf16[4,192,256]{2,1,0:T(8,128)(2,1)} %broadcast_select_fusion.2.src_ref), kind=kLoop, calls=%fused_computation.8 | loop fusion | flops 786432 | bytes 3538948 | tf_op jit(solution)/shard_map/jit(_where)/select_n | solution.py:259
  52.7 23.0 %shard_map.85 = bf16[8,192,512]{2,1,0:T(8,128)(2,1)} custom-call(bf16[192,512]{1,0:T(8,128)(2,1)} %src_ref.1), custom_call_target="tpu_custom_call" | custom-call | tf_op jit(solution)/shard_map/pallas_call | solution.py:86
  75.8 0.0 copy-done.4
  75.8 4.2 %fusion.15 = bf16[24,4,8,128]{3,2,1,0:T(8,128)(2,1)S(1)} fusion(bf16[64,8,8,512]{3,2,1,0:T(8,128)(2,1)} %bitcast.61, bf16[8,192,512]{2,1,0:T(8,128)(2,1)} %shard_map.85, pred[8]{0:T(512)(128)(4,1)S(1)} %iota_compare_fusion.4, bf16[192,512]{1,0:T(8,128)(2,1)S(1)} %copy-done.4), kind=kOutput, calls=%fused_computation.12 | convolution fusion | flops 806191104 | bytes 6160392 | tf_op jit(solution)/shard_map/hte,che->tc/dot_general | solution.py:283
  80.0 0.0 copy-start.1
  80.0 0.7 copy.43
  80.7 3.8 %shard_map.88 = bf16[2,4,4,192,256]{4,3,2,1,0:T(8,128)(2,1)} custom-call(bf16[4,4,192,256]{3,2,1,0:T(8,128)(2,1)} %broadcast_select_fusion.1.src_ref), custom_call_target="tpu_custom_call" | custom-call | tf_op jit(solution)/shard_map/pallas_call | solution.py:86
  84.5 0.0 copy-done.1
  84.5 4.0 %broadcast_select_fusion.kv_ref = bf16[2,4,4,192,256]{4,3,2,1,0:T(8,128)(2,1)} fusion(bf16[2,4,4,192,256]{4,3,2,1,0:T(8,128)(2,1)} %shard_map.88, pred[2]{0:T(512)(128)(4,1)S(1)} %iota_compare_fusion.3, bf16[4,4,192,256]{3,2,1,0:T(8,128)(2,1)S(1)} %copy-done.1), kind=kLoop, calls=%fused_computation.6 | loop fusion | flops 1572864 | bytes 7864322 | tf_op jit(solution)/shard_map/jit(_where)/select_n | solution.py:259
  88.5 6.0 %shard_map.89 = (f32[768,1]{1,0:T(8,128)}, f32[768,1]{1,0:T(8,128)}) custom-call(s32[2]{0:T(128)} %pad_add_fusion.bounds_ref, bf16[768,128]{1,0:T(8,128)(2,1)} %bitcast.54, bf16[768,128]{1,0:T(8,128)(2,1)} %bitcast.56, bf16[2,4,4,192,256]{4,3,2,1,0:T(8,128)(2,1)} %broadcast_select_fusion.kv_ref, s32[768,1]{1,0:T(8,128)} %fusion.21.rowpos_ref, ...), custom_call_target="tpu_custom_call" | custom-call | flops 2415919104 | bytes 3145728 | tf_op jit(solution)/shard_map/pallas_call | solution.py:209
  94.5 9.5 %shard_map.90 = (bf16[768,128]{1,0:T(8,128)(2,1)}, bf16[2,4,4,192,256]{4,3,2,1,0:T(8,128)(2,1)}) custom-call(s32[2]{0:T(128)} %pad_add_fusion.bounds_ref, bf16[768,128]{1,0:T(8,128)(2,1)} %bitcast.55, bf16[768,128]{1,0:T(8,128)(2,1)} %bitcast.57, bf16[2,4,4,192,256]{4,3,2,1,0:T(8,128)(2,1)} %broadcast_select_fusion.kv_ref, s32[768,1]{1,0:T(8,128)} %fusion.21.rowpos_ref, ...), custom_call_target="tpu_custom_call" | custom-call | flops 6039797760 | bytes 6291456 | tf_op jit(solution)/shard_map/pallas_call | solution.py:223
  103.9 1.6 copy.42
  105.6 3.8 %shard_map.91 = bf16[2,4,4,192,256]{4,3,2,1,0:T(8,128)(2,1)} custom-call(bf16[2,4,4,192,256]{4,3,2,1,0:T(8,128)(2,1)} %get-tuple-element.10.src_ref), custom_call_target="tpu_custom_call" | custom-call | tf_op jit(solution)/shard_map/pallas_call | solution.py:86
  109.3 0.0 copy-start.2
  109.3 3.2 %select_reduce_fusion = f32[4,4,192,256]{3,2,1,0:T(8,128)S(1)} fusion(bf16[2,4,4,192,256]{4,3,2,1,0:T(8,128)(2,1)} %shard_map.91, pred[2]{0:T(512)(128)(4,1)S(1)} %iota_compare_fusion.3), kind=kLoop, calls=%fused_computation | loop fusion | flops 3932160 | bytes 6291458 | tf_op jit(solution)/shard_map/reduce_sum | solution.py:250
  112.5 0.0 copy-done.2
  112.5 1.7 fusion.32
  114.2 29.5 %shard_map.92 = bf16[4,4,192,256]{3,2,1,0:T(8,128)(2,1)} custom-call(bf16[4,4,192,256]{3,2,1,0:T(8,128)(2,1)} %get-tuple-element.13.src_ref), custom_call_target="tpu_custom_call" | custom-call | tf_op jit(solution)/shard_map/pallas_call | solution.py:86
  143.7 1.9 %select_reduce_fusion.1 = f32[4,192,256]{2,1,0:T(8,128)S(1)} fusion(bf16[4,4,192,256]{3,2,1,0:T(8,128)(2,1)} %shard_map.92, pred[4]{0:T(512)(128)(4,1)S(1)} %iota_compare_fusion.2), kind=kLoop, calls=%fused_computation.5 | loop fusion | flops 2162688 | bytes 2359300 | tf_op jit(solution)/shard_map/reduce_sum | solution.py:250
  145.6 1.1 fusion.31
  146.8 22.0 %shard_map.93 = bf16[4,192,256]{2,1,0:T(8,128)(2,1)} custom-call(bf16[4,192,256]{2,1,0:T(8,128)(2,1)} %get-tuple-element.11.src_ref), custom_call_target="tpu_custom_call" | custom-call | tf_op jit(solution)/shard_map/pallas_call | solution.py:86
  168.7 1.2 select_reduce_fusion.2
  169.9 1.0 fusion.25
  170.9 0.6 fusion.33
  (5 shorter events, 0.0 us)
Async XLA Ops:
  0.6 7.8 %copy-start = (bf16[192,512]{1,0:T(8,128)(2,1)S(1)}, bf16[192,512]{1,0:T(8,128)(2,1)}, u32[]{:S(2)}) copy-start(bf16[192,512]{1,0:T(8,128)(2,1)} %param.6) | copy-start | bytes 589828
  8.4 2.6 %copy-start.3 = (bf16[192,256]{1,0:T(8,128)(2,1)}, bf16[192,256]{1,0:T(8,128)(2,1)S(1)}, u32[]{:S(2)}) copy-start(bf16[192,256]{1,0:T(8,128)(2,1)S(1)} %constant_dynamic-update-slice_fusion.src_ref) | copy-start | bytes 294916
  49.8 25.9 %copy-start.4 = (bf16[192,512]{1,0:T(8,128)(2,1)S(1)}, bf16[192,512]{1,0:T(8,128)(2,1)}, u32[]{:S(2)}) copy-start(bf16[192,512]{1,0:T(8,128)(2,1)} %src_ref.1) | copy-start | bytes 589828
  80.0 4.5 %copy-start.1 = (bf16[4,4,192,256]{3,2,1,0:T(8,128)(2,1)S(1)}, bf16[4,4,192,256]{3,2,1,0:T(8,128)(2,1)}, u32[]{:S(2)}) copy-start(bf16[4,4,192,256]{3,2,1,0:T(8,128)(2,1)} %broadcast_select_fusion.1.src_ref) | copy-start | bytes 4718596
  109.3 3.2 %copy-start.2 = (bf16[2,4,4,192,256]{4,3,2,1,0:T(8,128)(2,1)S(1)}, bf16[2,4,4,192,256]{4,3,2,1,0:T(8,128)(2,1)}, u32[]{:S(2)}) copy-start(bf16[2,4,4,192,256]{4,3,2,1,0:T(8,128)(2,1)} %get-tuple-element.10.src_ref) | copy-start | bytes 9437188

commit v10 on v9

--- a/solution.py
+++ b/solution.py
@@ -259,6 +259,64 @@
     return jnp.where(ids == me, block[None], slots)
 
 
+def _multi_kernel(groups, *refs):
+    n_groups = len(groups)
+    srcs, outs = refs[:n_groups], refs[n_groups:2 * n_groups]
+    send_sems, recv_sems = refs[2 * n_groups:3 * n_groups], refs[3 * n_groups:]
+    barrier = pltpu.get_barrier_semaphore()
+    for n, axis in groups:
+        me = lax.axis_index(axis)
+
+        def greet(k, carry, n=n, axis=axis, me=me):
+            pl.semaphore_signal(barrier, 1, device_id={axis: lax.rem(me + k, n)},
+                                device_id_type=pl.DeviceIdType.MESH)
+            return carry
+
+        lax.fori_loop(1, n, greet, 0)
+    pl.semaphore_wait(barrier, sum(n - 1 for n, _ in groups))
+
+    def desc(g, k, sending):
+        n, axis = groups[g]
+        me = lax.axis_index(axis)
+        peer = lax.rem(me + k, n) if sending else lax.rem(me + n - k, n)
+        slot = me if sending else peer
+        return pltpu.make_async_remote_copy(
+            srcs[g], outs[g].at[slot], send_sems[g].at[k - 1], recv_sems[g].at[k - 1],
+            device_id={axis: peer}, device_id_type=pl.DeviceIdType.MESH)
+
+    for g, (n, _) in enumerate(groups):
+        def start_one(k, carry, g=g):
+            desc(g, k, True).start()
+            return carry
+
+        lax.fori_loop(1, n, start_one, 0)
+    for g, (n, _) in enumerate(groups):
+        def finish_one(k, carry, g=g):
+            desc(g, k, True).wait_send()
+            desc(g, k, False).wait_recv()
+            return carry
+
+        lax.fori_loop(1, n, finish_one, 0)
+
+
+def gather_many(blocks, cid):
+    groups = tuple((lax.axis_size(axis), axis) for _, axis in blocks)
+    srcs = [b for b, _ in blocks]
+    slots = pl.pallas_call(
+        functools.partial(_multi_kernel, groups),
+        out_shape=[jax.ShapeDtypeStruct((n,) + b.shape, b.dtype) for b, (n, _) in zip(srcs, groups)],
+        in_specs=[pl.BlockSpec(memory_space=pl.ANY)] * len(srcs),
+        out_specs=[pl.BlockSpec(memory_space=pl.ANY)] * len(srcs),
+        scratch_shapes=[pltpu.SemaphoreType.DMA((n - 1,)) for n, _ in groups] * 2,
+        compiler_params=pltpu.CompilerParams(collective_id=cid, has_side_effects=True),
+    )(*srcs)
+    result = []
+    for b, (n, axis), s in zip(srcs, groups, slots):
+        ids = jnp.arange(n, dtype=jnp.int32).reshape((n,) + (1,) * b.ndim)
+        result.append(jnp.where(ids == lax.axis_index(axis), b[None], s))
+    return result
+
+
 def shards(queries, keys, values, d_out, w_out, doc_starts):
     rows_here = queries.shape[0]
     head_size = DH
@@ -272,14 +330,11 @@
     me = (lax.axis_index("zhi") * n_x + lax.axis_index("xx")) * n_core + lax.axis_index("core")
     first_row = me * rows_here
     my_rows = first_row + jnp.arange(rows_here, dtype=jnp.int32)
-    kv_block = jnp.concatenate([keys, values], axis=1)
-    for cid, axis in enumerate(("zhi", "xx", "core")):
+    n_head = lax.axis_size("head")
+    d_all, kv_block = gather_many(
+        [(d_out, "head"), (jnp.concatenate([keys, values], axis=1), "zhi")], 0)
+    for cid, axis in enumerate(("xx", "core")):
         kv_block = stage_gather(kv_block, axis, cid + 4)
-    n_head = lax.axis_size("head")
-    me_head = lax.axis_index("head")
-    d_slots = peer_blocks(d_out, n_head, "head", None, False, 0)
-    head_ids = jnp.arange(n_head, dtype=jnp.int32)[:, None, None]
-    d_all = jnp.where(head_ids == me_head, d_out[None], d_slots)
     attn_grad = jnp.einsum(
         "hte,che->tc",
         d_all,

time: 174 us -> 172 us (0.989)
    pallas_call x0 -> x1, Pallas kernels: none -> 35.4 us  [gather_many(): pl.pallas_call(functools.partial(_multi_kernel, groups), out_shape=[jax.S...]
    pallas_call x7 -> x5, Pallas kernels: 119 us -> 84 us  [peer_blocks(): pl.pallas_call(functools.partial(_peer_kernel, n, axis, upward, per_targe...]
    select_n x3 -> x2, other arithmetic: 8.72 us -> 6.84 us  [stage_gather(): return jnp.where(ids == me, block[None], slots)]
where the time goes in v10:
time: 172 us; the launch traced here: 171 us
  Pallas kernels  135 us (78%)
  other arithmetic  22.7 us (13%)
  local copies, waits for them, and re-layouts  6.27 us (4%)
  matrix products  4.38 us (3%)
  between operations  2.8 us (2%)
    pallas_call x5, Pallas kernels, peer_blocks(): pl.pallas_call(functools.partial(_peer_kernel, n, axis, upward, per_targe...  84 us
    pallas_call x1, Pallas kernels, gather_many(): pl.pallas_call(functools.partial(_multi_kernel, groups), out_shape=[jax.S...  35.4 us
    pallas_call x1, Pallas kernels, attention_grads(): pl.pallas_call(functools.partial(_grad_kernel, scaling, tk, dh), grid_spe...  9.46 us
    select_n x2, other arithmetic, stage_gather(): return jnp.where(ids == me, block[None], slots)  6.84 us
    reduce_sum x3, other arithmetic, stage_reduce(): jnp.sum(jnp.where(ids == me, 0.0, slots.astype(jnp.float32)), axis=0)  6.2 us
    pallas_call x1, Pallas kernels, attention_grads(): pl.pallas_call(functools.partial(_stats_kernel, scaling, tk, dh), grid_sp...  5.97 us
    dot_general x1, matrix products, shards(): jnp.einsum('hte,che->tc', d_all, w_out.reshape(w_out.shape[0], n_head, d_...  4.38 us

profile of v10, /device:TPU:8, one launch (start us, length us, event | category | flops | bytes accessed | tf_op | source)
XLA Modules:
  0.0 171.0 jit_solution(10843128418345238946)
XLA Ops:
  0.6 0.0 copy-start
  0.7 1.3 fusion.30
  4.0 0.6 pad_add_fusion.bounds_ref
  4.6 0.7 convert_reduce_fusion.1
  5.3 1.4 convert_reduce_fusion
  6.7 0.8 constant_dynamic-update-slice_fusion.1
  7.6 0.8 constant_dynamic-update-slice_fusion.refs_1_
  8.4 0.0 copy-done
  8.4 0.0 copy-start.3
  8.4 0.7 copy_bitcast_fusion.2
  9.1 0.9 broadcast_in_dim.127.rowdoc_ref
  10.0 0.9 fusion.21.rowpos_ref
  11.0 0.0 copy-done.3
  11.0 35.4 %shard_map.85 = (bf16[8,192,512]{2,1,0:T(8,128)(2,1)}, bf16[4,192,256]{2,1,0:T(8,128)(2,1)}) custom-call(bf16[192,512]{1,0:T(8,128)(2,1)} %refs_0_.1, bf16[192,256]{1,0:T(8,128)(2,1)} %copy-done.3), custom_call_target="tpu_custom_call" | custom-call | tf_op jit(solution)/shard_map/pallas_call | solution.py:305
  46.4 0.0 copy-start.4
  46.4 0.0 copy-start.5
  46.4 4.4 %fusion.15 = bf16[24,4,8,128]{3,2,1,0:T(8,128)(2,1)S(1)} fusion(bf16[64,8,8,512]{3,2,1,0:T(8,128)(2,1)} %bitcast.61, bf16[8,192,512]{2,1,0:T(8,128)(2,1)} %get-tuple-element.9, pred[8]{0:T(512)(128)(4,1)S(1)} %iota_compare_fusion.4, bf16[192,512]{1,0:T(8,128)(2,1)} %refs_0_.1), kind=kOutput, calls=%fused_computation.12 | convolution fusion | flops 806191104 | bytes 6160392 | tf_op jit(solution)/shard_map/hte,che->tc/dot_general | solution.py:338
  50.8 0.7 copy.43
  51.5 0.0 copy-done.4
  51.5 0.0 copy-done.5
  51.5 0.8 broadcast_select_fusion.2.src_ref
  52.4 20.1 %shard_map.86 = bf16[4,4,192,256]{3,2,1,0:T(8,128)(2,1)} custom-call(bf16[4,192,256]{2,1,0:T(8,128)(2,1)} %broadcast_select_fusion.2.src_ref), custom_call_target="tpu_custom_call" | custom-call | tf_op jit(solution)/shard_map/pallas_call | solution.py:86
  72.5 2.9 %broadcast_select_fusion.1.src_ref = bf16[4,4,192,256]{3,2,1,0:T(8,128)(2,1)} fusion(bf16[4,4,192,256]{3,2,1,0:T(8,128)(2,1)} %shard_map.86, pred[4]{0:T(512)(128)(4,1)S(1)} %iota_compare_fusion.2, bf16[4,192,256]{2,1,0:T(8,128)(2,1)} %broadcast_select_fusion.2.src_ref), kind=kLoop, calls=%fused_computation.8 | loop fusion | flops 786432 | bytes 3538948 | tf_op jit(solution)/shard_map/jit(_where)/select_n | solution.py:259
  75.3 0.0 copy-start.1
  75.3 3.8 %shard_map.87 = bf16[2,4,4,192,256]{4,3,2,1,0:T(8,128)(2,1)} custom-call(bf16[4,4,192,256]{3,2,1,0:T(8,128)(2,1)} %broadcast_select_fusion.1.src_ref), custom_call_target="tpu_custom_call" | custom-call | tf_op jit(solution)/shard_map/pallas_call | solution.py:86
  79.1 0.0 copy-done.1
  79.1 4.0 %broadcast_select_fusion.kv_ref = bf16[2,4,4,192,256]{4,3,2,1,0:T(8,128)(2,1)} fusion(bf16[2,4,4,192,256]{4,3,2,1,0:T(8,128)(2,1)} %shard_map.87, pred[2]{0:T(512)(128)(4,1)S(1)} %iota_compare_fusion.3, bf16[4,4,192,256]{3,2,1,0:T(8,128)(2,1)S(1)} %copy-done.1), kind=kLoop, calls=%fused_computation.6 | loop fusion | flops 1572864 | bytes 7864322 | tf_op jit(solution)/shard_map/jit(_where)/select_n | solution.py:259
  83.1 6.0 %shard_map.88 = (f32[768,1]{1,0:T(8,128)}, f32[768,1]{1,0:T(8,128)}) custom-call(s32[2]{0:T(128)} %pad_add_fusion.bounds_ref, bf16[768,128]{1,0:T(8,128)(2,1)} %bitcast.54, bf16[768,128]{1,0:T(8,128)(2,1)} %bitcast.56, bf16[2,4,4,192,256]{4,3,2,1,0:T(8,128)(2,1)} %broadcast_select_fusion.kv_ref, s32[768,1]{1,0:T(8,128)} %fusion.21.rowpos_ref, ...), custom_call_target="tpu_custom_call" | custom-call | flops 2415919104 | bytes 3145728 | tf_op jit(solution)/shard_map/pallas_call | solution.py:209
  89.1 9.5 %shard_map.89 = (bf16[768,128]{1,0:T(8,128)(2,1)}, bf16[2,4,4,192,256]{4,3,2,1,0:T(8,128)(2,1)}) custom-call(s32[2]{0:T(128)} %pad_add_fusion.bounds_ref, bf16[768,128]{1,0:T(8,128)(2,1)} %bitcast.55, bf16[768,128]{1,0:T(8,128)(2,1)} %bitcast.57, bf16[2,4,4,192,256]{4,3,2,1,0:T(8,128)(2,1)} %broadcast_select_fusion.kv_ref, s32[768,1]{1,0:T(8,128)} %fusion.21.rowpos_ref, ...), custom_call_target="tpu_custom_call" | custom-call | flops 6039797760 | bytes 6291456 | tf_op jit(solution)/shard_map/pallas_call | solution.py:223
  98.5 1.6 copy.42
  100.2 3.8 %shard_map.90 = bf16[2,4,4,192,256]{4,3,2,1,0:T(8,128)(2,1)} custom-call(bf16[2,4,4,192,256]{4,3,2,1,0:T(8,128)(2,1)} %get-tuple-element.14.src_ref), custom_call_target="tpu_custom_call" | custom-call | tf_op jit(solution)/shard_map/pallas_call | solution.py:86
  103.9 0.0 copy-start.2
  103.9 3.2 %select_reduce_fusion = f32[4,4,192,256]{3,2,1,0:T(8,128)S(1)} fusion(bf16[2,4,4,192,256]{4,3,2,1,0:T(8,128)(2,1)} %shard_map.90, pred[2]{0:T(512)(128)(4,1)S(1)} %iota_compare_fusion.3), kind=kLoop, calls=%fused_computation | loop fusion | flops 3932160 | bytes 6291458 | tf_op jit(solution)/shard_map/reduce_sum | solution.py:250
  107.1 0.0 copy-done.2
  107.1 1.7 fusion.32
  108.8 28.7 %shard_map.91 = bf16[4,4,192,256]{3,2,1,0:T(8,128)(2,1)} custom-call(bf16[4,4,192,256]{3,2,1,0:T(8,128)(2,1)} %get-tuple-element.17.src_ref), custom_call_target="tpu_custom_call" | custom-call | tf_op jit(solution)/shard_map/pallas_call | solution.py:86
  137.5 1.9 %select_reduce_fusion.1 = f32[4,192,256]{2,1,0:T(8,128)S(1)} fusion(bf16[4,4,192,256]{3,2,1,0:T(8,128)(2,1)} %shard_map.91, pred[4]{0:T(512)(128)(4,1)S(1)} %iota_compare_fusion.2), kind=kLoop, calls=%fused_computation.5 | loop fusion | flops 2162688 | bytes 2359300 | tf_op jit(solution)/shard_map/reduce_sum | solution.py:250
  139.4 1.1 fusion.31
  140.5 27.7 %shard_map.92 = bf16[4,192,256]{2,1,0:T(8,128)(2,1)} custom-call(bf16[4,192,256]{2,1,0:T(8,128)(2,1)} %get-tuple-element.15.src_ref), custom_call_target="tpu_custom_call" | custom-call | tf_op jit(solution)/shard_map/pallas_call | solution.py:86
  168.2 1.2 select_reduce_fusion.2
  169.4 1.0 fusion.25
  170.4 0.6 fusion.33
  (5 shorter events, 0.0 us)
Async XLA Ops:
  0.6 7.8 %copy-start = (bf16[192,512]{1,0:T(8,128)(2,1)S(1)}, bf16[192,512]{1,0:T(8,128)(2,1)}, u32[]{:S(2)}) copy-start(bf16[192,512]{1,0:T(8,128)(2,1)} %param.6) | copy-start | bytes 589828
  8.4 2.6 %copy-start.3 = (bf16[192,256]{1,0:T(8,128)(2,1)}, bf16[192,256]{1,0:T(8,128)(2,1)S(1)}, u32[]{:S(2)}) copy-start(bf16[192,256]{1,0:T(8,128)(2,1)S(1)} %constant_dynamic-update-slice_fusion.refs_1_) | copy-start | bytes 294916
  46.4 5.1 %copy-start.4 = (bf16[192,256]{1,0:T(8,128)(2,1)S(1)}, bf16[192,256]{1,0:T(8,128)(2,1)}, u32[]{:S(2)}) copy-start(bf16[192,256]{1,0:T(8,128)(2,1)} %copy-done.3) | copy-start | bytes 294916
  46.4 5.1 %copy-start.5 = (bf16[4,192,256]{2,1,0:T(8,128)(2,1)S(1)}, bf16[4,192,256]{2,1,0:T(8,128)(2,1)}, u32[]{:S(2)}) copy-start(bf16[4,192,256]{2,1,0:T(8,128)(2,1)} %get-tuple-element.10) | copy-start | bytes 1179652
  75.3 3.8 %copy-start.1 = (bf16[4,4,192,256]{3,2,1,0:T(8,128)(2,1)S(1)}, bf16[4,4,192,256]{3,2,1,0:T(8,128)(2,1)}, u32[]{:S(2)}) copy-start(bf16[4,4,192,256]{3,2,1,0:T(8,128)(2,1)} %broadcast_select_fusion.1.src_ref) | copy-start | bytes 4718596
  103.9 3.2 %copy-start.2 = (bf16[2,4,4,192,256]{4,3,2,1,0:T(8,128)(2,1)S(1)}, bf16[2,4,4,192,256]{4,3,2,1,0:T(8,128)(2,1)}, u32[]{:S(2)}) copy-start(bf16[2,4,4,192,256]{4,3,2,1,0:T(8,128)(2,1)} %get-tuple-element.14.src_ref) | copy-start | bytes 9437188

commit v11 on v9

--- a/solution.py
+++ b/solution.py
@@ -275,15 +275,10 @@
     kv_block = jnp.concatenate([keys, values], axis=1)
     for cid, axis in enumerate(("zhi", "xx", "core")):
         kv_block = stage_gather(kv_block, axis, cid + 4)
-    n_head = lax.axis_size("head")
-    me_head = lax.axis_index("head")
-    d_slots = peer_blocks(d_out, n_head, "head", None, False, 0)
-    head_ids = jnp.arange(n_head, dtype=jnp.int32)[:, None, None]
-    d_all = jnp.where(head_ids == me_head, d_out[None], d_slots)
-    attn_grad = jnp.einsum(
-        "hte,che->tc",
-        d_all,
-        w_out.reshape(w_out.shape[0], n_head, d_out.shape[1]),
+    attn_grad = lax.dot_general(
+        lax.all_gather(d_out, "head", axis=1, tiled=True),
+        w_out,
+        (((1,), (1,)), ((), ())),
         preferred_element_type=jnp.float32,
     ).astype(jnp.bfloat16)
     heads = groups * per_group

time: 174 us -> 180 us (1.034); the launches traced: 172 us -> 179 us
  between operations: 2.81 us -> 16.2 us
  Pallas kernels: 134 us -> 128 us
    pallas_call x7 -> x6, Pallas kernels: 119 us -> 113 us  [peer_blocks(): pl.pallas_call(functools.partial(_peer_kernel, n, axis, upward, per_targe...]
  transfers between devices with their start and end apart: 0 -> 1, of which waited for: 0 -> 0; matrix products, arithmetic and copies ran while one was open for 0% -> 9% of each run, Pallas kernels for 0% -> 24%
where the time goes in v11:
time: 180 us; the launch traced here: 179 us
  Pallas kernels  128 us (71%)
  other arithmetic  23 us (13%)
  between operations  16.2 us (9%)
  local copies, waits for them, and re-layouts  6.92 us (4%)
  matrix products  4.2 us (2%)
    pallas_call x6, Pallas kernels, peer_blocks(): pl.pallas_call(functools.partial(_peer_kernel, n, axis, upward, per_targe...  113 us
    pallas_call x1, Pallas kernels, attention_grads(): pl.pallas_call(functools.partial(_grad_kernel, scaling, tk, dh), grid_spe...  9.46 us
    select_n x3, other arithmetic, stage_gather(): return jnp.where(ids == me, block[None], slots)  8.69 us
    reduce_sum x3, other arithmetic, stage_reduce(): jnp.sum(jnp.where(ids == me, 0.0, slots.astype(jnp.float32)), axis=0)  6.2 us
    pallas_call x1, Pallas kernels, attention_grads(): pl.pallas_call(functools.partial(_stats_kernel, scaling, tk, dh), grid_sp...  5.97 us
    dot_general x1, matrix products, shards(): lax.dot_general(lax.all_gather(d_out, 'head', axis=1, tiled=True), w_out,...  4.2 us
  transfers between devices with their start and end apart: 1, of which 0 were waited for; matrix products, arithmetic and copies ran while one was open for 9% of the time, Pallas kernels for 24%

profile of v11, /device:TPU:8, one launch (start us, length us, event | category | flops | bytes accessed | tf_op | source)
XLA Modules:
  0.0 179.4 jit_solution(2508051054627127783)
XLA Ops:
  7.2 0.0 copy-start
  7.2 0.0 all-gather.2.cloned.1.call-start
  7.2 0.7 all-gather.2.cloned.1.call-update
  7.9 1.3 fusion.10
  11.2 0.7 convert_reduce_fusion.1
  11.9 0.9 broadcast_in_dim.108.rowdoc_ref
  12.9 0.8 constant_dynamic-update-slice_fusion.1
  13.7 0.8 constant_dynamic-update-slice_fusion.src_ref
  14.5 0.0 copy-start.3
  14.5 0.6 copy-done.3
  15.2 19.6 %shard_map.85 = bf16[4,192,256]{2,1,0:T(8,128)(2,1)} custom-call(bf16[192,256]{1,0:T(8,128)(2,1)} %copy-done.3), custom_call_target="tpu_custom_call" | custom-call | tf_op jit(solution)/shard_map/pallas_call | solution.py:86
  34.8 1.9 %broadcast_select_fusion.2.src_ref = bf16[4,192,256]{2,1,0:T(8,128)(2,1)} fusion(bf16[4,192,256]{2,1,0:T(8,128)(2,1)} %shard_map.85, pred[4]{0:T(512)(128)(4,1)S(1)} %iota_compare_fusion.1, bf16[192,256]{1,0:T(8,128)(2,1)} %copy-done.3), kind=kLoop, calls=%fused_computation.14 | loop fusion | flops 196608 | bytes 884740 | tf_op jit(solution)/shard_map/jit(_where)/select_n | solution.py:259
  36.7 19.0 %shard_map.86 = bf16[4,4,192,256]{3,2,1,0:T(8,128)(2,1)} custom-call(bf16[4,192,256]{2,1,0:T(8,128)(2,1)} %broadcast_select_fusion.2.src_ref), custom_call_target="tpu_custom_call" | custom-call | tf_op jit(solution)/shard_map/pallas_call | solution.py:86
  55.7 2.9 %broadcast_select_fusion.1.src_ref = bf16[4,4,192,256]{3,2,1,0:T(8,128)(2,1)} fusion(bf16[4,4,192,256]{3,2,1,0:T(8,128)(2,1)} %shard_map.86, pred[4]{0:T(512)(128)(4,1)S(1)} %iota_compare_fusion.2, bf16[4,192,256]{2,1,0:T(8,128)(2,1)} %broadcast_select_fusion.2.src_ref), kind=kLoop, calls=%fused_computation.4 | loop fusion | flops 786432 | bytes 3538948 | tf_op jit(solution)/shard_map/jit(_where)/select_n | solution.py:259
  58.6 0.0 copy-start.4
  58.6 0.0 copy-start.1
  58.6 3.8 %shard_map.87 = bf16[2,4,4,192,256]{4,3,2,1,0:T(8,128)(2,1)} custom-call(bf16[4,4,192,256]{3,2,1,0:T(8,128)(2,1)} %broadcast_select_fusion.1.src_ref), custom_call_target="tpu_custom_call" | custom-call | tf_op jit(solution)/shard_map/pallas_call | solution.py:86
  62.4 0.6 pad_add_fusion.bounds_ref
  63.0 0.0 copy-done.4
  63.0 0.7 convert_reduce_fusion
  63.7 0.9 fusion.1.rowpos_ref
  64.6 0.0 copy-done
  64.6 0.7 copy_bitcast_fusion.2
  65.3 0.0 copy-done.1
  65.3 4.0 %broadcast_select_fusion.kv_ref = bf16[2,4,4,192,256]{4,3,2,1,0:T(8,128)(2,1)} fusion(bf16[2,4,4,192,256]{4,3,2,1,0:T(8,128)(2,1)} %shard_map.87, pred[2]{0:T(512)(128)(4,1)S(1)} %iota_compare_fusion.3, bf16[4,4,192,256]{3,2,1,0:T(8,128)(2,1)S(1)} %copy-done.1), kind=kLoop, calls=%fused_computation.3 | loop fusion | flops 1572864 | bytes 7864322 | tf_op jit(solution)/shard_map/jit(_where)/select_n | solution.py:259
  69.3 0.0 all-gather.2.cloned.1.call-done
  69.3 4.2 %fusion = bf16[24,4,8,128]{3,2,1,0:T(8,128)(2,1)S(1)} fusion(bf16[192,4096]{1,0:T(8,128)(2,1)} %all-gather.2.cloned.1.call-done, bf16[512,4096]{1,0:T(8,128)(2,1)} %param.10), kind=kOutput, calls=%fused_computation.6 | convolution fusion | flops 805404672 | bytes 5963776 | tf_op jit(solution)/shard_map/dot_general | solution.py:278
  73.5 0.7 copy.29
  74.2 6.0 %shard_map.88 = (f32[768,1]{1,0:T(8,128)}, f32[768,1]{1,0:T(8,128)}) custom-call(s32[2]{0:T(128)} %pad_add_fusion.bounds_ref, bf16[768,128]{1,0:T(8,128)(2,1)} %bitcast.40, bf16[768,128]{1,0:T(8,128)(2,1)} %bitcast.42, bf16[2,4,4,192,256]{4,3,2,1,0:T(8,128)(2,1)} %broadcast_select_fusion.kv_ref, s32[768,1]{1,0:T(8,128)} %fusion.1.rowpos_ref, ...), custom_call_target="tpu_custom_call" | custom-call | flops 2415919104 | bytes 3145728 | tf_op jit(solution)/shard_map/pallas_call | solution.py:209
  80.2 9.5 %shard_map.89 = (bf16[768,128]{1,0:T(8,128)(2,1)}, bf16[2,4,4,192,256]{4,3,2,1,0:T(8,128)(2,1)}) custom-call(s32[2]{0:T(128)} %pad_add_fusion.bounds_ref, bf16[768,128]{1,0:T(8,128)(2,1)} %bitcast.41, bf16[768,128]{1,0:T(8,128)(2,1)} %bitcast.43, bf16[2,4,4,192,256]{4,3,2,1,0:T(8,128)(2,1)} %broadcast_select_fusion.kv_ref, s32[768,1]{1,0:T(8,128)} %fusion.1.rowpos_ref, ...), custom_call_target="tpu_custom_call" | custom-call | flops 6039797760 | bytes 6291456 | tf_op jit(solution)/shard_map/pallas_call | solution.py:223
  89.6 1.6 copy.28
  91.3 3.8 %shard_map.90 = bf16[2,4,4,192,256]{4,3,2,1,0:T(8,128)(2,1)} custom-call(bf16[2,4,4,192,256]{4,3,2,1,0:T(8,128)(2,1)} %get-tuple-element.10.src_ref), custom_call_target="tpu_custom_call" | custom-call | tf_op jit(solution)/shard_map/pallas_call | solution.py:86
  95.1 0.0 copy-start.2
  95.1 3.2 %select_reduce_fusion = f32[4,4,192,256]{3,2,1,0:T(8,128)S(1)} fusion(bf16[2,4,4,192,256]{4,3,2,1,0:T(8,128)(2,1)} %shard_map.90, pred[2]{0:T(512)(128)(4,1)S(1)} %iota_compare_fusion.3), kind=kLoop, calls=%fused_computation | loop fusion | flops 3932160 | bytes 6291458 | tf_op jit(solution)/shard_map/reduce_sum | solution.py:250
  98.2 0.0 copy-done.2
  98.2 1.7 fusion.12
  99.9 28.6 %shard_map.91 = bf16[4,4,192,256]{3,2,1,0:T(8,128)(2,1)} custom-call(bf16[4,4,192,256]{3,2,1,0:T(8,128)(2,1)} %get-tuple-element.13.src_ref), custom_call_target="tpu_custom_call" | custom-call | tf_op jit(solution)/shard_map/pallas_call | solution.py:86
  128.6 1.9 %select_reduce_fusion.1 = f32[4,192,256]{2,1,0:T(8,128)S(1)} fusion(bf16[4,4,192,256]{3,2,1,0:T(8,128)(2,1)} %shard_map.91, pred[4]{0:T(512)(128)(4,1)S(1)} %iota_compare_fusion.2), kind=kLoop, calls=%fused_computation.2 | loop fusion | flops 2162688 | bytes 2359300 | tf_op jit(solution)/shard_map/reduce_sum | solution.py:250
  130.5 1.1 fusion.11
  131.6 38.2 %shard_map.92 = bf16[4,192,256]{2,1,0:T(8,128)(2,1)} custom-call(bf16[4,192,256]{2,1,0:T(8,128)(2,1)} %get-tuple-element.11.src_ref), custom_call_target="tpu_custom_call" | custom-call | tf_op jit(solution)/shard_map/pallas_call | solution.py:86
  169.8 1.2 select_reduce_fusion.2
  171.0 1.0 fusion.5
  171.9 0.6 fusion.13
  (4 shorter events, 0.0 us)
Async XLA Ops:
  7.2 57.5 %copy-start = (bf16[192,512]{1,0:T(8,128)(2,1)S(1)}, bf16[192,512]{1,0:T(8,128)(2,1)}, u32[]{:S(2)}) copy-start(bf16[192,512]{1,0:T(8,128)(2,1)} %param.6) | copy-start | bytes 589828
  7.2 62.1 %all-gather.2.cloned.1.call-start = ((), (), s32[]{:S(2)}) async-start(), calls=%async_computation | async-start | bytes 1769472 | tf_op jit(solution)/shard_map/all_gather | solution.py:279
  14.5 0.6 copy-start.3
  58.6 4.4 %copy-start.4 = (s32[4]{0:T(128)S(1)}, s32[4]{0:T(128)}, u32[]{:S(2)}) copy-start(s32[4]{0:T(128)} %param.11) | copy-start | bytes 52
  58.6 6.7 %copy-start.1 = (bf16[4,4,192,256]{3,2,1,0:T(8,128)(2,1)S(1)}, bf16[4,4,192,256]{3,2,1,0:T(8,128)(2,1)}, u32[]{:S(2)}) copy-start(bf16[4,4,192,256]{3,2,1,0:T(8,128)(2,1)} %broadcast_select_fusion.1.src_ref) | copy-start | bytes 4718596
  95.1 3.2 %copy-start.2 = (bf16[2,4,4,192,256]{4,3,2,1,0:T(8,128)(2,1)S(1)}, bf16[2,4,4,192,256]{4,3,2,1,0:T(8,128)(2,1)}, u32[]{:S(2)}) copy-start(bf16[2,4,4,192,256]{4,3,2,1,0:T(8,128)(2,1)} %get-tuple-element.10.src_ref) | copy-start | bytes 9437188
Sparse Core Ops, SparseCore 0:
  9.8 52.7 all-gather.1

commit v12 on v11

--- a/solution.py
+++ b/solution.py
@@ -24,8 +24,12 @@
     return (earlier & same_doc)[None, None]
 
 
-def _peer_kernel(n, axis, upward, per_target, src_ref, out_ref, send_sem, recv_sem):
+def _peer_kernel(n, axis, upward, per_target, src_ref, out_ref, send_sem, recv_sem, own_sem):
     me = lax.axis_index(axis)
+    own = None
+    if not per_target:
+        own = pltpu.make_async_copy(src_ref, out_ref.at[me], own_sem)
+        own.start()
     barrier = pltpu.get_barrier_semaphore()
 
     def greet(k, carry):
@@ -79,6 +83,8 @@
 
     lax.fori_loop(1, n, start_one, 0)
     lax.fori_loop(1, n, finish_one, 0)
+    if own is not None:
+        own.wait()
 
 
 def peer_blocks(src, n, axis, upward, per_target, cid):
@@ -88,7 +94,8 @@
         out_shape=jax.ShapeDtypeStruct((n,) + tuple(blk), src.dtype),
         in_specs=[pl.BlockSpec(memory_space=pl.ANY)],
         out_specs=pl.BlockSpec(memory_space=pl.ANY),
-        scratch_shapes=[pltpu.SemaphoreType.DMA((n - 1,)), pltpu.SemaphoreType.DMA((n - 1,))],
+        scratch_shapes=[pltpu.SemaphoreType.DMA((n - 1,)), pltpu.SemaphoreType.DMA((n - 1,)),
+                        pltpu.SemaphoreType.DMA(())],
         compiler_params=pltpu.CompilerParams(collective_id=cid, has_side_effects=True),
     )(src)
 
@@ -253,10 +260,7 @@
 
 def stage_gather(block, axis, cid):
     n = lax.axis_size(axis)
-    me = lax.axis_index(axis)
-    slots = peer_blocks(block, n, axis, None, False, cid)
-    ids = jnp.arange(n, dtype=jnp.int32).reshape((n,) + (1,) * block.ndim)
-    return jnp.where(ids == me, block[None], slots)
+    return peer_blocks(block, n, axis, None, False, cid)
 
 
 def shards(queries, keys, values, d_out, w_out, doc_starts):

time: 180 us -> 211 us (1.17)
  Pallas kernels: 128 us -> 170 us
  other arithmetic: 23 us -> 15.1 us
  local copies, waits for them, and re-layouts: 6.92 us -> 4.64 us
    pallas_call x6, Pallas kernels: 113 us -> 154 us  [peer_blocks(): pl.pallas_call(functools.partial(_peer_kernel, n, axis, upward, per_targe...]
    select_n x3 -> x0, other arithmetic: 8.69 us -> none  [stage_gather(): return jnp.where(ids == me, block[None], slots)]
  transfers between devices with their start and end apart: 1 -> 1, of which waited for: 0 -> 0; matrix products, arithmetic and copies ran while one was open for 9% -> 3% of each run, Pallas kernels for 24% -> 41%
where the time goes in v12:
time: 211 us
  Pallas kernels  170 us (81%)
  between operations  16.2 us (8%)
  other arithmetic  15.1 us (7%)
  local copies, waits for them, and re-layouts  4.64 us (2%)
  matrix products  4.2 us (2%)
    pallas_call x6, Pallas kernels, peer_blocks(): pl.pallas_call(functools.partial(_peer_kernel, n, axis, upward, per_targe...  154 us
    pallas_call x1, Pallas kernels, attention_grads(): pl.pallas_call(functools.partial(_grad_kernel, scaling, tk, dh), grid_spe...  9.54 us
    reduce_sum x3, other arithmetic, stage_reduce(): jnp.sum(jnp.where(ids == me, 0.0, slots.astype(jnp.float32)), axis=0)  6.2 us
    pallas_call x1, Pallas kernels, attention_grads(): pl.pallas_call(functools.partial(_stats_kernel, scaling, tk, dh), grid_sp...  5.97 us
  transfers between devices with their start and end apart: 1, of which 0 were waited for; matrix products, arithmetic and copies ran while one was open for 3% of the time, Pallas kernels for 41%

profile of v12, /device:TPU:8, one launch (start us, length us, event | category | flops | bytes accessed | tf_op | source)
XLA Modules:
  0.0 210.6 jit_solution(6981329032649211322)
XLA Ops:
  7.2 0.0 copy-start
  7.2 0.0 all-gather.2.cloned.1.call-start
  7.2 0.7 all-gather.2.cloned.1.call-update
  7.9 1.3 fusion.10
  11.2 1.5 pad_maximum_fusion.src_ref
  12.7 16.9 %shard_map.85.src_ref = bf16[4,192,256]{2,1,0:T(8,128)(2,1)} custom-call(bf16[192,256]{1,0:T(8,128)(2,1)} %pad_maximum_fusion.src_ref), custom_call_target="tpu_custom_call" | custom-call | tf_op jit(solution)/shard_map/pallas_call | solution.py:92
  29.6 0.0 copy-start.2
  29.6 20.4 %shard_map.86.src_ref = bf16[4,4,192,256]{3,2,1,0:T(8,128)(2,1)} custom-call(bf16[4,192,256]{2,1,0:T(8,128)(2,1)} %shard_map.85.src_ref), custom_call_target="tpu_custom_call" | custom-call | tf_op jit(solution)/shard_map/pallas_call | solution.py:92
  49.9 48.9 %shard_map.87.kv_ref = bf16[2,4,4,192,256]{4,3,2,1,0:T(8,128)(2,1)} custom-call(bf16[4,4,192,256]{3,2,1,0:T(8,128)(2,1)} %shard_map.86.src_ref), custom_call_target="tpu_custom_call" | custom-call | tf_op jit(solution)/shard_map/pallas_call | solution.py:92
  98.9 0.0 copy-done.2
  98.9 0.1 convert_reduce_fusion.1
  99.0 0.9 broadcast_in_dim.60.rowdoc_ref
  99.9 0.6 pad_add_fusion.bounds_ref
  100.5 0.7 convert_reduce_fusion
  101.2 0.9 fusion.1.rowpos_ref
  102.2 0.0 copy-done
  102.2 0.7 copy_bitcast_fusion.2
  102.9 0.0 all-gather.2.cloned.1.call-done
  102.9 4.2 %fusion = bf16[24,4,8,128]{3,2,1,0:T(8,128)(2,1)S(1)} fusion(bf16[192,4096]{1,0:T(8,128)(2,1)} %all-gather.2.cloned.1.call-done, bf16[512,4096]{1,0:T(8,128)(2,1)} %param.10), kind=kOutput, calls=%fused_computation.4 | convolution fusion | flops 805404672 | bytes 5963776 | tf_op jit(solution)/shard_map/dot_general | solution.py:282
  107.1 0.7 copy.29
  107.8 6.0 %shard_map.88 = (f32[768,1]{1,0:T(8,128)}, f32[768,1]{1,0:T(8,128)}) custom-call(s32[2]{0:T(128)} %pad_add_fusion.bounds_ref, bf16[768,128]{1,0:T(8,128)(2,1)} %bitcast.40, bf16[768,128]{1,0:T(8,128)(2,1)} %bitcast.42, bf16[2,4,4,192,256]{4,3,2,1,0:T(8,128)(2,1)} %shard_map.87.kv_ref, s32[768,1]{1,0:T(8,128)} %fusion.1.rowpos_ref, ...), custom_call_target="tpu_custom_call" | custom-call | flops 2415919104 | bytes 3145728 | tf_op jit(solution)/shard_map/pallas_call | solution.py:216
  113.8 9.5 %shard_map.89 = (bf16[768,128]{1,0:T(8,128)(2,1)}, bf16[2,4,4,192,256]{4,3,2,1,0:T(8,128)(2,1)}) custom-call(s32[2]{0:T(128)} %pad_add_fusion.bounds_ref, bf16[768,128]{1,0:T(8,128)(2,1)} %bitcast.41, bf16[768,128]{1,0:T(8,128)(2,1)} %bitcast.43, bf16[2,4,4,192,256]{4,3,2,1,0:T(8,128)(2,1)} %shard_map.87.kv_ref, s32[768,1]{1,0:T(8,128)} %fusion.1.rowpos_ref, ...), custom_call_target="tpu_custom_call" | custom-call | flops 6039797760 | bytes 6291456 | tf_op jit(solution)/shard_map/pallas_call | solution.py:230
  123.3 1.6 copy.28
  124.9 3.8 %shard_map.90 = bf16[2,4,4,192,256]{4,3,2,1,0:T(8,128)(2,1)} custom-call(bf16[2,4,4,192,256]{4,3,2,1,0:T(8,128)(2,1)} %get-tuple-element.10.src_ref), custom_call_target="tpu_custom_call" | custom-call | tf_op jit(solution)/shard_map/pallas_call | solution.py:92
  128.7 0.0 copy-start.1
  128.7 3.2 %select_reduce_fusion = f32[4,4,192,256]{3,2,1,0:T(8,128)S(1)} fusion(bf16[2,4,4,192,256]{4,3,2,1,0:T(8,128)(2,1)} %shard_map.90, pred[2]{0:T(512)(128)(4,1)S(1)} %iota_compare_fusion.1), kind=kLoop, calls=%fused_computation | loop fusion | flops 3932160 | bytes 6291458 | tf_op jit(solution)/shard_map/reduce_sum | solution.py:257
  131.9 0.0 copy-done.1
  131.9 1.7 fusion.12
  133.6 28.6 %shard_map.91 = bf16[4,4,192,256]{3,2,1,0:T(8,128)(2,1)} custom-call(bf16[4,4,192,256]{3,2,1,0:T(8,128)(2,1)} %get-tuple-element.13.src_ref), custom_call_target="tpu_custom_call" | custom-call | tf_op jit(solution)/shard_map/pallas_call | solution.py:92
  162.2 1.9 select_reduce_fusion.1
  164.1 1.1 fusion.11
  165.2 35.8 %shard_map.92 = bf16[4,192,256]{2,1,0:T(8,128)(2,1)} custom-call(bf16[4,192,256]{2,1,0:T(8,128)(2,1)} %get-tuple-element.11.src_ref), custom_call_target="tpu_custom_call" | custom-call | tf_op jit(solution)/shard_map/pallas_call | solution.py:92
  201.0 1.2 select_reduce_fusion.2
  202.2 1.0 fusion.5
  203.2 0.6 fusion.13
  (4 shorter events, 0.0 us)
Async XLA Ops:
  7.2 95.0 %copy-start = (bf16[192,512]{1,0:T(8,128)(2,1)S(1)}, bf16[192,512]{1,0:T(8,128)(2,1)}, u32[]{:S(2)}) copy-start(bf16[192,512]{1,0:T(8,128)(2,1)} %param.6) | copy-start | bytes 589828
  7.2 95.7 %all-gather.2.cloned.1.call-start = ((), (), s32[]{:S(2)}) async-start(), calls=%async_computation | async-start | bytes 1769472 | tf_op jit(solution)/shard_map/all_gather | solution.py:283
  29.6 69.3 %copy-start.2 = (s32[4]{0:T(128)S(1)}, s32[4]{0:T(128)}, u32[]{:S(2)}) copy-start(s32[4]{0:T(128)} %param.11) | copy-start | bytes 52
  128.7 3.2 %copy-start.1 = (bf16[2,4,4,192,256]{4,3,2,1,0:T(8,128)(2,1)S(1)}, bf16[2,4,4,192,256]{4,3,2,1,0:T(8,128)(2,1)}, u32[]{:S(2)}) copy-start(bf16[2,4,4,192,256]{4,3,2,1,0:T(8,128)(2,1)} %get-tuple-element.10.src_ref) | copy-start | bytes 9437188
Sparse Core Ops, SparseCore 0:
  9.8 50.2 all-gather.1

commit v13 on v12

--- a/solution.py
+++ b/solution.py
@@ -24,10 +24,11 @@
     return (earlier & same_doc)[None, None]
 
 
-def _peer_kernel(n, axis, upward, per_target, src_ref, out_ref, send_sem, recv_sem, own_sem):
+def _peer_kernel(n, axis, upward, per_target, own_copy, src_ref, out_ref, send_sem, recv_sem,
+                 own_sem):
     me = lax.axis_index(axis)
     own = None
-    if not per_target:
+    if own_copy:
         own = pltpu.make_async_copy(src_ref, out_ref.at[me], own_sem)
         own.start()
     barrier = pltpu.get_barrier_semaphore()
@@ -87,10 +88,10 @@
         own.wait()
 
 
-def peer_blocks(src, n, axis, upward, per_target, cid):
+def peer_blocks(src, n, axis, upward, per_target, cid, own_copy=False):
     blk = src.shape[1:] if per_target else src.shape
     return pl.pallas_call(
-        functools.partial(_peer_kernel, n, axis, upward, per_target),
+        functools.partial(_peer_kernel, n, axis, upward, per_target, own_copy),
         out_shape=jax.ShapeDtypeStruct((n,) + tuple(blk), src.dtype),
         in_specs=[pl.BlockSpec(memory_space=pl.ANY)],
         out_specs=pl.BlockSpec(memory_space=pl.ANY),
@@ -260,7 +261,11 @@
 
 def stage_gather(block, axis, cid):
     n = lax.axis_size(axis)
-    return peer_blocks(block, n, axis, None, False, cid)
+    if block.size * n * block.dtype.itemsize <= (1 << 21):
+        return peer_blocks(block, n, axis, None, False, cid, own_copy=True)
+    slots = peer_blocks(block, n, axis, None, False, cid)
+    ids = jnp.arange(n, dtype=jnp.int32).reshape((n,) + (1,) * block.ndim)
+    return jnp.where(ids == lax.axis_index(axis), block[None], slots)
 
 
 def shards(queries, keys, values, d_out, w_out, doc_starts):

time: 211 us -> 162 us (0.77)
  Pallas kernels: 170 us -> 115 us
  other arithmetic: 15.1 us -> 19.1 us
    pallas_call x6, Pallas kernels: 154 us -> 99.4 us  [peer_blocks(): pl.pallas_call(functools.partial(_peer_kernel, n, axis, upward, per_targe...]
    select_n x0 -> x1, other arithmetic: none -> 3.98 us  [stage_gather(): return jnp.where(ids == lax.axis_index(axis), block[None], slots)]
  transfers between devices with their start and end apart: 1 -> 1, of which waited for: 0 -> 0; matrix products, arithmetic and copies ran while one was open for 3% -> 7% of each run, Pallas kernels for 41% -> 26%
where the time goes in v13:
time: 162 us; the launch traced here: 160 us
  Pallas kernels  115 us (71%)
  other arithmetic  19.1 us (12%)
  between operations  16.2 us (10%)
  local copies, waits for them, and re-layouts  4.64 us (3%)
  matrix products  4.2 us (3%)
    pallas_call x6, Pallas kernels, peer_blocks(): pl.pallas_call(functools.partial(_peer_kernel, n, axis, upward, per_targe...  99.4 us
    pallas_call x1, Pallas kernels, attention_grads(): pl.pallas_call(functools.partial(_grad_kernel, scaling, tk, dh), grid_spe...  9.46 us
    reduce_sum x3, other arithmetic, stage_reduce(): jnp.sum(jnp.where(ids == me, 0.0, slots.astype(jnp.float32)), axis=0)  6.2 us
    pallas_call x1, Pallas kernels, attention_grads(): pl.pallas_call(functools.partial(_stats_kernel, scaling, tk, dh), grid_sp...  5.97 us
    dot_general x1, matrix products, shards(): lax.dot_general(lax.all_gather(d_out, 'head', axis=1, tiled=True), w_out,...  4.2 us
    select_n x1, other arithmetic, stage_gather(): return jnp.where(ids == lax.axis_index(axis), block[None], slots)  3.98 us
  transfers between devices with their start and end apart: 1, of which 0 were waited for; matrix products, arithmetic and copies ran while one was open for 7% of the time, Pallas kernels for 26%

profile of v13, /device:TPU:8, one launch (start us, length us, event | category | flops | bytes accessed | tf_op | source)
XLA Modules:
  0.0 159.6 jit_solution(15577982579889453298)
XLA Ops:
  7.2 0.0 copy-start
  7.2 0.0 all-gather.2.cloned.1.call-start
  7.2 0.7 all-gather.2.cloned.1.call-update
  7.9 1.3 fusion.10
  11.2 1.5 pad_maximum_fusion.src_ref
  12.7 16.9 %shard_map.85.src_ref = bf16[4,192,256]{2,1,0:T(8,128)(2,1)} custom-call(bf16[192,256]{1,0:T(8,128)(2,1)} %pad_maximum_fusion.src_ref), custom_call_target="tpu_custom_call" | custom-call | tf_op jit(solution)/shard_map/pallas_call | solution.py:93
  29.6 0.0 copy-start.3
  29.6 20.4 %shard_map.86.src_ref = bf16[4,4,192,256]{3,2,1,0:T(8,128)(2,1)} custom-call(bf16[4,192,256]{2,1,0:T(8,128)(2,1)} %shard_map.85.src_ref), custom_call_target="tpu_custom_call" | custom-call | tf_op jit(solution)/shard_map/pallas_call | solution.py:93
  49.9 0.0 copy-start.1
  49.9 3.9 %shard_map.87 = bf16[2,4,4,192,256]{4,3,2,1,0:T(8,128)(2,1)} custom-call(bf16[4,4,192,256]{3,2,1,0:T(8,128)(2,1)} %shard_map.86.src_ref), custom_call_target="tpu_custom_call" | custom-call | tf_op jit(solution)/shard_map/pallas_call | solution.py:93
  53.9 0.0 copy-done.3
  53.9 0.1 convert_reduce_fusion.1
  54.0 0.9 broadcast_in_dim.76.rowdoc_ref
  54.9 0.6 pad_add_fusion.bounds_ref
  55.5 0.7 convert_reduce_fusion
  56.3 0.9 fusion.1.rowpos_ref
  57.2 0.0 copy-done
  57.2 0.7 copy_bitcast_fusion.2
  57.9 0.0 copy-done.1
  57.9 4.0 %broadcast_select_fusion.kv_ref = bf16[2,4,4,192,256]{4,3,2,1,0:T(8,128)(2,1)} fusion(bf16[2,4,4,192,256]{4,3,2,1,0:T(8,128)(2,1)} %shard_map.87, pred[2]{0:T(512)(128)(4,1)S(1)} %iota_compare_fusion.3, bf16[4,4,192,256]{3,2,1,0:T(8,128)(2,1)S(1)} %copy-done.1), kind=kLoop, calls=%fused_computation.3 | loop fusion | flops 1572864 | bytes 7864322 | tf_op jit(solution)/shard_map/jit(_where)/select_n | solution.py:268
  61.9 0.0 all-gather.2.cloned.1.call-done
  61.9 4.2 %fusion = bf16[24,4,8,128]{3,2,1,0:T(8,128)(2,1)S(1)} fusion(bf16[192,4096]{1,0:T(8,128)(2,1)} %all-gather.2.cloned.1.call-done, bf16[512,4096]{1,0:T(8,128)(2,1)} %param.10), kind=kOutput, calls=%fused_computation.5 | convolution fusion | flops 805404672 | bytes 5963776 | tf_op jit(solution)/shard_map/dot_general | solution.py:287
  66.1 0.7 copy.29
  66.8 6.0 %shard_map.88 = (f32[768,1]{1,0:T(8,128)}, f32[768,1]{1,0:T(8,128)}) custom-call(s32[2]{0:T(128)} %pad_add_fusion.bounds_ref, bf16[768,128]{1,0:T(8,128)(2,1)} %bitcast.40, bf16[768,128]{1,0:T(8,128)(2,1)} %bitcast.42, bf16[2,4,4,192,256]{4,3,2,1,0:T(8,128)(2,1)} %broadcast_select_fusion.kv_ref, s32[768,1]{1,0:T(8,128)} %fusion.1.rowpos_ref, ...), custom_call_target="tpu_custom_call" | custom-call | flops 2415919104 | bytes 3145728 | tf_op jit(solution)/shard_map/pallas_call | solution.py:217
  72.8 9.5 %shard_map.89 = (bf16[768,128]{1,0:T(8,128)(2,1)}, bf16[2,4,4,192,256]{4,3,2,1,0:T(8,128)(2,1)}) custom-call(s32[2]{0:T(128)} %pad_add_fusion.bounds_ref, bf16[768,128]{1,0:T(8,128)(2,1)} %bitcast.41, bf16[768,128]{1,0:T(8,128)(2,1)} %bitcast.43, bf16[2,4,4,192,256]{4,3,2,1,0:T(8,128)(2,1)} %broadcast_select_fusion.kv_ref, s32[768,1]{1,0:T(8,128)} %fusion.1.rowpos_ref, ...), custom_call_target="tpu_custom_call" | custom-call | flops 6039797760 | bytes 6291456 | tf_op jit(solution)/shard_map/pallas_call | solution.py:231
  82.2 1.6 %copy.28 = bf16[4,24,8,128]{3,2,0,1:T(8,128)(2,1)} copy(bf16[4,24,8,128]{3,2,1,0:T(8,128)(2,1)} %bitcast.44) | data formatting | bytes 393216 | tf_op jit(solution)/shard_map/reshape | solution.py:301
  83.9 3.8 %shard_map.90 = bf16[2,4,4,192,256]{4,3,2,1,0:T(8,128)(2,1)} custom-call(bf16[2,4,4,192,256]{4,3,2,1,0:T(8,128)(2,1)} %get-tuple-element.10.src_ref), custom_call_target="tpu_custom_call" | custom-call | tf_op jit(solution)/shard_map/pallas_call | solution.py:93
  87.6 0.0 copy-start.2
  87.7 3.2 %select_reduce_fusion = f32[4,4,192,256]{3,2,1,0:T(8,128)S(1)} fusion(bf16[2,4,4,192,256]{4,3,2,1,0:T(8,128)(2,1)} %shard_map.90, pred[2]{0:T(512)(128)(4,1)S(1)} %iota_compare_fusion.3), kind=kLoop, calls=%fused_computation | loop fusion | flops 3932160 | bytes 6291458 | tf_op jit(solution)/shard_map/reduce_sum | solution.py:258
  90.8 0.0 copy-done.2
  90.8 1.7 %fusion.12 = (bf16[4,4,192,256]{3,2,1,0:T(8,128)(2,1)}, f32[4,4,192,256]{3,2,1,0:T(8,128)S(1)}) fusion(f32[4,4,192,256]{3,2,1,0:T(8,128)S(1)} %select_reduce_fusion, bf16[2,4,4,192,256]{4,3,2,1,0:T(8,128)(2,1)S(1)} %copy-done.2, s32[]{:T(128)S(6)} %select_n.63), kind=kLoop, calls=%fused_computation.36 | loop fusion | flops 2359296 | bytes 9437188 | tf_op jit(solution)/shard_map/convert_element_type | solution.py:256
  92.5 26.1 %shard_map.91 = bf16[4,4,192,256]{3,2,1,0:T(8,128)(2,1)} custom-call(bf16[4,4,192,256]{3,2,1,0:T(8,128)(2,1)} %get-tuple-element.13.src_ref), custom_call_target="tpu_custom_call" | custom-call | tf_op jit(solution)/shard_map/pallas_call | solution.py:93
  118.6 1.9 %select_reduce_fusion.1 = f32[4,192,256]{2,1,0:T(8,128)S(1)} fusion(bf16[4,4,192,256]{3,2,1,0:T(8,128)(2,1)} %shard_map.91, pred[4]{0:T(512)(128)(4,1)S(1)} %iota_compare_fusion.1), kind=kLoop, calls=%fused_computation.2 | loop fusion | flops 2162688 | bytes 2359300 | tf_op jit(solution)/shard_map/reduce_sum | solution.py:258
  120.5 1.1 fusion.11
  121.7 28.3 %shard_map.92 = bf16[4,192,256]{2,1,0:T(8,128)(2,1)} custom-call(bf16[4,192,256]{2,1,0:T(8,128)(2,1)} %get-tuple-element.11.src_ref), custom_call_target="tpu_custom_call" | custom-call | tf_op jit(solution)/shard_map/pallas_call | solution.py:93
  150.0 1.2 select_reduce_fusion.2
  151.2 1.0 fusion.5
  152.1 0.6 fusion.13
  (4 shorter events, 0.0 us)
Async XLA Ops:
  7.2 50.0 %copy-start = (bf16[192,512]{1,0:T(8,128)(2,1)S(1)}, bf16[192,512]{1,0:T(8,128)(2,1)}, u32[]{:S(2)}) copy-start(bf16[192,512]{1,0:T(8,128)(2,1)} %param.6) | copy-start | bytes 589828
  7.2 54.7 %all-gather.2.cloned.1.call-start = ((), (), s32[]{:S(2)}) async-start(), calls=%async_computation | async-start | bytes 1769472 | tf_op jit(solution)/shard_map/all_gather | solution.py:288
  29.6 24.3 %copy-start.3 = (s32[4]{0:T(128)S(1)}, s32[4]{0:T(128)}, u32[]{:S(2)}) copy-start(s32[4]{0:T(128)} %param.11) | copy-start | bytes 52
  49.9 8.0 %copy-start.1 = (bf16[4,4,192,256]{3,2,1,0:T(8,128)(2,1)S(1)}, bf16[4,4,192,256]{3,2,1,0:T(8,128)(2,1)}, u32[]{:S(2)}) copy-start(bf16[4,4,192,256]{3,2,1,0:T(8,128)(2,1)} %shard_map.86.src_ref) | copy-start | bytes 4718596
  87.6 3.2 %copy-start.2 = (bf16[2,4,4,192,256]{4,3,2,1,0:T(8,128)(2,1)S(1)}, bf16[2,4,4,192,256]{4,3,2,1,0:T(8,128)(2,1)}, u32[]{:S(2)}) copy-start(bf16[2,4,4,192,256]{4,3,2,1,0:T(8,128)(2,1)} %get-tuple-element.10.src_ref) | copy-start | bytes 9437188
Sparse Core Ops, SparseCore 0:
  9.8 50.2 all-gather.1

commit v14 on v13

--- a/solution.py
+++ b/solution.py
@@ -207,7 +207,7 @@
         full((n_rows, dh)),
         full((n_rows, dh)),
         pl.BlockSpec((n_core, 1, 1, rows_here, 2 * dh),
-                     lambda j, b: (0, tile_of(j, b) % n_x, tile_of(j, b) // n_x, 0, 0)),
+                     lambda j, b: (0, tile_of(j, b) // n_x, tile_of(j, b) % n_x, 0, 0)),
         full((n_rows, 1)),
         full((n_rows, 1)),
         pl.BlockSpec((1, tk), lambda j, b: (0, tile_of(j, b))),
@@ -282,7 +282,7 @@
     first_row = me * rows_here
     my_rows = first_row + jnp.arange(rows_here, dtype=jnp.int32)
     kv_block = jnp.concatenate([keys, values], axis=1)
-    for cid, axis in enumerate(("zhi", "xx", "core")):
+    for cid, axis in enumerate(("xx", "zhi", "core")):
         kv_block = stage_gather(kv_block, axis, cid + 4)
     attn_grad = lax.dot_general(
         lax.all_gather(d_out, "head", axis=1, tiled=True),

time: 162 us -> 194 us (1.20)
  Pallas kernels: 115 us -> 148 us
    pallas_call x6, Pallas kernels: 99.4 us -> 133 us  [peer_blocks(): pl.pallas_call(functools.partial(_peer_kernel, n, axis, upward, per_targe...]
  transfers between devices with their start and end apart: 1 -> 1, of which waited for: 0 -> 0; matrix products, arithmetic and copies ran while one was open for 7% -> 6% of each run, Pallas kernels for 26% -> 38%
where the time goes in v14:
time: 194 us; the launch traced here: 193 us
  Pallas kernels  148 us (76%)
  other arithmetic  19.1 us (10%)
  between operations  16.2 us (8%)
  local copies, waits for them, and re-layouts  4.64 us (2%)
  matrix products  4.2 us (2%)
    pallas_call x6, Pallas kernels, peer_blocks(): pl.pallas_call(functools.partial(_peer_kernel, n, axis, upward, per_targe...  133 us
    pallas_call x1, Pallas kernels, attention_grads(): pl.pallas_call(functools.partial(_grad_kernel, scaling, tk, dh), grid_spe...  9.46 us
    reduce_sum x3, other arithmetic, stage_reduce(): jnp.sum(jnp.where(ids == me, 0.0, slots.astype(jnp.float32)), axis=0)  6.2 us
    pallas_call x1, Pallas kernels, attention_grads(): pl.pallas_call(functools.partial(_stats_kernel, scaling, tk, dh), grid_sp...  5.93 us
    dot_general x1, matrix products, shards(): lax.dot_general(lax.all_gather(d_out, 'head', axis=1, tiled=True), w_out,...  4.2 us
    select_n x1, other arithmetic, stage_gather(): return jnp.where(ids == lax.axis_index(axis), block[None], slots)  3.98 us
  transfers between devices with their start and end apart: 1, of which 0 were waited for; matrix products, arithmetic and copies ran while one was open for 6% of the time, Pallas kernels for 38%

profile of v14, /device:TPU:8, one launch (start us, length us, event | category | flops | bytes accessed | tf_op | source)
XLA Modules:
  0.0 192.9 jit_solution(17163766952110051247)
XLA Ops:
  7.2 0.0 copy-start
  7.2 0.0 all-gather.2.cloned.1.call-start
  7.2 0.7 all-gather.2.cloned.1.call-update
  7.9 1.3 fusion.10
  11.2 1.5 pad_maximum_fusion.src_ref
  12.7 9.2 %shard_map.85.src_ref = bf16[4,192,256]{2,1,0:T(8,128)(2,1)} custom-call(bf16[192,256]{1,0:T(8,128)(2,1)} %pad_maximum_fusion.src_ref), custom_call_target="tpu_custom_call" | custom-call | tf_op jit(solution)/shard_map/pallas_call | solution.py:93
  21.9 0.0 copy-start.3
  21.9 60.0 %shard_map.86.src_ref = bf16[4,4,192,256]{3,2,1,0:T(8,128)(2,1)} custom-call(bf16[4,192,256]{2,1,0:T(8,128)(2,1)} %shard_map.85.src_ref), custom_call_target="tpu_custom_call" | custom-call | tf_op jit(solution)/shard_map/pallas_call | solution.py:93
  82.0 0.0 copy-start.1
  82.0 3.9 %shard_map.87 = bf16[2,4,4,192,256]{4,3,2,1,0:T(8,128)(2,1)} custom-call(bf16[4,4,192,256]{3,2,1,0:T(8,128)(2,1)} %shard_map.86.src_ref), custom_call_target="tpu_custom_call" | custom-call | tf_op jit(solution)/shard_map/pallas_call | solution.py:93
  85.9 0.0 copy-done.3
  86.0 0.1 convert_reduce_fusion.1
  86.0 0.9 broadcast_in_dim.76.rowdoc_ref
  87.0 0.6 pad_add_fusion.bounds_ref
  87.6 0.7 convert_reduce_fusion
  88.3 0.9 fusion.1.rowpos_ref
  89.2 0.0 copy-done
  89.2 0.7 copy_bitcast_fusion.2
  89.9 0.0 copy-done.1
  89.9 4.0 %broadcast_select_fusion.kv_ref = bf16[2,4,4,192,256]{4,3,2,1,0:T(8,128)(2,1)} fusion(bf16[2,4,4,192,256]{4,3,2,1,0:T(8,128)(2,1)} %shard_map.87, pred[2]{0:T(512)(128)(4,1)S(1)} %iota_compare_fusion.3, bf16[4,4,192,256]{3,2,1,0:T(8,128)(2,1)S(1)} %copy-done.1), kind=kLoop, calls=%fused_computation.3 | loop fusion | flops 1572864 | bytes 7864322 | tf_op jit(solution)/shard_map/jit(_where)/select_n | solution.py:268
  93.9 0.0 all-gather.2.cloned.1.call-done
  93.9 4.2 %fusion = bf16[24,4,8,128]{3,2,1,0:T(8,128)(2,1)S(1)} fusion(bf16[192,4096]{1,0:T(8,128)(2,1)} %all-gather.2.cloned.1.call-done, bf16[512,4096]{1,0:T(8,128)(2,1)} %param.10), kind=kOutput, calls=%fused_computation.5 | convolution fusion | flops 805404672 | bytes 5963776 | tf_op jit(solution)/shard_map/dot_general | solution.py:287
  98.1 0.7 copy.29
  98.8 5.9 %shard_map.88 = (f32[768,1]{1,0:T(8,128)}, f32[768,1]{1,0:T(8,128)}) custom-call(s32[2]{0:T(128)} %pad_add_fusion.bounds_ref, bf16[768,128]{1,0:T(8,128)(2,1)} %bitcast.40, bf16[768,128]{1,0:T(8,128)(2,1)} %bitcast.42, bf16[2,4,4,192,256]{4,3,2,1,0:T(8,128)(2,1)} %broadcast_select_fusion.kv_ref, s32[768,1]{1,0:T(8,128)} %fusion.1.rowpos_ref, ...), custom_call_target="tpu_custom_call" | custom-call | flops 2415919104 | bytes 3145728 | tf_op jit(solution)/shard_map/pallas_call | solution.py:217
  104.8 9.5 %shard_map.89 = (bf16[768,128]{1,0:T(8,128)(2,1)}, bf16[2,4,4,192,256]{4,3,2,1,0:T(8,128)(2,1)}) custom-call(s32[2]{0:T(128)} %pad_add_fusion.bounds_ref, bf16[768,128]{1,0:T(8,128)(2,1)} %bitcast.41, bf16[768,128]{1,0:T(8,128)(2,1)} %bitcast.43, bf16[2,4,4,192,256]{4,3,2,1,0:T(8,128)(2,1)} %broadcast_select_fusion.kv_ref, s32[768,1]{1,0:T(8,128)} %fusion.1.rowpos_ref, ...), custom_call_target="tpu_custom_call" | custom-call | flops 6039797760 | bytes 6291456 | tf_op jit(solution)/shard_map/pallas_call | solution.py:231
  114.2 1.6 copy.28
  115.9 3.8 %shard_map.90 = bf16[2,4,4,192,256]{4,3,2,1,0:T(8,128)(2,1)} custom-call(bf16[2,4,4,192,256]{4,3,2,1,0:T(8,128)(2,1)} %get-tuple-element.10.src_ref), custom_call_target="tpu_custom_call" | custom-call | tf_op jit(solution)/shard_map/pallas_call | solution.py:93
  119.6 0.0 copy-start.2
  119.7 3.2 %select_reduce_fusion = f32[4,4,192,256]{3,2,1,0:T(8,128)S(1)} fusion(bf16[2,4,4,192,256]{4,3,2,1,0:T(8,128)(2,1)} %shard_map.90, pred[2]{0:T(512)(128)(4,1)S(1)} %iota_compare_fusion.3), kind=kLoop, calls=%fused_computation | loop fusion | flops 3932160 | bytes 6291458 | tf_op jit(solution)/shard_map/reduce_sum | solution.py:258
  122.8 0.0 copy-done.2
  122.8 1.7 fusion.12
  124.5 29.2 %shard_map.91 = bf16[4,4,192,256]{3,2,1,0:T(8,128)(2,1)} custom-call(bf16[4,4,192,256]{3,2,1,0:T(8,128)(2,1)} %get-tuple-element.13.src_ref), custom_call_target="tpu_custom_call" | custom-call | tf_op jit(solution)/shard_map/pallas_call | solution.py:93
  153.7 1.9 select_reduce_fusion.1
  155.6 1.1 fusion.11
  156.7 26.5 %shard_map.92 = bf16[4,192,256]{2,1,0:T(8,128)(2,1)} custom-call(bf16[4,192,256]{2,1,0:T(8,128)(2,1)} %get-tuple-element.11.src_ref), custom_call_target="tpu_custom_call" | custom-call | tf_op jit(solution)/shard_map/pallas_call | solution.py:93
  183.2 1.2 select_reduce_fusion.2
  184.4 1.0 fusion.5
  185.4 0.6 fusion.13
  (4 shorter events, 0.0 us)
Async XLA Ops:
  7.2 82.1 %copy-start = (bf16[192,512]{1,0:T(8,128)(2,1)S(1)}, bf16[192,512]{1,0:T(8,128)(2,1)}, u32[]{:S(2)}) copy-start(bf16[192,512]{1,0:T(8,128)(2,1)} %param.6) | copy-start | bytes 589828
  7.2 86.7 %all-gather.2.cloned.1.call-start = ((), (), s32[]{:S(2)}) async-start(), calls=%async_computation | async-start | bytes 1769472 | tf_op jit(solution)/shard_map/all_gather | solution.py:288
  21.9 64.0 %copy-start.3 = (s32[4]{0:T(128)S(1)}, s32[4]{0:T(128)}, u32[]{:S(2)}) copy-start(s32[4]{0:T(128)} %param.11) | copy-start | bytes 52
  82.0 8.0 %copy-start.1 = (bf16[4,4,192,256]{3,2,1,0:T(8,128)(2,1)S(1)}, bf16[4,4,192,256]{3,2,1,0:T(8,128)(2,1)}, u32[]{:S(2)}) copy-start(bf16[4,4,192,256]{3,2,1,0:T(8,128)(2,1)} %shard_map.86.src_ref) | copy-start | bytes 4718596
  119.6 3.2 %copy-start.2 = (bf16[2,4,4,192,256]{4,3,2,1,0:T(8,128)(2,1)S(1)}, bf16[2,4,4,192,256]{4,3,2,1,0:T(8,128)(2,1)}, u32[]{:S(2)}) copy-start(bf16[2,4,4,192,256]{4,3,2,1,0:T(8,128)(2,1)} %get-tuple-element.10.src_ref) | copy-start | bytes 9437188
Sparse Core Ops, SparseCore 0:
  9.8 79.7 all-gather.1

commit v15 on v13

--- a/solution.py
+++ b/solution.py
@@ -255,8 +255,10 @@
     me = lax.axis_index(axis)
     slots = peer_blocks(parts.astype(jnp.bfloat16), n, axis, None, True, cid)
     ids = jnp.arange(n, dtype=jnp.int32).reshape((n,) + (1,) * (parts.ndim - 1))
-    others = jnp.sum(jnp.where(ids == me, 0.0, slots.astype(jnp.float32)), axis=0)
-    return others + lax.dynamic_index_in_dim(parts, me, 0, keepdims=False).astype(jnp.float32)
+    total = lax.dynamic_index_in_dim(parts, me, 0, keepdims=False).astype(jnp.float32)
+    for i in range(n):
+        total = total + jnp.where(me == i, 0.0, slots[i].astype(jnp.float32))
+    return total.astype(jnp.bfloat16)
 
 
 def stage_gather(block, axis, cid):

time: 162 us -> 173 us (1.068); the launches traced: 160 us -> 172 us
  Pallas kernels: 115 us -> 130 us
  other arithmetic: 19.1 us -> 17.3 us
    pallas_call x6, Pallas kernels: 99.4 us -> 115 us  [peer_blocks(): pl.pallas_call(functools.partial(_peer_kernel, n, axis, upward, per_targe...]
    reduce_sum x3 -> x0, other arithmetic: 6.2 us -> none  [stage_reduce(): jnp.sum(jnp.where(ids == me, 0.0, slots.astype(jnp.float32)), axis=0)]
    another operation x0 -> x1, other arithmetic: none -> 3.85 us
    convert_element_type x3 -> x2, other arithmetic: 3.79 us -> 3.74 us  [stage_reduce(): return total.astype(jnp.bfloat16)]
  transfers between devices with their start and end apart: 1 -> 1, of which waited for: 0 -> 0; matrix products, arithmetic and copies ran while one was open for 7% -> 7% of each run, Pallas kernels for 26% -> 24%
where the time goes in v15:
time: 173 us; the launch traced here: 172 us
  Pallas kernels  130 us (75%)
  other arithmetic  17.3 us (10%)
  between operations  16.2 us (9%)
  matrix products  4.2 us (2%)
  local copies, waits for them, and re-layouts  3.72 us (2%)
    pallas_call x6, Pallas kernels, peer_blocks(): pl.pallas_call(functools.partial(_peer_kernel, n, axis, upward, per_targe...  115 us
    pallas_call x1, Pallas kernels, attention_grads(): pl.pallas_call(functools.partial(_grad_kernel, scaling, tk, dh), grid_spe...  9.53 us
    pallas_call x1, Pallas kernels, attention_grads(): pl.pallas_call(functools.partial(_stats_kernel, scaling, tk, dh), grid_sp...  5.97 us
    dot_general x1, matrix products, shards(): lax.dot_general(lax.all_gather(d_out, 'head', axis=1, tiled=True), w_out,...  4.2 us
    select_n x1, other arithmetic, stage_gather(): return jnp.where(ids == lax.axis_index(axis), block[None], slots)  3.95 us
    another operation x1, other arithmetic  3.85 us
    convert_element_type x2, other arithmetic, stage_reduce(): return total.astype(jnp.bfloat16)  3.74 us
  transfers between devices with their start and end apart: 1, of which 0 were waited for; matrix products, arithmetic and copies ran while one was open for 7% of the time, Pallas kernels for 24%

profile of v15, /device:TPU:8, one launch (start us, length us, event | category | flops | bytes accessed | tf_op | source)
XLA Modules:
  0.0 172.4 jit_solution(3595431011878510504)
XLA Ops:
  7.2 0.0 copy-start
  7.2 0.0 all-gather.2.cloned.1.call-start
  7.2 0.7 all-gather.2.cloned.1.call-update
  7.9 1.3 fusion.18
  11.2 0.7 convert_reduce_fusion.1
  12.0 0.9 broadcast_in_dim.59.rowdoc_ref
  12.9 1.5 pad_maximum_fusion.src_ref
  14.4 18.6 %shard_map.85.src_ref = bf16[4,192,256]{2,1,0:T(8,128)(2,1)} custom-call(bf16[192,256]{1,0:T(8,128)(2,1)} %pad_maximum_fusion.src_ref), custom_call_target="tpu_custom_call" | custom-call | tf_op jit(solution)/shard_map/pallas_call | solution.py:93
  32.9 0.0 copy-start.4
  32.9 18.9 %shard_map.86.src_ref = bf16[4,4,192,256]{3,2,1,0:T(8,128)(2,1)} custom-call(bf16[4,192,256]{2,1,0:T(8,128)(2,1)} %shard_map.85.src_ref), custom_call_target="tpu_custom_call" | custom-call | tf_op jit(solution)/shard_map/pallas_call | solution.py:93
  51.8 0.0 copy-start.1
  51.9 3.9 %shard_map.87 = bf16[2,4,4,192,256]{4,3,2,1,0:T(8,128)(2,1)} custom-call(bf16[4,4,192,256]{3,2,1,0:T(8,128)(2,1)} %shard_map.86.src_ref), custom_call_target="tpu_custom_call" | custom-call | tf_op jit(solution)/shard_map/pallas_call | solution.py:93
  55.8 0.6 pad_add_fusion.bounds_ref
  56.4 0.0 copy-done.4
  56.4 0.7 convert_reduce_fusion
  57.2 0.9 fusion.5.rowpos_ref
  58.1 0.0 copy-done
  58.1 0.7 copy_bitcast_fusion.2
  58.8 0.0 copy-done.1
  58.8 4.0 %broadcast_select_fusion.kv_ref = bf16[2,4,4,192,256]{4,3,2,1,0:T(8,128)(2,1)} fusion(bf16[2,4,4,192,256]{4,3,2,1,0:T(8,128)(2,1)} %shard_map.87, pred[2]{0:T(512)(128)(4,1)S(1)} %iota_compare_fusion.1, bf16[4,4,192,256]{3,2,1,0:T(8,128)(2,1)S(1)} %copy-done.1), kind=kLoop, calls=%fused_computation.1 | loop fusion | flops 1572864 | bytes 7864322 | tf_op jit(solution)/shard_map/jit(_where)/select_n | solution.py:270
  62.8 0.0 all-gather.2.cloned.1.call-done
  62.8 4.2 %fusion = bf16[24,4,8,128]{3,2,1,0:T(8,128)(2,1)S(1)} fusion(bf16[192,4096]{1,0:T(8,128)(2,1)} %all-gather.2.cloned.1.call-done, bf16[512,4096]{1,0:T(8,128)(2,1)} %param.10), kind=kOutput, calls=%fused_computation.3 | convolution fusion | flops 805404672 | bytes 5963776 | tf_op jit(solution)/shard_map/dot_general | solution.py:289
  67.0 0.7 copy.29
  67.7 6.0 %shard_map.88 = (f32[768,1]{1,0:T(8,128)}, f32[768,1]{1,0:T(8,128)}) custom-call(s32[2]{0:T(128)} %pad_add_fusion.bounds_ref, bf16[768,128]{1,0:T(8,128)(2,1)} %bitcast.41, bf16[768,128]{1,0:T(8,128)(2,1)} %bitcast.43, bf16[2,4,4,192,256]{4,3,2,1,0:T(8,128)(2,1)} %broadcast_select_fusion.kv_ref, s32[768,1]{1,0:T(8,128)} %fusion.5.rowpos_ref, ...), custom_call_target="tpu_custom_call" | custom-call | flops 2415919104 | bytes 3145728 | tf_op jit(solution)/shard_map/pallas_call | solution.py:217
  73.7 9.5 %shard_map.89 = (bf16[768,128]{1,0:T(8,128)(2,1)}, bf16[2,4,4,192,256]{4,3,2,1,0:T(8,128)(2,1)}) custom-call(s32[2]{0:T(128)} %pad_add_fusion.bounds_ref, bf16[768,128]{1,0:T(8,128)(2,1)} %bitcast.42, bf16[768,128]{1,0:T(8,128)(2,1)} %bitcast.44, bf16[2,4,4,192,256]{4,3,2,1,0:T(8,128)(2,1)} %broadcast_select_fusion.kv_ref, s32[768,1]{1,0:T(8,128)} %fusion.5.rowpos_ref, ...), custom_call_target="tpu_custom_call" | custom-call | flops 6039797760 | bytes 6291456 | tf_op jit(solution)/shard_map/pallas_call | solution.py:231
  83.2 0.0 copy-start.2
  83.2 3.9 %shard_map.90 = bf16[2,4,4,192,256]{4,3,2,1,0:T(8,128)(2,1)} custom-call(bf16[2,4,4,192,256]{4,3,2,1,0:T(8,128)(2,1)} %get-tuple-element.10.src_ref), custom_call_target="tpu_custom_call" | custom-call | tf_op jit(solution)/shard_map/pallas_call | solution.py:93
  87.1 0.0 copy-done.2
  87.1 3.9 %add_convert_fusion = bf16[1,4,4,192,256]{4,3,2,1,0:T(8,128)(2,1)} fusion(bf16[2,4,4,192,256]{4,3,2,1,0:T(8,128)(2,1)} %shard_map.90, bf16[2,4,4,192,256]{4,3,2,1,0:T(8,128)(2,1)S(1)} %copy-done.2, s32[]{:T(128)S(6)} %select_n.134, pred[]{:T(512)S(6)} %eq.46, pred[]{:T(512)S(6)} %eq.45), kind=kLoop, calls=%fused_computation | loop fusion | flops 6291456 | bytes 6291462 | tf_op jit(solution)/shard_map/convert
  91.0 0.0 copy-start.3
  91.0 25.4 %shard_map.91 = bf16[4,4,192,256]{3,2,1,0:T(8,128)(2,1)} custom-call(bf16[4,4,192,256]{3,2,1,0:T(8,128)(2,1)} %bitcast.38), custom_call_target="tpu_custom_call" | custom-call | tf_op jit(solution)/shard_map/pallas_call | solution.py:93
  116.4 2.6 %fusion.4 = bf16[1,4,192,256]{3,2,1,0:T(8,128)(2,1)} fusion(bf16[4,4,192,256]{3,2,1,0:T(8,128)(2,1)} %shard_map.91, bf16[1,4,4,192,256]{4,3,2,1,0:T(8,128)(2,1)} %add_convert_fusion, s32[]{:T(128)S(6)} %select_n.139, pred[]{:T(512)S(6)} %eq.50, pred[]{:T(512)S(6)} %eq.49, pred[]{:T(512)S(6)} %eq.48, pred[]{:T(512)S(6)} %eq.47), kind=kLoop, calls=%fused_computation.8 | loop fusion | flops 2752512 | bytes 2359304 | tf_op jit(solution)/shard_map/convert_element_type | solution.py:261
  119.0 44.0 %shard_map.92 = bf16[4,192,256]{2,1,0:T(8,128)(2,1)} custom-call(bf16[4,192,256]{2,1,0:T(8,128)(2,1)} %bitcast.39), custom_call_target="tpu_custom_call" | custom-call | tf_op jit(solution)/shard_map/pallas_call | solution.py:93
  163.0 1.2 fusion.13
  164.2 0.6 fusion.19
  164.8 0.0 copy-done.3
  164.8 0.7 copy.28
  (2 shorter events, 0.0 us)
Async XLA Ops:
  7.2 50.9 %copy-start = (bf16[192,512]{1,0:T(8,128)(2,1)S(1)}, bf16[192,512]{1,0:T(8,128)(2,1)}, u32[]{:S(2)}) copy-start(bf16[192,512]{1,0:T(8,128)(2,1)} %param.6) | copy-start | bytes 589828
  7.2 55.6 %all-gather.2.cloned.1.call-start = ((), (), s32[]{:S(2)}) async-start(), calls=%async_computation | async-start | bytes 1769472 | tf_op jit(solution)/shard_map/all_gather | solution.py:290
  32.9 23.5 %copy-start.4 = (s32[4]{0:T(128)S(1)}, s32[4]{0:T(128)}, u32[]{:S(2)}) copy-start(s32[4]{0:T(128)} %param.11) | copy-start | bytes 52
  51.8 7.0 %copy-start.1 = (bf16[4,4,192,256]{3,2,1,0:T(8,128)(2,1)S(1)}, bf16[4,4,192,256]{3,2,1,0:T(8,128)(2,1)}, u32[]{:S(2)}) copy-start(bf16[4,4,192,256]{3,2,1,0:T(8,128)(2,1)} %shard_map.86.src_ref) | copy-start | bytes 4718596
  83.2 3.9 %copy-start.2 = (bf16[2,4,4,192,256]{4,3,2,1,0:T(8,128)(2,1)S(1)}, bf16[2,4,4,192,256]{4,3,2,1,0:T(8,128)(2,1)}, u32[]{:S(2)}) copy-start(bf16[2,4,4,192,256]{4,3,2,1,0:T(8,128)(2,1)} %get-tuple-element.10.src_ref) | copy-start | bytes 9437188
  91.0 73.9 %copy-start.3 = (bf16[768,128]{1,0:T(8,128)(2,1)S(1)}, bf16[768,128]{1,0:T(8,128)(2,1)}, u32[]{:S(2)}) copy-start(bf16[768,128]{1,0:T(8,128)(2,1)} %get-tuple-element.9) | copy-start | bytes 589828
Sparse Core Ops, SparseCore 0:
  9.8 52.0 all-gather.1

commit v16 on v13

--- a/solution.py
+++ b/solution.py
@@ -101,17 +101,24 @@
     )(src)
 
 
-def _tile_mask(j, tk, rowpos_ref, rowdoc_ref, coldoc_ref):
+def _tile_mask(j, tk, meta_ref, n_rows, rows_here, n_docs):
     col = j * tk + lax.broadcasted_iota(jnp.int32, (1, tk), 1)
-    return (col <= rowpos_ref[...]) & (coldoc_ref[...] == rowdoc_ref[...])
+    row = meta_ref[2] + lax.broadcasted_iota(jnp.int32, (n_rows, 1), 0) % rows_here
+    col_doc = jnp.zeros((1, tk), jnp.int32)
+    row_doc = jnp.zeros((n_rows, 1), jnp.int32)
+    for k in range(n_docs):
+        start = meta_ref[3 + k]
+        col_doc = col_doc + (col >= start).astype(jnp.int32)
+        row_doc = row_doc + (row >= start).astype(jnp.int32)
+    return (col <= row) & (col_doc == row_doc)
 
 
 def _key_tile(kv_ref):
     return jnp.concatenate([kv_ref[c, 0, 0] for c in range(kv_ref.shape[0])], axis=0)
 
 
-def _stats_kernel(scaling, tk, dh, bounds_ref, q_ref, g_ref, kv_ref, rowpos_ref, rowdoc_ref,
-                  coldoc_ref, lt_ref, delta_ref, m_sc, l_sc, a_sc):
+def _stats_kernel(scaling, tk, dh, rows_here, n_docs, bounds_ref, q_ref, g_ref, kv_ref,
+                  lt_ref, delta_ref, m_sc, l_sc, a_sc):
     j = pl.program_id(0)
 
     @pl.when(j == 0)
@@ -126,7 +133,7 @@
         kv = _key_tile(kv_ref)
         scores = lax.dot_general(q_ref[...], kv[:, :dh], dims,
                                  preferred_element_type=jnp.float32) * scaling
-        allowed = _tile_mask(j, tk, rowpos_ref, rowdoc_ref, coldoc_ref)
+        allowed = _tile_mask(j, tk, bounds_ref, q_ref.shape[0], rows_here, n_docs)
         scores = jnp.where(allowed, scores, NEG_FILL)
         m_old = m_sc[...]
         m_new = jnp.maximum(m_old, jnp.max(scores, axis=1, keepdims=True))
@@ -144,8 +151,8 @@
         delta_ref[...] = a_sc[...] / l_sc[...]
 
 
-def _grad_kernel(scaling, tk, dh, bounds_ref, q_ref, g_ref, kv_ref, rowpos_ref, rowdoc_ref,
-                 coldoc_ref, lt_ref, delta_ref, dq_ref, dkv_ref, dq_sc):
+def _grad_kernel(scaling, tk, dh, rows_here, n_docs, bounds_ref, q_ref, g_ref, kv_ref,
+                 lt_ref, delta_ref, dq_ref, dkv_ref, dq_sc):
     j = pl.program_id(0)
     active = (j >= bounds_ref[0]) & (j <= bounds_ref[1])
 
@@ -161,7 +168,7 @@
         k_t = kv[:, :dh]
         scores = lax.dot_general(q_ref[...], k_t, dims,
                                  preferred_element_type=jnp.float32) * scaling
-        allowed = _tile_mask(j, tk, rowpos_ref, rowdoc_ref, coldoc_ref)
+        allowed = _tile_mask(j, tk, bounds_ref, q_ref.shape[0], rows_here, n_docs)
         probs = jnp.where(allowed, jnp.exp(scores - lt_ref[...]), 0.0)
         gd = lax.dot_general(g_ref[...], kv[:, dh:], dims,
                              preferred_element_type=jnp.float32)
@@ -191,13 +198,12 @@
     n_zh, n_x, n_core = chips
     tk = n_core * rows_here
     n_tiles = n_keys // tk
-    row_pos = first_row + jnp.arange(n_rows, dtype=jnp.int32) % rows_here
-    row_doc = doc_index(doc_starts, row_pos)
-    col_doc = doc_index(doc_starts, jnp.arange(n_keys, dtype=jnp.int32))[None, :]
+    n_docs = doc_starts.shape[0]
     doc_first = jnp.max(jnp.where(doc_starts <= first_row, doc_starts, 0))
-    bounds = jnp.stack([doc_first // tk, (first_row + rows_here - 1) // tk]).astype(jnp.int32)
-    row_pos = row_pos[:, None]
-    row_doc = row_doc[:, None]
+    bounds = jnp.concatenate([
+        jnp.stack([doc_first // tk, (first_row + rows_here - 1) // tk, first_row]),
+        doc_starts,
+    ]).astype(jnp.int32)
 
     def tile_of(j, b):
         return jnp.minimum(jnp.maximum(j, b[0]), b[1])
@@ -208,14 +214,11 @@
         full((n_rows, dh)),
         pl.BlockSpec((n_core, 1, 1, rows_here, 2 * dh),
                      lambda j, b: (0, tile_of(j, b) % n_x, tile_of(j, b) // n_x, 0, 0)),
-        full((n_rows, 1)),
-        full((n_rows, 1)),
-        pl.BlockSpec((1, tk), lambda j, b: (0, tile_of(j, b))),
     ]
     params = pltpu.CompilerParams(dimension_semantics=("arbitrary",))
     mm = 2 * n_rows * n_keys * dh
     log_total, delta = pl.pallas_call(
-        functools.partial(_stats_kernel, scaling, tk, dh),
+        functools.partial(_stats_kernel, scaling, tk, dh, rows_here, n_docs),
         grid_spec=pltpu.PrefetchScalarGridSpec(
             num_scalar_prefetch=1,
             grid=(n_tiles,),
@@ -227,9 +230,9 @@
         compiler_params=params,
         cost_estimate=pl.CostEstimate(flops=2 * mm, transcendentals=n_rows * n_keys,
                                       bytes_accessed=n_keys * 4 * dh),
-    )(bounds, q_rows, g_rows, kv_full, row_pos, row_doc, col_doc)
+    )(bounds, q_rows, g_rows, kv_full)
     dq, dkv = pl.pallas_call(
-        functools.partial(_grad_kernel, scaling, tk, dh),
+        functools.partial(_grad_kernel, scaling, tk, dh, rows_here, n_docs),
         grid_spec=pltpu.PrefetchScalarGridSpec(
             num_scalar_prefetch=1,
             grid=(n_tiles,),
@@ -246,7 +249,7 @@
         compiler_params=params,
         cost_estimate=pl.CostEstimate(flops=5 * mm, transcendentals=n_rows * n_keys,
                                       bytes_accessed=n_keys * 8 * dh),
-    )(bounds, q_rows, g_rows, kv_full, row_pos, row_doc, col_doc, log_total, delta)
+    )(bounds, q_rows, g_rows, kv_full, log_total, delta)
     return dq, dkv
 
 

time: 162 us -> 169 us (1.043)
  Pallas kernels: 115 us -> 123 us
  other arithmetic: 19.1 us -> 17.4 us
    pallas_call x6, Pallas kernels: 99.4 us -> 108 us  [peer_blocks(): pl.pallas_call(functools.partial(_peer_kernel, n, axis, upward, per_targe...]
  transfers between devices with their start and end apart: 1 -> 1, of which waited for: 0 -> 1; matrix products, arithmetic and copies ran while one was open for 7% -> 5% of each run, Pallas kernels for 26% -> 25%
where the time goes in v16:
time: 169 us; the launch traced here: 166 us
  Pallas kernels  123 us (73%)
  other arithmetic  17.4 us (10%)
  between operations  16.2 us (10%)
  matrix products  4.2 us (2%)
  local copies, waits for them, and re-layouts  3.74 us (2%)
    pallas_call x6, Pallas kernels, peer_blocks(): pl.pallas_call(functools.partial(_peer_kernel, n, axis, upward, per_targe...  108 us
    pallas_call x1, Pallas kernels, attention_grads(): pl.pallas_call(functools.partial(_grad_kernel, scaling, tk, dh, rows_here...  9.41 us
    reduce_sum x3, other arithmetic, stage_reduce(): jnp.sum(jnp.where(ids == me, 0.0, slots.astype(jnp.float32)), axis=0)  6.2 us
    pallas_call x1, Pallas kernels, attention_grads(): pl.pallas_call(functools.partial(_stats_kernel, scaling, tk, dh, rows_her...  5.93 us
    dot_general x1, matrix products, shards(): lax.dot_general(lax.all_gather(d_out, 'head', axis=1, tiled=True), w_out,...  4.2 us
    select_n x1, other arithmetic, stage_gather(): return jnp.where(ids == lax.axis_index(axis), block[None], slots)  3.99 us
  transfers between devices with their start and end apart: 1, of which 1 were waited for; matrix products, arithmetic and copies ran while one was open for 5% of the time, Pallas kernels for 25%

profile of v16, /device:TPU:8, one launch (start us, length us, event | category | flops | bytes accessed | tf_op | source)
XLA Modules:
  0.0 166.4 jit_solution(841538656764596076)
XLA Ops:
  7.2 0.0 copy-start
  7.2 0.0 all-gather.2.cloned.1.call-start
  7.2 0.7 all-gather.2.cloned.1.call-update
  7.9 1.3 fusion.2
  11.2 1.5 pad_maximum_fusion.src_ref
  12.7 16.9 %shard_map.85.src_ref = bf16[4,192,256]{2,1,0:T(8,128)(2,1)} custom-call(bf16[192,256]{1,0:T(8,128)(2,1)} %pad_maximum_fusion.src_ref), custom_call_target="tpu_custom_call" | custom-call | tf_op jit(solution)/shard_map/pallas_call | solution.py:93
  29.6 0.0 copy-start.3
  29.6 20.4 %shard_map.86.src_ref = bf16[4,4,192,256]{3,2,1,0:T(8,128)(2,1)} custom-call(bf16[4,192,256]{2,1,0:T(8,128)(2,1)} %shard_map.85.src_ref), custom_call_target="tpu_custom_call" | custom-call | tf_op jit(solution)/shard_map/pallas_call | solution.py:93
  49.9 0.0 copy-start.1
  49.9 3.9 %shard_map.87 = bf16[2,4,4,192,256]{4,3,2,1,0:T(8,128)(2,1)} custom-call(bf16[4,4,192,256]{3,2,1,0:T(8,128)(2,1)} %shard_map.86.src_ref), custom_call_target="tpu_custom_call" | custom-call | tf_op jit(solution)/shard_map/pallas_call | solution.py:93
  53.9 0.0 copy-done.3
  53.9 0.6 pad_add_fusion.bounds_ref
  54.5 0.0 copy-done
  54.5 0.7 copy_bitcast_fusion.2
  55.2 0.0 copy-done.1
  55.2 4.0 %broadcast_select_fusion.kv_ref = bf16[2,4,4,192,256]{4,3,2,1,0:T(8,128)(2,1)} fusion(bf16[2,4,4,192,256]{4,3,2,1,0:T(8,128)(2,1)} %shard_map.87, pred[2]{0:T(512)(128)(4,1)S(1)} %iota_compare_fusion.2, bf16[4,4,192,256]{3,2,1,0:T(8,128)(2,1)S(1)} %copy-done.1), kind=kLoop, calls=%fused_computation.3 | loop fusion | flops 1572864 | bytes 7864322 | tf_op jit(solution)/shard_map/jit(_where)/select_n | solution.py:271
  59.2 0.9 all-gather.2.cloned.1.call-done
  60.1 4.2 %fusion = bf16[24,4,8,128]{3,2,1,0:T(8,128)(2,1)S(1)} fusion(bf16[192,4096]{1,0:T(8,128)(2,1)} %all-gather.2.cloned.1.call-done, bf16[512,4096]{1,0:T(8,128)(2,1)} %param.10), kind=kOutput, calls=%fused_computation.5 | convolution fusion | flops 805404672 | bytes 5963776 | tf_op jit(solution)/shard_map/dot_general | solution.py:290
  64.4 0.7 copy.19
  65.1 5.9 %shard_map.88 = (f32[768,1]{1,0:T(8,128)}, f32[768,1]{1,0:T(8,128)}) custom-call(s32[7]{0:T(128)} %pad_add_fusion.bounds_ref, bf16[768,128]{1,0:T(8,128)(2,1)} %bitcast.40, bf16[768,128]{1,0:T(8,128)(2,1)} %bitcast.42, bf16[2,4,4,192,256]{4,3,2,1,0:T(8,128)(2,1)} %broadcast_select_fusion.kv_ref), custom_call_target="tpu_custom_call" | custom-call | flops 2415919104 | bytes 3145728 | tf_op jit(solution)/shard_map/pallas_call | solution.py:220
  71.0 9.4 %shard_map.89 = (bf16[768,128]{1,0:T(8,128)(2,1)}, bf16[2,4,4,192,256]{4,3,2,1,0:T(8,128)(2,1)}) custom-call(s32[7]{0:T(128)} %pad_add_fusion.bounds_ref, bf16[768,128]{1,0:T(8,128)(2,1)} %bitcast.41, bf16[768,128]{1,0:T(8,128)(2,1)} %bitcast.43, bf16[2,4,4,192,256]{4,3,2,1,0:T(8,128)(2,1)} %broadcast_select_fusion.kv_ref, ...), custom_call_target="tpu_custom_call" | custom-call | flops 6039797760 | bytes 6291456 | tf_op jit(solution)/shard_map/pallas_call | solution.py:234
  80.4 1.6 copy.18
  82.1 3.8 %shard_map.90 = bf16[2,4,4,192,256]{4,3,2,1,0:T(8,128)(2,1)} custom-call(bf16[2,4,4,192,256]{4,3,2,1,0:T(8,128)(2,1)} %get-tuple-element.10.src_ref), custom_call_target="tpu_custom_call" | custom-call | tf_op jit(solution)/shard_map/pallas_call | solution.py:93
  85.8 0.0 copy-start.2
  85.9 3.2 %select_reduce_fusion = f32[4,4,192,256]{3,2,1,0:T(8,128)S(1)} fusion(bf16[2,4,4,192,256]{4,3,2,1,0:T(8,128)(2,1)} %shard_map.90, pred[2]{0:T(512)(128)(4,1)S(1)} %iota_compare_fusion.2), kind=kLoop, calls=%fused_computation | loop fusion | flops 3932160 | bytes 6291458 | tf_op jit(solution)/shard_map/reduce_sum | solution.py:261
  89.0 0.0 copy-done.2
  89.0 1.7 %fusion.4 = (bf16[4,4,192,256]{3,2,1,0:T(8,128)(2,1)}, f32[4,4,192,256]{3,2,1,0:T(8,128)S(1)}) fusion(f32[4,4,192,256]{3,2,1,0:T(8,128)S(1)} %select_reduce_fusion, bf16[2,4,4,192,256]{4,3,2,1,0:T(8,128)(2,1)S(1)} %copy-done.2, s32[]{:T(128)S(6)} %select_n.45), kind=kLoop, calls=%fused_computation.21 | loop fusion | flops 2359296 | bytes 9437188 | tf_op jit(solution)/shard_map/convert_element_type | solution.py:259
  90.7 31.9 %shard_map.91 = bf16[4,4,192,256]{3,2,1,0:T(8,128)(2,1)} custom-call(bf16[4,4,192,256]{3,2,1,0:T(8,128)(2,1)} %get-tuple-element.13.src_ref), custom_call_target="tpu_custom_call" | custom-call | tf_op jit(solution)/shard_map/pallas_call | solution.py:93
  122.6 1.9 %select_reduce_fusion.1 = f32[4,192,256]{2,1,0:T(8,128)S(1)} fusion(bf16[4,4,192,256]{3,2,1,0:T(8,128)(2,1)} %shard_map.91, pred[4]{0:T(512)(128)(4,1)S(1)} %iota_compare_fusion), kind=kLoop, calls=%fused_computation.2 | loop fusion | flops 2162688 | bytes 2359300 | tf_op jit(solution)/shard_map/reduce_sum | solution.py:261
  124.5 1.1 fusion.3
  125.7 31.1 %shard_map.92 = bf16[4,192,256]{2,1,0:T(8,128)(2,1)} custom-call(bf16[4,192,256]{2,1,0:T(8,128)(2,1)} %get-tuple-element.11.src_ref), custom_call_target="tpu_custom_call" | custom-call | tf_op jit(solution)/shard_map/pallas_call | solution.py:93
  156.8 1.2 select_reduce_fusion.2
  158.0 1.0 fusion.1
  158.9 0.6 fusion.5
  (3 shorter events, 0.0 us)
Async XLA Ops:
  7.2 47.4 %copy-start = (bf16[192,512]{1,0:T(8,128)(2,1)S(1)}, bf16[192,512]{1,0:T(8,128)(2,1)}, u32[]{:S(2)}) copy-start(bf16[192,512]{1,0:T(8,128)(2,1)} %param.6) | copy-start | bytes 589828
  7.2 53.0 %all-gather.2.cloned.1.call-start = ((), (), s32[]{:S(2)}) async-start(), calls=%async_computation | async-start | bytes 1769472 | tf_op jit(solution)/shard_map/all_gather | solution.py:291
  29.6 24.4 %copy-start.3 = (s32[4]{0:T(128)S(1)}, s32[4]{0:T(128)}, u32[]{:S(2)}) copy-start(s32[4]{0:T(128)} %param.11) | copy-start | bytes 52
  49.9 5.3 %copy-start.1 = (bf16[4,4,192,256]{3,2,1,0:T(8,128)(2,1)S(1)}, bf16[4,4,192,256]{3,2,1,0:T(8,128)(2,1)}, u32[]{:S(2)}) copy-start(bf16[4,4,192,256]{3,2,1,0:T(8,128)(2,1)} %shard_map.86.src_ref) | copy-start | bytes 4718596
  85.8 3.2 %copy-start.2 = (bf16[2,4,4,192,256]{4,3,2,1,0:T(8,128)(2,1)S(1)}, bf16[2,4,4,192,256]{4,3,2,1,0:T(8,128)(2,1)}, u32[]{:S(2)}) copy-start(bf16[2,4,4,192,256]{4,3,2,1,0:T(8,128)(2,1)} %get-tuple-element.10.src_ref) | copy-start | bytes 9437188
Sparse Core Ops, SparseCore 0:
  9.8 50.2 all-gather.1

commit v17 on v16

--- a/solution.py
+++ b/solution.py
@@ -117,23 +117,28 @@
     return jnp.concatenate([kv_ref[c, 0, 0] for c in range(kv_ref.shape[0])], axis=0)
 
 
-def _stats_kernel(scaling, tk, dh, rows_here, n_docs, bounds_ref, q_ref, g_ref, kv_ref,
-                  lt_ref, delta_ref, m_sc, l_sc, a_sc):
-    j = pl.program_id(0)
-
-    @pl.when(j == 0)
-    def _():
-        m_sc[...] = jnp.full(m_sc.shape, NEG_FILL, jnp.float32)
-        l_sc[...] = jnp.zeros(l_sc.shape, jnp.float32)
-        a_sc[...] = jnp.zeros(a_sc.shape, jnp.float32)
-
-    @pl.when((j >= bounds_ref[0]) & (j <= bounds_ref[1]))
-    def _():
-        dims = (((1,), (1,)), ((), ()))
-        kv = _key_tile(kv_ref)
+def _attn_kernel(scaling, dh, rows_here, n_docs, n_x, meta_ref, q_ref, g_ref, kv_ref,
+                 dq_ref, dkv_ref, m_sc, l_sc, a_sc, dq_sc):
+    n_core = kv_ref.shape[0]
+    tk = n_core * rows_here
+    n_rows = q_ref.shape[0]
+    lo, hi = meta_ref[0], meta_ref[1]
+    dims = (((1,), (1,)), ((), ()))
+    tdims = (((0,), (0,)), ((), ()))
+
+    def key_tile(t):
+        x, zh = t % n_x, t // n_x
+        return jnp.concatenate([kv_ref[c, x, zh] for c in range(n_core)], axis=0)
+
+    m_sc[...] = jnp.full(m_sc.shape, NEG_FILL, jnp.float32)
+    l_sc[...] = jnp.zeros(l_sc.shape, jnp.float32)
+    a_sc[...] = jnp.zeros(a_sc.shape, jnp.float32)
+
+    def stats_body(t, carry):
+        kv = key_tile(t)
         scores = lax.dot_general(q_ref[...], kv[:, :dh], dims,
                                  preferred_element_type=jnp.float32) * scaling
-        allowed = _tile_mask(j, tk, bounds_ref, q_ref.shape[0], rows_here, n_docs)
+        allowed = _tile_mask(t, tk, meta_ref, n_rows, rows_here, n_docs)
         scores = jnp.where(allowed, scores, NEG_FILL)
         m_old = m_sc[...]
         m_new = jnp.maximum(m_old, jnp.max(scores, axis=1, keepdims=True))
@@ -144,114 +149,64 @@
         l_sc[...] = alpha * l_sc[...] + jnp.sum(e, axis=1, keepdims=True)
         a_sc[...] = alpha * a_sc[...] + jnp.sum(e * gd, axis=1, keepdims=True)
         m_sc[...] = m_new
-
-    @pl.when(j == pl.num_programs(0) - 1)
-    def _():
-        lt_ref[...] = m_sc[...] + jnp.log(l_sc[...])
-        delta_ref[...] = a_sc[...] / l_sc[...]
-
-
-def _grad_kernel(scaling, tk, dh, rows_here, n_docs, bounds_ref, q_ref, g_ref, kv_ref,
-                 lt_ref, delta_ref, dq_ref, dkv_ref, dq_sc):
-    j = pl.program_id(0)
-    active = (j >= bounds_ref[0]) & (j <= bounds_ref[1])
-
-    @pl.when(j == 0)
-    def _():
-        dq_sc[...] = jnp.zeros(dq_sc.shape, jnp.float32)
-
-    @pl.when(active)
-    def _():
-        dims = (((1,), (1,)), ((), ()))
-        tdims = (((0,), (0,)), ((), ()))
-        kv = _key_tile(kv_ref)
+        return carry
+
+    lax.fori_loop(lo, hi + 1, stats_body, 0)
+    m_sc[...] = m_sc[...] + jnp.log(l_sc[...])
+    a_sc[...] = a_sc[...] / l_sc[...]
+    dq_sc[...] = jnp.zeros(dq_sc.shape, jnp.float32)
+    dkv_ref[...] = jnp.zeros(dkv_ref.shape, dkv_ref.dtype)
+
+    def grad_body(t, carry):
+        kv = key_tile(t)
         k_t = kv[:, :dh]
         scores = lax.dot_general(q_ref[...], k_t, dims,
                                  preferred_element_type=jnp.float32) * scaling
-        allowed = _tile_mask(j, tk, bounds_ref, q_ref.shape[0], rows_here, n_docs)
-        probs = jnp.where(allowed, jnp.exp(scores - lt_ref[...]), 0.0)
+        allowed = _tile_mask(t, tk, meta_ref, n_rows, rows_here, n_docs)
+        probs = jnp.where(allowed, jnp.exp(scores - m_sc[...]), 0.0)
         gd = lax.dot_general(g_ref[...], kv[:, dh:], dims,
                              preferred_element_type=jnp.float32)
-        ds = (probs * (gd - delta_ref[...]) * scaling).astype(jnp.bfloat16)
+        ds = (probs * (gd - a_sc[...]) * scaling).astype(jnp.bfloat16)
         dq_sc[...] += jnp.dot(ds, k_t, preferred_element_type=jnp.float32)
         dk = lax.dot_general(ds, q_ref[...], tdims, preferred_element_type=jnp.float32)
         dv = lax.dot_general(probs.astype(jnp.bfloat16), g_ref[...], tdims,
                              preferred_element_type=jnp.float32)
-        owner_rows = dkv_ref.shape[3]
-        for c in range(dkv_ref.shape[0]):
-            part = slice(c * owner_rows, (c + 1) * owner_rows)
-            dkv_ref[c, 0, 0, :, :dh] = dk[part].astype(dkv_ref.dtype)
-            dkv_ref[c, 0, 0, :, dh:] = dv[part].astype(dkv_ref.dtype)
-
-    @pl.when(jnp.logical_not(active))
-    def _():
-        dkv_ref[...] = jnp.zeros(dkv_ref.shape, dkv_ref.dtype)
-
-    @pl.when(j == pl.num_programs(0) - 1)
-    def _():
-        dq_ref[...] = dq_sc[...].astype(dq_ref.dtype)
+        x, zh = t % n_x, t // n_x
+        for c in range(n_core):
+            part = slice(c * rows_here, (c + 1) * rows_here)
+            dkv_ref[c, x, zh, :, :dh] = dk[part].astype(dkv_ref.dtype)
+            dkv_ref[c, x, zh, :, dh:] = dv[part].astype(dkv_ref.dtype)
+        return carry
+
+    lax.fori_loop(lo, hi + 1, grad_body, 0)
+    dq_ref[...] = dq_sc[...].astype(dq_ref.dtype)
 
 
 def attention_grads(q_rows, g_rows, kv_full, doc_starts, first_row, rows_here, scaling, chips):
     n_rows, dh = q_rows.shape
-    n_keys = kv_full.shape[0] * kv_full.shape[1] * kv_full.shape[2] * kv_full.shape[3]
     n_zh, n_x, n_core = chips
+    n_keys = n_core * n_x * n_zh * rows_here
     tk = n_core * rows_here
-    n_tiles = n_keys // tk
     n_docs = doc_starts.shape[0]
     doc_first = jnp.max(jnp.where(doc_starts <= first_row, doc_starts, 0))
-    bounds = jnp.concatenate([
+    meta = jnp.concatenate([
         jnp.stack([doc_first // tk, (first_row + rows_here - 1) // tk, first_row]),
         doc_starts,
     ]).astype(jnp.int32)
-
-    def tile_of(j, b):
-        return jnp.minimum(jnp.maximum(j, b[0]), b[1])
-
-    full = lambda shape: pl.BlockSpec(shape, lambda j, b: (0, 0))
-    in_specs = [
-        full((n_rows, dh)),
-        full((n_rows, dh)),
-        pl.BlockSpec((n_core, 1, 1, rows_here, 2 * dh),
-                     lambda j, b: (0, tile_of(j, b) % n_x, tile_of(j, b) // n_x, 0, 0)),
-    ]
-    params = pltpu.CompilerParams(dimension_semantics=("arbitrary",))
+    vmem = pl.BlockSpec(memory_space=pltpu.VMEM)
     mm = 2 * n_rows * n_keys * dh
-    log_total, delta = pl.pallas_call(
-        functools.partial(_stats_kernel, scaling, tk, dh, rows_here, n_docs),
-        grid_spec=pltpu.PrefetchScalarGridSpec(
-            num_scalar_prefetch=1,
-            grid=(n_tiles,),
-            in_specs=in_specs,
-            out_specs=[full((n_rows, 1)), full((n_rows, 1))],
-            scratch_shapes=[pltpu.VMEM((n_rows, 1), jnp.float32)] * 3,
-        ),
-        out_shape=[jax.ShapeDtypeStruct((n_rows, 1), jnp.float32)] * 2,
-        compiler_params=params,
-        cost_estimate=pl.CostEstimate(flops=2 * mm, transcendentals=n_rows * n_keys,
-                                      bytes_accessed=n_keys * 4 * dh),
-    )(bounds, q_rows, g_rows, kv_full)
     dq, dkv = pl.pallas_call(
-        functools.partial(_grad_kernel, scaling, tk, dh, rows_here, n_docs),
-        grid_spec=pltpu.PrefetchScalarGridSpec(
-            num_scalar_prefetch=1,
-            grid=(n_tiles,),
-            in_specs=in_specs + [full((n_rows, 1)), full((n_rows, 1))],
-            out_specs=[
-                full((n_rows, dh)),
-                pl.BlockSpec((n_core, 1, 1, rows_here, 2 * dh),
-                             lambda j, b: (0, j % n_x, j // n_x, 0, 0)),
-            ],
-            scratch_shapes=[pltpu.VMEM((n_rows, dh), jnp.float32)],
-        ),
+        functools.partial(_attn_kernel, scaling, dh, rows_here, n_docs, n_x),
+        in_specs=[pl.BlockSpec(memory_space=pltpu.SMEM), vmem, vmem, vmem],
+        out_specs=[vmem, vmem],
         out_shape=[jax.ShapeDtypeStruct((n_rows, dh), jnp.bfloat16),
                    jax.ShapeDtypeStruct((n_core, n_x, n_zh, rows_here, 2 * dh), jnp.bfloat16)],
-        compiler_params=params,
-        cost_estimate=pl.CostEstimate(flops=5 * mm, transcendentals=n_rows * n_keys,
+        scratch_shapes=[pltpu.VMEM((n_rows, 1), jnp.float32)] * 3
+        + [pltpu.VMEM((n_rows, dh), jnp.float32)],
+        cost_estimate=pl.CostEstimate(flops=7 * mm, transcendentals=2 * n_rows * n_keys,
                                       bytes_accessed=n_keys * 8 * dh),
-    )(bounds, q_rows, g_rows, kv_full, log_total, delta)
+    )(meta, q_rows, g_rows, kv_full)
     return dq, dkv
-
 
 def stage_reduce(parts, axis, cid):
     n = lax.axis_size(axis)

time: 169 us -> 161 us (0.953); the launches traced: 166 us -> 161 us
  Pallas kernels: 123 us -> 118 us
    pallas_call x2 -> x1, Pallas kernels: 15.3 us -> 7.68 us  [attention_grads(): pl.pallas_call(functools.partial(_attn_kernel, scaling, dh, rows_here, n_...]
    pallas_call x6, Pallas kernels: 108 us -> 110 us  [peer_blocks(): pl.pallas_call(functools.partial(_peer_kernel, n, axis, upward, per_targe...]
  transfers between devices with their start and end apart: 1 -> 1, of which waited for: 1 -> 1; matrix products, arithmetic and copies ran while one was open for 5% -> 5% of each run, Pallas kernels for 25% -> 26%
where the time goes in v17:
time: 161 us
  Pallas kernels  118 us (73%)
  other arithmetic  17.4 us (11%)
  between operations  16.2 us (10%)
  matrix products  4.2 us (3%)
  local copies, waits for them, and re-layouts  3.72 us (2%)
    pallas_call x6, Pallas kernels, peer_blocks(): pl.pallas_call(functools.partial(_peer_kernel, n, axis, upward, per_targe...  110 us
    pallas_call x1, Pallas kernels, attention_grads(): pl.pallas_call(functools.partial(_attn_kernel, scaling, dh, rows_here, n_...  7.68 us
    reduce_sum x3, other arithmetic, stage_reduce(): jnp.sum(jnp.where(ids == me, 0.0, slots.astype(jnp.float32)), axis=0)  6.2 us
    dot_general x1, matrix products, shards(): lax.dot_general(lax.all_gather(d_out, 'head', axis=1, tiled=True), w_out,...  4.2 us
    select_n x1, other arithmetic, stage_gather(): return jnp.where(ids == lax.axis_index(axis), block[None], slots)  3.99 us
  transfers between devices with their start and end apart: 1, of which 1 were waited for; matrix products, arithmetic and copies ran while one was open for 5% of the time, Pallas kernels for 26%

profile of v17, /device:TPU:8, one launch (start us, length us, event | category | flops | bytes accessed | tf_op | source)
XLA Modules:
  0.0 161.0 jit_solution(17442845138853301447)
XLA Ops:
  7.2 0.0 copy-start
  7.2 0.0 all-gather.2.cloned.1.call-start
  7.2 0.7 all-gather.2.cloned.1.call-update
  7.9 1.3 fusion.2
  11.2 1.5 pad_maximum_fusion.src_ref
  12.7 16.9 %shard_map.85.src_ref = bf16[4,192,256]{2,1,0:T(8,128)(2,1)} custom-call(bf16[192,256]{1,0:T(8,128)(2,1)} %pad_maximum_fusion.src_ref), custom_call_target="tpu_custom_call" | custom-call | tf_op jit(solution)/shard_map/pallas_call | solution.py:93
  29.6 0.0 copy-start.3
  29.6 20.4 %shard_map.86.src_ref = bf16[4,4,192,256]{3,2,1,0:T(8,128)(2,1)} custom-call(bf16[4,192,256]{2,1,0:T(8,128)(2,1)} %shard_map.85.src_ref), custom_call_target="tpu_custom_call" | custom-call | tf_op jit(solution)/shard_map/pallas_call | solution.py:93
  49.9 0.0 copy-start.1
  49.9 3.9 %shard_map.87 = bf16[2,4,4,192,256]{4,3,2,1,0:T(8,128)(2,1)} custom-call(bf16[4,4,192,256]{3,2,1,0:T(8,128)(2,1)} %shard_map.86.src_ref), custom_call_target="tpu_custom_call" | custom-call | tf_op jit(solution)/shard_map/pallas_call | solution.py:93
  53.9 0.0 copy-done.3
  53.9 0.7 pad_add_fusion.meta_ref
  54.6 0.0 copy-done
  54.6 0.7 copy_bitcast_fusion.2
  55.3 0.0 copy-done.1
  55.3 4.0 %broadcast_select_fusion.kv_ref = bf16[2,4,4,192,256]{4,3,2,1,0:T(8,128)(2,1)} fusion(bf16[2,4,4,192,256]{4,3,2,1,0:T(8,128)(2,1)} %shard_map.87, pred[2]{0:T(512)(128)(4,1)S(1)} %iota_compare_fusion.2, bf16[4,4,192,256]{3,2,1,0:T(8,128)(2,1)S(1)} %copy-done.1), kind=kLoop, calls=%fused_computation.3 | loop fusion | flops 1572864 | bytes 7864322 | tf_op jit(solution)/shard_map/jit(_where)/select_n | solution.py:226
  59.3 0.8 all-gather.2.cloned.1.call-done
  60.1 4.2 %fusion = bf16[24,4,8,128]{3,2,1,0:T(8,128)(2,1)S(1)} fusion(bf16[192,4096]{1,0:T(8,128)(2,1)} %all-gather.2.cloned.1.call-done, bf16[512,4096]{1,0:T(8,128)(2,1)} %param.10), kind=kOutput, calls=%fused_computation.5 | convolution fusion | flops 805404672 | bytes 5963776 | tf_op jit(solution)/shard_map/dot_general | solution.py:245
  64.4 0.7 copy.19
  65.1 7.7 %shard_map.88 = (bf16[768,128]{1,0:T(8,128)(2,1)}, bf16[2,4,4,192,256]{4,3,2,1,0:T(8,128)(2,1)}) custom-call(s32[7]{0:T(128)} %pad_add_fusion.meta_ref, bf16[768,128]{1,0:T(8,128)(2,1)} %bitcast.40, bf16[768,128]{1,0:T(8,128)(2,1)} %bitcast.41, bf16[2,4,4,192,256]{4,3,2,1,0:T(8,128)(2,1)} %broadcast_select_fusion.kv_ref), custom_call_target="tpu_custom_call" | custom-call | flops 8455716864 | bytes 6291456 | tf_op jit(solution)/shard_map/pallas_call | solution.py:198
  72.7 1.6 %copy.18 = bf16[4,24,8,128]{3,2,0,1:T(8,128)(2,1)} copy(bf16[4,24,8,128]{3,2,1,0:T(8,128)(2,1)} %bitcast.42) | data formatting | bytes 393216 | tf_op jit(solution)/shard_map/reshape | solution.py:259
  74.4 3.8 %shard_map.89 = bf16[2,4,4,192,256]{4,3,2,1,0:T(8,128)(2,1)} custom-call(bf16[2,4,4,192,256]{4,3,2,1,0:T(8,128)(2,1)} %get-tuple-element.6.src_ref), custom_call_target="tpu_custom_call" | custom-call | tf_op jit(solution)/shard_map/pallas_call | solution.py:93
  78.2 0.0 copy-start.2
  78.2 3.2 %select_reduce_fusion = f32[4,4,192,256]{3,2,1,0:T(8,128)S(1)} fusion(bf16[2,4,4,192,256]{4,3,2,1,0:T(8,128)(2,1)} %shard_map.89, pred[2]{0:T(512)(128)(4,1)S(1)} %iota_compare_fusion.2), kind=kLoop, calls=%fused_computation | loop fusion | flops 3932160 | bytes 6291458 | tf_op jit(solution)/shard_map/reduce_sum | solution.py:216
  81.3 0.0 copy-done.2
  81.3 1.7 %fusion.4 = (bf16[4,4,192,256]{3,2,1,0:T(8,128)(2,1)}, f32[4,4,192,256]{3,2,1,0:T(8,128)S(1)}) fusion(f32[4,4,192,256]{3,2,1,0:T(8,128)S(1)} %select_reduce_fusion, bf16[2,4,4,192,256]{4,3,2,1,0:T(8,128)(2,1)S(1)} %copy-done.2, s32[]{:T(128)S(6)} %select_n.45), kind=kLoop, calls=%fused_computation.21 | loop fusion | flops 2359296 | bytes 9437188 | tf_op jit(solution)/shard_map/convert_element_type | solution.py:214
  83.0 32.5 %shard_map.90 = bf16[4,4,192,256]{3,2,1,0:T(8,128)(2,1)} custom-call(bf16[4,4,192,256]{3,2,1,0:T(8,128)(2,1)} %get-tuple-element.9.src_ref), custom_call_target="tpu_custom_call" | custom-call | tf_op jit(solution)/shard_map/pallas_call | solution.py:93
  115.6 1.9 %select_reduce_fusion.1 = f32[4,192,256]{2,1,0:T(8,128)S(1)} fusion(bf16[4,4,192,256]{3,2,1,0:T(8,128)(2,1)} %shard_map.90, pred[4]{0:T(512)(128)(4,1)S(1)} %iota_compare_fusion), kind=kLoop, calls=%fused_computation.2 | loop fusion | flops 2162688 | bytes 2359300 | tf_op jit(solution)/shard_map/reduce_sum | solution.py:216
  117.5 1.1 fusion.3
  118.6 32.8 %shard_map.91 = bf16[4,192,256]{2,1,0:T(8,128)(2,1)} custom-call(bf16[4,192,256]{2,1,0:T(8,128)(2,1)} %get-tuple-element.7.src_ref), custom_call_target="tpu_custom_call" | custom-call | tf_op jit(solution)/shard_map/pallas_call | solution.py:93
  151.4 1.2 select_reduce_fusion.2
  152.6 1.0 fusion.1
  153.5 0.6 fusion.5
  (3 shorter events, 0.0 us)
Async XLA Ops:
  7.2 47.5 %copy-start = (bf16[192,512]{1,0:T(8,128)(2,1)S(1)}, bf16[192,512]{1,0:T(8,128)(2,1)}, u32[]{:S(2)}) copy-start(bf16[192,512]{1,0:T(8,128)(2,1)} %param.6) | copy-start | bytes 589828
  7.2 53.0 %all-gather.2.cloned.1.call-start = ((), (), s32[]{:S(2)}) async-start(), calls=%async_computation | async-start | bytes 1769472 | tf_op jit(solution)/shard_map/all_gather | solution.py:246
  29.6 24.4 %copy-start.3 = (s32[4]{0:T(128)S(1)}, s32[4]{0:T(128)}, u32[]{:S(2)}) copy-start(s32[4]{0:T(128)} %param.11) | copy-start | bytes 52
  49.9 5.4 %copy-start.1 = (bf16[4,4,192,256]{3,2,1,0:T(8,128)(2,1)S(1)}, bf16[4,4,192,256]{3,2,1,0:T(8,128)(2,1)}, u32[]{:S(2)}) copy-start(bf16[4,4,192,256]{3,2,1,0:T(8,128)(2,1)} %shard_map.86.src_ref) | copy-start | bytes 4718596
  78.2 3.2 %copy-start.2 = (bf16[2,4,4,192,256]{4,3,2,1,0:T(8,128)(2,1)S(1)}, bf16[2,4,4,192,256]{4,3,2,1,0:T(8,128)(2,1)}, u32[]{:S(2)}) copy-start(bf16[2,4,4,192,256]{4,3,2,1,0:T(8,128)(2,1)} %get-tuple-element.6.src_ref) | copy-start | bytes 9437188
Sparse Core Ops, SparseCore 0:
  9.8 50.2 all-gather.1

commit v18 on v16

--- a/solution.py
+++ b/solution.py
@@ -258,8 +258,10 @@
     me = lax.axis_index(axis)
     slots = peer_blocks(parts.astype(jnp.bfloat16), n, axis, None, True, cid)
     ids = jnp.arange(n, dtype=jnp.int32).reshape((n,) + (1,) * (parts.ndim - 1))
-    others = jnp.sum(jnp.where(ids == me, 0.0, slots.astype(jnp.float32)), axis=0)
-    return others + lax.dynamic_index_in_dim(parts, me, 0, keepdims=False).astype(jnp.float32)
+    total = lax.dynamic_index_in_dim(parts, me, 0, keepdims=False).astype(jnp.float32)
+    for i in range(n):
+        total = total + jnp.where(me == i, 0.0, slots[i].astype(jnp.float32))
+    return total.astype(jnp.bfloat16)
 
 
 def stage_gather(block, axis, cid):

time: 169 us -> 168 us (level); the launches traced: 166 us -> 167 us
  Pallas kernels: 123 us -> 127 us
  other arithmetic: 17.4 us -> 15 us
    reduce_sum x3 -> x0, other arithmetic: 6.2 us -> none  [stage_reduce(): jnp.sum(jnp.where(ids == me, 0.0, slots.astype(jnp.float32)), axis=0)]
    another operation x0 -> x1, other arithmetic: none -> 3.83 us
    pallas_call x6, Pallas kernels: 108 us -> 111 us  [peer_blocks(): pl.pallas_call(functools.partial(_peer_kernel, n, axis, upward, per_targe...]
    convert_element_type x3 -> x2, other arithmetic: 3.8 us -> 3.76 us  [stage_reduce(): return total.astype(jnp.bfloat16)]
where the time goes in v18:
time: 168 us; the launch traced here: 167 us
  Pallas kernels  127 us (76%)
  between operations  16.2 us (10%)
  other arithmetic  15 us (9%)
  matrix products  4.2 us (2%)
  local copies, waits for them, and re-layouts  3.74 us (2%)
    pallas_call x6, Pallas kernels, peer_blocks(): pl.pallas_call(functools.partial(_peer_kernel, n, axis, upward, per_targe...  111 us
    pallas_call x1, Pallas kernels, attention_grads(): pl.pallas_call(functools.partial(_grad_kernel, scaling, tk, dh, rows_here...  9.34 us
    pallas_call x1, Pallas kernels, attention_grads(): pl.pallas_call(functools.partial(_stats_kernel, scaling, tk, dh, rows_her...  5.93 us
    dot_general x1, matrix products, shards(): lax.dot_general(lax.all_gather(d_out, 'head', axis=1, tiled=True), w_out,...  4.2 us
    select_n x1, other arithmetic, stage_gather(): return jnp.where(ids == lax.axis_index(axis), block[None], slots)  3.97 us
    another operation x1, other arithmetic  3.83 us
    convert_element_type x2, other arithmetic, stage_reduce(): return total.astype(jnp.bfloat16)  3.76 us
  transfers between devices with their start and end apart: 1, of which 1 were waited for; matrix products, arithmetic and copies ran while one was open for 5% of the time, Pallas kernels for 25%

profile of v18, /device:TPU:8, one launch (start us, length us, event | category | flops | bytes accessed | tf_op | source)
XLA Modules:
  0.0 167.3 jit_solution(15840616685569131577)
XLA Ops:
  7.2 0.0 copy-start
  7.2 0.0 all-gather.2.cloned.1.call-start
  7.2 0.7 all-gather.2.cloned.1.call-update
  7.9 1.3 fusion.10
  11.2 1.5 pad_maximum_fusion.src_ref
  12.7 16.9 %shard_map.85.src_ref = bf16[4,192,256]{2,1,0:T(8,128)(2,1)} custom-call(bf16[192,256]{1,0:T(8,128)(2,1)} %pad_maximum_fusion.src_ref), custom_call_target="tpu_custom_call" | custom-call | tf_op jit(solution)/shard_map/pallas_call | solution.py:93
  29.6 0.0 copy-start.3
  29.6 20.4 %shard_map.86.src_ref = bf16[4,4,192,256]{3,2,1,0:T(8,128)(2,1)} custom-call(bf16[4,192,256]{2,1,0:T(8,128)(2,1)} %shard_map.85.src_ref), custom_call_target="tpu_custom_call" | custom-call | tf_op jit(solution)/shard_map/pallas_call | solution.py:93
  50.0 0.0 copy-start.1
  50.0 3.9 %shard_map.87 = bf16[2,4,4,192,256]{4,3,2,1,0:T(8,128)(2,1)} custom-call(bf16[4,4,192,256]{3,2,1,0:T(8,128)(2,1)} %shard_map.86.src_ref), custom_call_target="tpu_custom_call" | custom-call | tf_op jit(solution)/shard_map/pallas_call | solution.py:93
  53.9 0.0 copy-done.3
  53.9 0.7 pad_add_fusion.bounds_ref
  54.6 0.0 copy-done
  54.6 0.7 copy_bitcast_fusion.2
  55.3 0.0 copy-done.1
  55.3 4.0 %broadcast_select_fusion.kv_ref = bf16[2,4,4,192,256]{4,3,2,1,0:T(8,128)(2,1)} fusion(bf16[2,4,4,192,256]{4,3,2,1,0:T(8,128)(2,1)} %shard_map.87, pred[2]{0:T(512)(128)(4,1)S(1)} %iota_compare_fusion, bf16[4,4,192,256]{3,2,1,0:T(8,128)(2,1)S(1)} %copy-done.1), kind=kLoop, calls=%fused_computation.1 | loop fusion | flops 1572864 | bytes 7864322 | tf_op jit(solution)/shard_map/jit(_where)/select_n | solution.py:273
  59.3 0.9 all-gather.2.cloned.1.call-done
  60.2 4.2 %fusion = bf16[24,4,8,128]{3,2,1,0:T(8,128)(2,1)S(1)} fusion(bf16[192,4096]{1,0:T(8,128)(2,1)} %all-gather.2.cloned.1.call-done, bf16[512,4096]{1,0:T(8,128)(2,1)} %param.10), kind=kOutput, calls=%fused_computation.3 | convolution fusion | flops 805404672 | bytes 5963776 | tf_op jit(solution)/shard_map/dot_general | solution.py:292
  64.4 0.7 copy.19
  65.1 5.9 %shard_map.88 = (f32[768,1]{1,0:T(8,128)}, f32[768,1]{1,0:T(8,128)}) custom-call(s32[7]{0:T(128)} %pad_add_fusion.bounds_ref, bf16[768,128]{1,0:T(8,128)(2,1)} %bitcast.41, bf16[768,128]{1,0:T(8,128)(2,1)} %bitcast.43, bf16[2,4,4,192,256]{4,3,2,1,0:T(8,128)(2,1)} %broadcast_select_fusion.kv_ref), custom_call_target="tpu_custom_call" | custom-call | flops 2415919104 | bytes 3145728 | tf_op jit(solution)/shard_map/pallas_call | solution.py:220
  71.0 9.3 %shard_map.89 = (bf16[768,128]{1,0:T(8,128)(2,1)}, bf16[2,4,4,192,256]{4,3,2,1,0:T(8,128)(2,1)}) custom-call(s32[7]{0:T(128)} %pad_add_fusion.bounds_ref, bf16[768,128]{1,0:T(8,128)(2,1)} %bitcast.42, bf16[768,128]{1,0:T(8,128)(2,1)} %bitcast.44, bf16[2,4,4,192,256]{4,3,2,1,0:T(8,128)(2,1)} %broadcast_select_fusion.kv_ref, ...), custom_call_target="tpu_custom_call" | custom-call | flops 6039797760 | bytes 6291456 | tf_op jit(solution)/shard_map/pallas_call | solution.py:234
  80.4 1.6 copy.18
  82.0 0.0 copy-start.2
  82.0 3.8 %shard_map.90 = bf16[2,4,4,192,256]{4,3,2,1,0:T(8,128)(2,1)} custom-call(bf16[2,4,4,192,256]{4,3,2,1,0:T(8,128)(2,1)} %get-tuple-element.10.src_ref), custom_call_target="tpu_custom_call" | custom-call | tf_op jit(solution)/shard_map/pallas_call | solution.py:93
  85.8 0.0 copy-done.2
  85.8 3.8 %add_convert_fusion = bf16[1,4,4,192,256]{4,3,2,1,0:T(8,128)(2,1)} fusion(bf16[2,4,4,192,256]{4,3,2,1,0:T(8,128)(2,1)} %shard_map.90, bf16[2,4,4,192,256]{4,3,2,1,0:T(8,128)(2,1)S(1)} %copy-done.2, s32[]{:T(128)S(6)} %select_n.116, pred[]{:T(512)S(6)} %eq.44, pred[]{:T(512)S(6)} %eq.43), kind=kLoop, calls=%fused_computation | loop fusion | flops 6291456 | bytes 6291462 | tf_op jit(solution)/shard_map/convert
  89.6 31.9 %shard_map.91 = bf16[4,4,192,256]{3,2,1,0:T(8,128)(2,1)} custom-call(bf16[4,4,192,256]{3,2,1,0:T(8,128)(2,1)} %bitcast.38), custom_call_target="tpu_custom_call" | custom-call | tf_op jit(solution)/shard_map/pallas_call | solution.py:93
  121.5 2.6 %fusion.4 = bf16[1,4,192,256]{3,2,1,0:T(8,128)(2,1)} fusion(bf16[4,4,192,256]{3,2,1,0:T(8,128)(2,1)} %shard_map.91, bf16[1,4,4,192,256]{4,3,2,1,0:T(8,128)(2,1)} %add_convert_fusion, s32[]{:T(128)S(6)} %select_n.121, pred[]{:T(512)S(6)} %eq.48, pred[]{:T(512)S(6)} %eq.47, pred[]{:T(512)S(6)} %eq.46, pred[]{:T(512)S(6)} %eq.45), kind=kLoop, calls=%fused_computation.8 | loop fusion | flops 2752512 | bytes 2359304 | tf_op jit(solution)/shard_map/convert_element_type | solution.py:264
  124.1 34.6 %shard_map.92 = bf16[4,192,256]{2,1,0:T(8,128)(2,1)} custom-call(bf16[4,192,256]{2,1,0:T(8,128)(2,1)} %bitcast.39), custom_call_target="tpu_custom_call" | custom-call | tf_op jit(solution)/shard_map/pallas_call | solution.py:93
  158.7 1.2 fusion.9
  159.8 0.6 fusion.11
  (1 shorter events, 0.0 us)
Async XLA Ops:
  7.2 47.4 %copy-start = (bf16[192,512]{1,0:T(8,128)(2,1)S(1)}, bf16[192,512]{1,0:T(8,128)(2,1)}, u32[]{:S(2)}) copy-start(bf16[192,512]{1,0:T(8,128)(2,1)} %param.6) | copy-start | bytes 589828
  7.2 53.0 %all-gather.2.cloned.1.call-start = ((), (), s32[]{:S(2)}) async-start(), calls=%async_computation | async-start | bytes 1769472 | tf_op jit(solution)/shard_map/all_gather | solution.py:293
  29.6 24.4 %copy-start.3 = (s32[4]{0:T(128)S(1)}, s32[4]{0:T(128)}, u32[]{:S(2)}) copy-start(s32[4]{0:T(128)} %param.11) | copy-start | bytes 52
  50.0 5.4 %copy-start.1 = (bf16[4,4,192,256]{3,2,1,0:T(8,128)(2,1)S(1)}, bf16[4,4,192,256]{3,2,1,0:T(8,128)(2,1)}, u32[]{:S(2)}) copy-start(bf16[4,4,192,256]{3,2,1,0:T(8,128)(2,1)} %shard_map.86.src_ref) | copy-start | bytes 4718596
  82.0 3.8 %copy-start.2 = (bf16[2,4,4,192,256]{4,3,2,1,0:T(8,128)(2,1)S(1)}, bf16[2,4,4,192,256]{4,3,2,1,0:T(8,128)(2,1)}, u32[]{:S(2)}) copy-start(bf16[2,4,4,192,256]{4,3,2,1,0:T(8,128)(2,1)} %get-tuple-element.10.src_ref) | copy-start | bytes 9437188
Sparse Core Ops, SparseCore 0:
  9.8 50.3 all-gather.1

commit v19 on v16

--- a/solution.py
+++ b/solution.py
@@ -189,7 +189,9 @@
 
     @pl.when(j == pl.num_programs(0) - 1)
     def _():
-        dq_ref[...] = dq_sc[...].astype(dq_ref.dtype)
+        for h in range(dq_ref.shape[1] // dh):
+            dq_ref[:, h * dh:(h + 1) * dh] = dq_sc[h * rows_here:(h + 1) * rows_here, :].astype(
+                dq_ref.dtype)
 
 
 def attention_grads(q_rows, g_rows, kv_full, doc_starts, first_row, rows_here, scaling, chips):
@@ -238,13 +240,13 @@
             grid=(n_tiles,),
             in_specs=in_specs + [full((n_rows, 1)), full((n_rows, 1))],
             out_specs=[
-                full((n_rows, dh)),
+                full((rows_here, n_rows // rows_here * dh)),
                 pl.BlockSpec((n_core, 1, 1, rows_here, 2 * dh),
                              lambda j, b: (0, j % n_x, j // n_x, 0, 0)),
             ],
             scratch_shapes=[pltpu.VMEM((n_rows, dh), jnp.float32)],
         ),
-        out_shape=[jax.ShapeDtypeStruct((n_rows, dh), jnp.bfloat16),
+        out_shape=[jax.ShapeDtypeStruct((rows_here, n_rows // rows_here * dh), jnp.bfloat16),
                    jax.ShapeDtypeStruct((n_core, n_x, n_zh, rows_here, 2 * dh), jnp.bfloat16)],
         compiler_params=params,
         cost_estimate=pl.CostEstimate(flops=5 * mm, transcendentals=n_rows * n_keys,
@@ -301,8 +303,7 @@
     dq_rows, kv_terms = attention_grads(
         q_rows, g_rows, kv_block, doc_starts, first_row, rows_here, scaling,
         (n_zh, n_x, n_core))
-    query_grad = dq_rows.reshape(heads, rows_here, head_size).transpose(1, 0, 2).reshape(
-        rows_here, heads * head_size)
+    query_grad = dq_rows
     kv_grad = kv_terms
     for cid, axis in enumerate(("core", "xx", "zhi")):
         kv_grad = stage_reduce(kv_grad, axis, cid + 1)

time: 169 us -> 162 us (0.959)
  Pallas kernels: 123 us -> 119 us
    pallas_call x6, Pallas kernels: 108 us -> 104 us  [peer_blocks(): pl.pallas_call(functools.partial(_peer_kernel, n, axis, upward, per_targe...]
  transfers between devices with their start and end apart: 1 -> 1, of which waited for: 1 -> 1; matrix products, arithmetic and copies ran while one was open for 5% -> 5% of each run, Pallas kernels for 25% -> 26%
where the time goes in v19:
time: 162 us; the launch traced here: 161 us
  Pallas kernels  119 us (73%)
  other arithmetic  17.4 us (11%)
  between operations  16.2 us (10%)
  matrix products  4.2 us (3%)
  local copies, waits for them, and re-layouts  2.11 us (1%)
    pallas_call x6, Pallas kernels, peer_blocks(): pl.pallas_call(functools.partial(_peer_kernel, n, axis, upward, per_targe...  104 us
    pallas_call x1, Pallas kernels, attention_grads(): pl.pallas_call(functools.partial(_grad_kernel, scaling, tk, dh, rows_here...  9.41 us
    reduce_sum x3, other arithmetic, stage_reduce(): jnp.sum(jnp.where(ids == me, 0.0, slots.astype(jnp.float32)), axis=0)  6.2 us
    pallas_call x1, Pallas kernels, attention_grads(): pl.pallas_call(functools.partial(_stats_kernel, scaling, tk, dh, rows_her...  5.93 us
    dot_general x1, matrix products, shards(): lax.dot_general(lax.all_gather(d_out, 'head', axis=1, tiled=True), w_out,...  4.2 us
    select_n x1, other arithmetic, stage_gather(): return jnp.where(ids == lax.axis_index(axis), block[None], slots)  3.99 us
  transfers between devices with their start and end apart: 1, of which 1 were waited for; matrix products, arithmetic and copies ran while one was open for 5% of the time, Pallas kernels for 26%

profile of v19, /device:TPU:8, one launch (start us, length us, event | category | flops | bytes accessed | tf_op | source)
XLA Modules:
  0.0 160.9 jit_solution(8852119580241686269)
XLA Ops:
  7.2 0.0 copy-start
  7.2 0.0 all-gather.2.cloned.1.call-start
  7.2 0.7 all-gather.2.cloned.1.call-update
  7.9 1.3 fusion.2
  11.2 1.5 pad_maximum_fusion.src_ref
  12.7 16.9 %shard_map.85.src_ref = bf16[4,192,256]{2,1,0:T(8,128)(2,1)} custom-call(bf16[192,256]{1,0:T(8,128)(2,1)} %pad_maximum_fusion.src_ref), custom_call_target="tpu_custom_call" | custom-call | tf_op jit(solution)/shard_map/pallas_call | solution.py:93
  29.6 0.0 copy-start.3
  29.6 20.4 %shard_map.86.src_ref = bf16[4,4,192,256]{3,2,1,0:T(8,128)(2,1)} custom-call(bf16[4,192,256]{2,1,0:T(8,128)(2,1)} %shard_map.85.src_ref), custom_call_target="tpu_custom_call" | custom-call | tf_op jit(solution)/shard_map/pallas_call | solution.py:93
  49.9 0.0 copy-start.1
  49.9 3.9 %shard_map.87 = bf16[2,4,4,192,256]{4,3,2,1,0:T(8,128)(2,1)} custom-call(bf16[4,4,192,256]{3,2,1,0:T(8,128)(2,1)} %shard_map.86.src_ref), custom_call_target="tpu_custom_call" | custom-call | tf_op jit(solution)/shard_map/pallas_call | solution.py:93
  53.9 0.0 copy-done.3
  53.9 0.6 pad_add_fusion.bounds_ref
  54.5 0.0 copy-done
  54.5 0.7 copy_bitcast_fusion.1
  55.3 0.0 copy-done.1
  55.3 4.0 %broadcast_select_fusion.kv_ref = bf16[2,4,4,192,256]{4,3,2,1,0:T(8,128)(2,1)} fusion(bf16[2,4,4,192,256]{4,3,2,1,0:T(8,128)(2,1)} %shard_map.87, pred[2]{0:T(512)(128)(4,1)S(1)} %iota_compare_fusion.2, bf16[4,4,192,256]{3,2,1,0:T(8,128)(2,1)S(1)} %copy-done.1), kind=kLoop, calls=%fused_computation.3 | loop fusion | flops 1572864 | bytes 7864322 | tf_op jit(solution)/shard_map/jit(_where)/select_n | solution.py:273
  59.3 0.9 all-gather.2.cloned.1.call-done
  60.1 4.2 %fusion = bf16[24,4,8,128]{3,2,1,0:T(8,128)(2,1)S(1)} fusion(bf16[192,4096]{1,0:T(8,128)(2,1)} %all-gather.2.cloned.1.call-done, bf16[512,4096]{1,0:T(8,128)(2,1)} %param.10), kind=kOutput, calls=%fused_computation.5 | convolution fusion | flops 805404672 | bytes 5963776 | tf_op jit(solution)/shard_map/dot_general | solution.py:292
  64.4 0.7 copy.15
  65.1 5.9 %shard_map.88 = (f32[768,1]{1,0:T(8,128)}, f32[768,1]{1,0:T(8,128)}) custom-call(s32[7]{0:T(128)} %pad_add_fusion.bounds_ref, bf16[768,128]{1,0:T(8,128)(2,1)} %bitcast.32, bf16[768,128]{1,0:T(8,128)(2,1)} %bitcast.34, bf16[2,4,4,192,256]{4,3,2,1,0:T(8,128)(2,1)} %broadcast_select_fusion.kv_ref), custom_call_target="tpu_custom_call" | custom-call | flops 2415919104 | bytes 3145728 | tf_op jit(solution)/shard_map/pallas_call | solution.py:222
  71.0 9.4 %shard_map.89 = (bf16[192,512]{1,0:T(8,128)(2,1)}, bf16[2,4,4,192,256]{4,3,2,1,0:T(8,128)(2,1)}) custom-call(s32[7]{0:T(128)} %pad_add_fusion.bounds_ref, bf16[768,128]{1,0:T(8,128)(2,1)} %bitcast.33, bf16[768,128]{1,0:T(8,128)(2,1)} %bitcast.35, bf16[2,4,4,192,256]{4,3,2,1,0:T(8,128)(2,1)} %broadcast_select_fusion.kv_ref, ...), custom_call_target="tpu_custom_call" | custom-call | flops 6039797760 | bytes 6291456 | tf_op jit(solution)/shard_map/pallas_call | solution.py:236
  80.4 3.8 %shard_map.90 = bf16[2,4,4,192,256]{4,3,2,1,0:T(8,128)(2,1)} custom-call(bf16[2,4,4,192,256]{4,3,2,1,0:T(8,128)(2,1)} %get-tuple-element.10.src_ref), custom_call_target="tpu_custom_call" | custom-call | tf_op jit(solution)/shard_map/pallas_call | solution.py:93
  84.2 0.0 copy-start.2
  84.2 3.2 %select_reduce_fusion = f32[4,4,192,256]{3,2,1,0:T(8,128)S(1)} fusion(bf16[2,4,4,192,256]{4,3,2,1,0:T(8,128)(2,1)} %shard_map.90, pred[2]{0:T(512)(128)(4,1)S(1)} %iota_compare_fusion.2), kind=kLoop, calls=%fused_computation | loop fusion | flops 3932160 | bytes 6291458 | tf_op jit(solution)/shard_map/reduce_sum | solution.py:263
  87.4 0.0 copy-done.2
  87.4 1.7 %fusion.4 = (bf16[4,4,192,256]{3,2,1,0:T(8,128)(2,1)}, f32[4,4,192,256]{3,2,1,0:T(8,128)S(1)}) fusion(f32[4,4,192,256]{3,2,1,0:T(8,128)S(1)} %select_reduce_fusion, bf16[2,4,4,192,256]{4,3,2,1,0:T(8,128)(2,1)S(1)} %copy-done.2, s32[]{:T(128)S(6)} %select_n.45), kind=kLoop, calls=%fused_computation.20 | loop fusion | flops 2359296 | bytes 9437188 | tf_op jit(solution)/shard_map/convert_element_type | solution.py:261
  89.1 31.9 %shard_map.91 = bf16[4,4,192,256]{3,2,1,0:T(8,128)(2,1)} custom-call(bf16[4,4,192,256]{3,2,1,0:T(8,128)(2,1)} %get-tuple-element.13.src_ref), custom_call_target="tpu_custom_call" | custom-call | tf_op jit(solution)/shard_map/pallas_call | solution.py:93
  121.0 1.9 %select_reduce_fusion.1 = f32[4,192,256]{2,1,0:T(8,128)S(1)} fusion(bf16[4,4,192,256]{3,2,1,0:T(8,128)(2,1)} %shard_map.91, pred[4]{0:T(512)(128)(4,1)S(1)} %iota_compare_fusion), kind=kLoop, calls=%fused_computation.2 | loop fusion | flops 2162688 | bytes 2359300 | tf_op jit(solution)/shard_map/reduce_sum | solution.py:263
  122.9 1.1 fusion.3
  124.0 27.2 %shard_map.92 = bf16[4,192,256]{2,1,0:T(8,128)(2,1)} custom-call(bf16[4,192,256]{2,1,0:T(8,128)(2,1)} %get-tuple-element.11.src_ref), custom_call_target="tpu_custom_call" | custom-call | tf_op jit(solution)/shard_map/pallas_call | solution.py:93
  151.3 1.2 select_reduce_fusion.2
  152.4 1.0 fusion.1
  153.4 0.6 fusion.5
  (3 shorter events, 0.0 us)
Async XLA Ops:
  7.2 47.4 %copy-start = (bf16[192,512]{1,0:T(8,128)(2,1)S(1)}, bf16[192,512]{1,0:T(8,128)(2,1)}, u32[]{:S(2)}) copy-start(bf16[192,512]{1,0:T(8,128)(2,1)} %param.6) | copy-start | bytes 589828
  7.2 53.0 %all-gather.2.cloned.1.call-start = ((), (), s32[]{:S(2)}) async-start(), calls=%async_computation | async-start | bytes 1769472 | tf_op jit(solution)/shard_map/all_gather | solution.py:293
  29.6 24.4 %copy-start.3 = (s32[4]{0:T(128)S(1)}, s32[4]{0:T(128)}, u32[]{:S(2)}) copy-start(s32[4]{0:T(128)} %param.11) | copy-start | bytes 52
  49.9 5.3 %copy-start.1 = (bf16[4,4,192,256]{3,2,1,0:T(8,128)(2,1)S(1)}, bf16[4,4,192,256]{3,2,1,0:T(8,128)(2,1)}, u32[]{:S(2)}) copy-start(bf16[4,4,192,256]{3,2,1,0:T(8,128)(2,1)} %shard_map.86.src_ref) | copy-start | bytes 4718596
  84.2 3.2 %copy-start.2 = (bf16[2,4,4,192,256]{4,3,2,1,0:T(8,128)(2,1)S(1)}, bf16[2,4,4,192,256]{4,3,2,1,0:T(8,128)(2,1)}, u32[]{:S(2)}) copy-start(bf16[2,4,4,192,256]{4,3,2,1,0:T(8,128)(2,1)} %get-tuple-element.10.src_ref) | copy-start | bytes 9437188
Sparse Core Ops, SparseCore 0:
  9.8 50.2 all-gather.1
